TPU v7x, 32 devices: a whole 2x2x4 slice. The times are simulated.
32 devices in a mesh: dp: 2 (over core), seq: 16 (over z, y, x).
Axes of the slice: x: 2, y: 2, z: 4, core: 2. Of those that a mesh axis runs over, the one named last changes fastest.
Arguments:
- tokens: bfloat16 [32768, 768], P(('dp', 'seq')), may hold values from -6 to 6
- cotangent: bfloat16 [16384, 768], P(('dp', 'seq')), may hold values from -6 to 6
- lengths: int32 [256], replicated, may hold values from 1 to 256, 16384 in all
- w_query: float32 [768, 768], P('seq'), may hold values from -0.4375 to 0.4375
- b_query: float32 [768], P('seq'), may hold values from -3 to 3
- w_key: float32 [768, 768], P('seq'), may hold values from -0.21875 to 0.21875
- w_value: float32 [768, 768], P('seq'), may hold values from -0.21875 to 0.21875
- b_value: float32 [768], P('seq'), may hold values from -3 to 3
- w_output: float32 [768, 768], P('seq'), may hold values from -1.75 to 1.75
- b_output: float32 [768], P('seq'), may hold values from -3 to 3
- gain_attn: float32 [768], P('seq'), may hold values from 0.1 to 1.9
- shift_attn: float32 [768], P('seq'), may hold values from -3 to 3
- w_up: float32 [768, 3072], P('seq'), may hold values from -0.21875 to 0.21875
- b_up: float32 [3072], P('seq'), may hold values from -3 to 3
- w_down: float32 [3072, 768], P('seq'), may hold values from -0.109375 to 0.109375
- b_down: float32 [768], P('seq'), may hold values from -3 to 3
- gain_ffn: float32 [768], P('seq'), may hold values from 0.1 to 1.9
- shift_ffn: float32 [768], P('seq'), may hold values from -3 to 3
- distance_slope: float32 [12], replicated, may hold values from 0.004 to 0.08
Outputs:
- pooled_out: bfloat16 [16384, 768], P(('dp', 'seq'))
- grad_tokens: float32 [32768, 768], P(('dp', 'seq'))
- grad_w_query: float32 [768, 768], P('seq')
- grad_b_query: float32 [768], P('seq')
- grad_w_key: float32 [768, 768], P('seq')
- grad_w_value: float32 [768, 768], P('seq')
- grad_b_value: float32 [768], P('seq')
- grad_w_output: float32 [768, 768], P('seq')
- grad_b_output: float32 [768], P('seq')
- grad_gain_attn: float32 [768], P('seq')
- grad_shift_attn: float32 [768], P('seq')
- grad_w_up: float32 [768, 3072], P('seq')
- grad_b_up: float32 [3072], P('seq')
- grad_w_down: float32 [3072, 768], P('seq')
- grad_b_down: float32 [768], P('seq')
- grad_gain_ffn: float32 [768], P('seq')
- grad_shift_ffn: float32 [768], P('seq')
- grad_distance_slope: float32 [12], replicated
Inputs may be any that keep to these rules, and one draw needn't show every extreme that they name: Lengths count token pairs; all 256 lengths sum to 16384, so the rows fill the pack exactly.
All inputs are finite; a program needn't handle non-finite values.
Results may differ from a plain program's by a relative error of at most 0.015.
The roundings to bfloat16 on the way count: a program that leaves them out, or rounds other values in their place, can miss the bound.
Values may be sent and summed in bfloat16 or wider, within the bound.
No kernel may reach another device: no remote copies, remote signals or barrier semaphores. Data moves between devices by JAX's collectives and lax.ppermute only.
A program may use at most 384 MiB of HBM per device.

v0:
```python
import jax
import jax.numpy as jnp
from jax import lax
from jax.sharding import PartitionSpec as P

HD = 64


epsilon = 1e-05


def with_halo(block, sides, width):
    for axis, dim in sides:
        count = lax.axis_size(axis)
        forward = [(i, i + 1) for i in range(count - 1)]
        backward = [(target, source) for source, target in forward]
        low = lax.ppermute(
            lax.slice_in_dim(block, block.shape[dim] - width, None, axis=dim), axis, forward
        )
        high = lax.ppermute(lax.slice_in_dim(block, 0, width, axis=dim), axis, backward)
        block = jnp.concatenate([low, block, high], axis=dim)
    return block


def shifted(x, axis, by):
    devices = lax.axis_size(axis)
    pairs = [(i, i + by) for i in range(devices) if 0 <= i + by < devices]
    return lax.ppermute(x, axis, pairs)


def product(left, right):
    return jnp.dot(left, right, preferred_element_type=jnp.float32)


def product_left(left, right):
    return lax.dot_general(
        left, right, (((0,), (0,)), ((), ())), preferred_element_type=jnp.float32
    )


def product_right(left, right):
    return lax.dot_general(
        left, right, (((1,), (1,)), ((), ())), preferred_element_type=jnp.float32
    )


def layer_norm(inputs, gain, shift):
    average = jnp.mean(inputs, -1, keepdims=True)
    centred = inputs - average
    spread = jnp.mean(centred * centred, -1, keepdims=True)
    return centred * lax.rsqrt(spread + epsilon) * gain + shift


def row_places(global_rows, lengths, token_total):
    starts = 2 * (jnp.cumsum(lengths) - lengths)
    before = starts[None, :] <= global_rows[:, None]
    row_of = jnp.sum(before.astype(jnp.int32), 1) - 1
    begin = jnp.max(jnp.where(before, starts[None, :], 0), 1)
    inside = (global_rows >= 0) & (global_rows < token_total)
    return (jnp.where(inside, row_of, -2), (global_rows - begin).astype(jnp.float32))


def local(
    tokens,
    cotangent,
    lengths,
    w_query,
    b_query,
    w_key,
    w_value,
    b_value,
    w_output,
    b_output,
    gain_attn,
    shift_attn,
    w_up,
    b_up,
    w_down,
    b_down,
    gain_ffn,
    shift_ffn,
    distance_slope,
):
    bf_type = jnp.bfloat16
    fl_type = jnp.float32
    low_wq = w_query.astype(bf_type)
    low_bq = b_query.astype(bf_type)
    low_wk = w_key.astype(bf_type)
    low_wv = w_value.astype(bf_type)
    low_bv = b_value.astype(bf_type)
    low_wo = w_output.astype(bf_type)
    low_bo = b_output.astype(bf_type)
    low_g1 = gain_attn.astype(bf_type)
    low_s1 = shift_attn.astype(bf_type)
    low_w1 = w_up.astype(bf_type)
    low_c1 = b_up.astype(bf_type)
    low_w2 = w_down.astype(bf_type)
    low_c2 = b_down.astype(bf_type)
    low_g2 = gain_ffn.astype(bf_type)
    low_s2 = shift_ffn.astype(bf_type)
    (
        query_mat,
        query_bias,
        key_mat,
        value_mat,
        value_bias,
        output_mat,
        output_bias,
        attn_gain,
        attn_shift,
        up_mat,
        up_bias,
        down_mat,
        down_bias,
        ffn_gain,
        ffn_shift,
    ) = (
        lax.all_gather(low_wq, "seq", axis=0, tiled=True),
        lax.all_gather(low_bq, "seq", axis=0, tiled=True),
        lax.all_gather(low_wk, "seq", axis=0, tiled=True),
        lax.all_gather(low_wv, "seq", axis=0, tiled=True),
        lax.all_gather(low_bv, "seq", axis=0, tiled=True),
        lax.all_gather(low_wo, "seq", axis=0, tiled=True),
        lax.all_gather(low_bo, "seq", axis=0, tiled=True),
        lax.all_gather(low_g1, "seq", axis=0, tiled=True),
        lax.all_gather(low_s1, "seq", axis=0, tiled=True),
        lax.all_gather(low_w1, "seq", axis=0, tiled=True),
        lax.all_gather(low_c1, "seq", axis=0, tiled=True),
        lax.all_gather(low_w2, "seq", axis=0, tiled=True),
        lax.all_gather(low_c2, "seq", axis=0, tiled=True),
        lax.all_gather(low_g2, "seq", axis=0, tiled=True),
        lax.all_gather(low_s2, "seq", axis=0, tiled=True),
    )
    rows_here = tokens.shape[0]
    pooled_rows = rows_here // 2
    model_width = tokens.shape[1]
    head_count = model_width // HD
    head_group = 4
    score_scale = HD ** (-0.5)
    span_rows = rows_here + 2 * rows_here
    first_row = lax.axis_index(("dp", "seq")) * rows_here
    token_total = lax.axis_size(("dp", "seq")) * rows_here
    global_rows = first_row - rows_here + jnp.arange(span_rows, dtype=jnp.int32)
    key_row, key_place = row_places(global_rows, lengths, token_total)
    query_row = key_row[rows_here : rows_here + rows_here : 2]
    query_place = key_place[rows_here : rows_here + rows_here : 2] + 0.5
    same_row = query_row[:, None] == key_row[None, :]
    distance = jnp.abs(query_place[:, None] - key_place[None, :])
    tok_float = tokens.astype(fl_type)
    pooled_in = jnp.sum(tok_float.reshape(pooled_rows, 2, model_width), 1) * 0.5
    pooled_low = pooled_in.astype(bf_type)
    query_low = (product(pooled_low, query_mat) + query_bias.astype(fl_type)).astype(bf_type)
    key_float = product(tokens, key_mat)
    value_float = product(tokens, value_mat) + value_bias.astype(fl_type)
    both_low = jnp.stack([key_float, value_float]).astype(bf_type)
    extended = with_halo(both_low, ((("dp", "seq"), 1),), rows_here)
    query_heads = query_low.reshape(pooled_rows, head_count, HD)
    key_heads = extended[0].reshape(span_rows, head_count, HD)
    value_heads = extended[1].reshape(span_rows, head_count, HD)

    def scores_of(q_part, k_part, slope_part):
        raw_scores = (
            jnp.einsum("qhd,khd->hqk", q_part, k_part, preferred_element_type=fl_type) * score_scale
        )
        biased = raw_scores - slope_part[:, None, None] * distance[None]
        return jnp.where(same_row[None], biased, -1000000000.0)

    outputs = []
    totals = []
    for head_start in range(0, head_count, head_group):
        head_end = head_start + head_group
        masked = scores_of(
            query_heads[:, head_start:head_end],
            key_heads[:, head_start:head_end],
            distance_slope[head_start:head_end],
        )
        highest = jnp.max(masked, -1, keepdims=True)
        exponent = jnp.exp(masked - highest)
        denominator = jnp.sum(exponent, -1, keepdims=True)
        probability = (exponent / denominator).astype(bf_type)
        outputs.append(
            jnp.einsum(
                "hqk,khd->qhd",
                probability,
                value_heads[:, head_start:head_end],
                preferred_element_type=fl_type,
            )
        )
        totals.append(highest + jnp.log(denominator))
    attended = jnp.concatenate(outputs, 1).reshape(pooled_rows, model_width).astype(bf_type)
    branch = product(attended, output_mat) + output_bias.astype(fl_type)
    hidden, norm_one_back = jax.vjp(
        layer_norm, pooled_in + branch, attn_gain.astype(fl_type), attn_shift.astype(fl_type)
    )
    hidden_low = hidden.astype(bf_type)
    inner_act = product(hidden_low, up_mat) + up_bias.astype(fl_type)
    active, gelu_back = jax.vjp(jax.nn.gelu, inner_act)
    active_low = active.astype(bf_type)
    ffn_out = product(active_low, down_mat) + down_bias.astype(fl_type)
    result, norm_two_back = jax.vjp(
        layer_norm, hidden + ffn_out, ffn_gain.astype(fl_type), ffn_shift.astype(fl_type)
    )
    pooled_out = result.astype(bf_type)
    d_sum_two, grad_gain_two, grad_shift_two = norm_two_back(cotangent.astype(fl_type))
    d_ffn = d_sum_two.astype(bf_type)
    grad_down_mat = product_left(active_low, d_ffn)
    grad_down_bias = jnp.sum(d_ffn.astype(fl_type), 0)
    d_inner = gelu_back(product_right(d_ffn, down_mat))[0].astype(bf_type)
    grad_up_mat = product_left(hidden_low, d_inner)
    grad_up_bias = jnp.sum(d_inner.astype(fl_type), 0)
    d_hidden = d_sum_two + product_right(d_inner, up_mat)
    d_mixed, grad_gain_one, grad_shift_one = norm_one_back(d_hidden)
    d_branch = d_mixed.astype(bf_type)
    grad_output_mat = product_left(attended, d_branch)
    grad_output_bias = jnp.sum(d_branch.astype(fl_type), 0)
    d_attended = product_right(d_branch, output_mat).astype(bf_type)
    d_att_heads = d_attended.reshape(pooled_rows, head_count, HD)
    query_parts = []
    key_parts = []
    value_parts = []
    slope_parts = []
    for group_index, head_start in enumerate(range(0, head_count, head_group)):
        head_end = head_start + head_group
        q_group = query_heads[:, head_start:head_end]
        k_group = key_heads[:, head_start:head_end]
        v_group = value_heads[:, head_start:head_end]
        att_group = d_att_heads[:, head_start:head_end]
        masked = scores_of(q_group, k_group, distance_slope[head_start:head_end])
        probability = jnp.exp(masked - totals[group_index])
        d_probability = jnp.einsum(
            "qhd,khd->hqk", att_group, v_group, preferred_element_type=fl_type
        )
        value_parts.append(
            jnp.einsum(
                "hqk,qhd->khd",
                probability.astype(bf_type),
                att_group,
                preferred_element_type=fl_type,
            )
        )
        row_carry = jnp.sum(probability * d_probability, -1, keepdims=True)
        d_scores = (probability * (d_probability - row_carry)).astype(bf_type)
        query_parts.append(
            jnp.einsum("hqk,khd->qhd", d_scores, k_group, preferred_element_type=fl_type)
            * score_scale
        )
        key_parts.append(
            jnp.einsum("hqk,qhd->khd", d_scores, q_group, preferred_element_type=fl_type)
            * score_scale
        )
        slope_parts.append(-jnp.sum(d_scores.astype(fl_type) * distance[None], (1, 2)))
    grad_slope = jnp.concatenate(slope_parts, 0)
    d_query = jnp.concatenate(query_parts, 1).reshape(pooled_rows, model_width).astype(bf_type)
    grad_query_mat = product_left(pooled_low, d_query)
    grad_query_bias = jnp.sum(d_query.astype(fl_type), 0)
    d_pooled = d_mixed + product_right(d_query, query_mat)
    d_keys_ext = jnp.concatenate(key_parts, 1).reshape(span_rows, model_width)
    d_values_ext = jnp.concatenate(value_parts, 1).reshape(span_rows, model_width)
    d_both = jnp.stack([d_keys_ext, d_values_ext])
    from_above = shifted(d_both[:, :rows_here].astype(jnp.bfloat16), ("dp", "seq"), -1).astype(
        jnp.float32
    )
    from_below = shifted(
        d_both[:, rows_here + rows_here :].astype(jnp.bfloat16), ("dp", "seq"), 1
    ).astype(jnp.float32)
    d_own = (d_both[:, rows_here : rows_here + rows_here] + from_above + from_below).astype(bf_type)
    d_key = d_own[0]
    d_value = d_own[1]
    grad_key_mat = product_left(tokens, d_key)
    grad_value_mat = product_left(tokens, d_value)
    grad_value_bias = jnp.sum(d_value.astype(fl_type), 0)
    pair_spread = jnp.broadcast_to(
        (d_pooled * 0.5)[:, None, :], (pooled_rows, 2, model_width)
    ).reshape(rows_here, model_width)
    grad_tokens = pair_spread + product_right(d_key, key_mat) + product_right(d_value, value_mat)
    slope_tiled = jnp.tile(grad_slope, lax.axis_size("seq"))
    (
        sum_wq,
        sum_bq,
        sum_wk,
        sum_wv,
        sum_bv,
        sum_wo,
        sum_bo,
        sum_g1,
        sum_s1,
        sum_w1,
        sum_c1,
        sum_w2,
        sum_c2,
        sum_g2,
        sum_s2,
        sum_slope,
    ) = (
        lax.psum(grad_query_mat.astype(jnp.bfloat16), "dp").astype(jnp.float32),
        lax.psum(grad_query_bias.astype(jnp.bfloat16), "dp").astype(jnp.float32),
        lax.psum(grad_key_mat.astype(jnp.bfloat16), "dp").astype(jnp.float32),
        lax.psum(grad_value_mat.astype(jnp.bfloat16), "dp").astype(jnp.float32),
        lax.psum(grad_value_bias.astype(jnp.bfloat16), "dp").astype(jnp.float32),
        lax.psum(grad_output_mat.astype(jnp.bfloat16), "dp").astype(jnp.float32),
        lax.psum(grad_output_bias.astype(jnp.bfloat16), "dp").astype(jnp.float32),
        lax.psum(grad_gain_one.astype(jnp.bfloat16), "dp").astype(jnp.float32),
        lax.psum(grad_shift_one.astype(jnp.bfloat16), "dp").astype(jnp.float32),
        lax.psum(grad_up_mat.astype(jnp.bfloat16), "dp").astype(jnp.float32),
        lax.psum(grad_up_bias.astype(jnp.bfloat16), "dp").astype(jnp.float32),
        lax.psum(grad_down_mat.astype(jnp.bfloat16), "dp").astype(jnp.float32),
        lax.psum(grad_down_bias.astype(jnp.bfloat16), "dp").astype(jnp.float32),
        lax.psum(grad_gain_two.astype(jnp.bfloat16), "dp").astype(jnp.float32),
        lax.psum(grad_shift_two.astype(jnp.bfloat16), "dp").astype(jnp.float32),
        lax.psum(slope_tiled.astype(jnp.bfloat16), "dp").astype(jnp.float32),
    )
    shares = (
        lax.psum_scatter(sum_wq, "seq", scatter_dimension=0, tiled=True),
        lax.psum_scatter(sum_bq, "seq", scatter_dimension=0, tiled=True),
        lax.psum_scatter(sum_wk, "seq", scatter_dimension=0, tiled=True),
        lax.psum_scatter(sum_wv, "seq", scatter_dimension=0, tiled=True),
        lax.psum_scatter(sum_bv, "seq", scatter_dimension=0, tiled=True),
        lax.psum_scatter(sum_wo, "seq", scatter_dimension=0, tiled=True),
        lax.psum_scatter(sum_bo, "seq", scatter_dimension=0, tiled=True),
        lax.psum_scatter(sum_g1, "seq", scatter_dimension=0, tiled=True),
        lax.psum_scatter(sum_s1, "seq", scatter_dimension=0, tiled=True),
        lax.psum_scatter(sum_w1, "seq", scatter_dimension=0, tiled=True),
        lax.psum_scatter(sum_c1, "seq", scatter_dimension=0, tiled=True),
        lax.psum_scatter(sum_w2, "seq", scatter_dimension=0, tiled=True),
        lax.psum_scatter(sum_c2, "seq", scatter_dimension=0, tiled=True),
        lax.psum_scatter(sum_g2, "seq", scatter_dimension=0, tiled=True),
        lax.psum_scatter(sum_s2, "seq", scatter_dimension=0, tiled=True),
        lax.psum_scatter(sum_slope, "seq", scatter_dimension=0, tiled=True),
    )
    return (
        pooled_out,
        grad_tokens,
        shares[0],
        shares[1],
        shares[2],
        shares[3],
        shares[4],
        shares[5],
        shares[6],
        shares[7],
        shares[8],
        shares[9],
        shares[10],
        shares[11],
        shares[12],
        shares[13],
        shares[14],
        shares[15],
    )


def solution(mesh):
    return jax.shard_map(
        local,
        mesh=mesh,
        in_specs=(
            P(("dp", "seq"), None),
            P(("dp", "seq"), None),
            P(),
            P("seq", None),
            P("seq"),
            P("seq", None),
            P("seq", None),
            P("seq"),
            P("seq", None),
            P("seq"),
            P("seq"),
            P("seq"),
            P("seq", None),
            P("seq"),
            P("seq", None),
            P("seq"),
            P("seq"),
            P("seq"),
            P(),
        ),
        out_specs=(
            P(("dp", "seq"), None),
            P(("dp", "seq"), None),
            P("seq", None),
            P("seq"),
            P("seq", None),
            P("seq", None),
            P("seq"),
            P("seq", None),
            P("seq"),
            P("seq"),
            P("seq"),
            P("seq", None),
            P("seq"),
            P("seq", None),
            P("seq"),
            P("seq"),
            P("seq"),
            P(),
        ),
        check_vma=False,
    )
```

profile of v0, /device:TPU:0, one launch (start us, length us, event | category | flops | bytes accessed | tf_op | source)
XLA Modules:
  0.0 1810.0 jit_solution(3686857327707483168)
XLA Ops:
  27.9 78.8 %all-reduce.20 = (bf16[768]{0:T(1024)(128)(2,1)S(1)}, bf16[768]{0:T(1024)(128)(2,1)S(1)}, bf16[768]{0:T(1024)(128)(2,1)S(1)}, bf16[768]{0:T(1024)(128)(2,1)S(1)}...) all-reduce(bf16[768]{0:T(1024)(128)(2,1)S(1)} %dynamic-update-slice, ...), channel_id=1, replica_groups=mesh['dp'=2,'seq'=16] {'seq'}, use_global_device_ids=true, to_apply=%add | all-reduce | flops 9216 | bytes 36864
  116.9 12.0 all-gather.9.cloned.1.call-done
  135.7 6.4 collective-permute-start
  158.8 83.7 %all-gather.11.cloned.1.call-done = bf16[768,768]{1,0:T(8,128)(2,1)} async-done(((bf16[48,768]{1,0:T(8,128)(2,1)}), bf16[768,768]{1,0:T(8,128)(2,1)}) %all-gather.11.cloned.1.call-update) | async-done | bytes 1179664 | tf_op jit(solution)/shard_map/all_gather | solution.py:118
  245.8 35.8 %collective-permute-done = bf16[2,1024,768]{2,1,0:T(8,128)(2,1)} collective-permute-done((bf16[2,1024,768]{2,1,0:T(8,128)(2,1)}, bf16[2,1024,768]{2,1,0:T(8,128)(2,1)}, u32[]{:S(2)}, u32[]{:S(2)}) %collective-permute-start) | collective-permute-done | bytes 3145760 | tf_op jit(solution)/shard_map/ppermute | solution.py:17
  281.6 5.9 pad_maximum_fusion.1
  291.8 6.6 copy.63
  298.4 6.8 copy.65
  305.2 14.9 fusion.104
  320.2 12.4 fusion.105
  332.6 12.3 fusion.106
  344.9 11.6 fusion.2
  356.5 11.0 fusion.81
  367.5 11.7 fusion.1
  379.2 11.0 fusion
  390.3 10.8 fusion.80
  401.1 10.6 fusion.79
  416.0 7.2 fusion.91
  423.2 44.0 %all-gather.17.cloned.1.call-done = bf16[3072,768]{1,0:T(8,128)(2,1)} async-done(((bf16[192,768]{1,0:T(8,128)(2,1)}), bf16[3072,768]{1,0:T(8,128)(2,1)}) %all-gather.17.cloned.1.call-update) | async-done | bytes 4718608 | tf_op jit(solution)/shard_map/all_gather | solution.py:129
  467.1 7.8 fusion.108
  479.5 7.2 fusion.94
  494.1 16.7 multiply_reduce_fusion.5
  510.9 17.0 multiply_reduce_fusion.4
  527.8 16.8 multiply_reduce_fusion.3
  544.6 63.9 %multiply_reduce_fusion.2 = (f32[4]{0:T(128)}, f32[4]{0:T(128)}, f32[4]{0:T(128)}, bf16[4,512,3072]{2,1,0:T(8,128)(2,1)}, bf16[4,512,3072]{2,1,0:T(8,128)(2,1)}, /*index=5*/bf16[4,512,3072]{2,1,0:T(8,128)(2,1)}) fusion(f32[512,3072]{1,0:T(8,128)} %subtract_abs_fusion, f32[4,512,3072]{2,1,0:T(8,128)} %get-tuple-element.172, ...), kind=kLoop, calls=%fused_computation.2 | loop fusion | flops 132120576 | bytes 195084336 | tf_op jit(solution)/shard_map/reduce_sum | solution.py:251
  608.5 9.1 fusion.73
  617.5 8.5 fusion.39
  626.1 9.7 fusion.72
  635.8 8.5 fusion.40
  644.3 12.0 fusion.36
  656.3 12.0 fusion.33
  668.4 11.9 fusion.30
  680.2 8.8 fusion.41
  689.0 7.5 pad_maximum_fusion.2
  696.5 8.8 pad_maximum_fusion.3
  705.3 7.3 fusion.6
  721.2 8.5 fusion.71
  738.9 8.7 convolution_convert_fusion
  747.6 106.2 %collective-permute-done.3 = bf16[2,1024,768]{1,2,0:T(8,128)(2,1)S(1)} collective-permute-done((bf16[2,1024,768]{1,2,0:T(8,128)(2,1)}, bf16[2,1024,768]{1,2,0:T(8,128)(2,1)S(1)}, u32[]{:S(2)}, u32[]{:S(2)}) %collective-permute-start.3) | collective-permute-done | bytes 3145760 | tf_op jit(solution)/shard_map/ppermute | solution.py:28
  864.0 52.7 %all-reduce.25.cloned.1.call-done = (bf16[768,768]{0,1:T(8,128)(2,1)}, bf16[768,768]{0,1:T(8,128)(2,1)}, bf16[768,768]{1,0:T(8,128)(2,1)}, bf16[768,768]{1,0:T(8...) async-done(((bf16[768,768]{0,1:T(8,128)(2,1)}, bf16[768,768]{0,1:T(8,128)(2,1)}, bf16[768,768]{1,0:T(8,128)(2,1)}, bf16[768,768]{1,0:T(8,128)(2,1)}, ...) | async-done | bytes 14155792 | tf_op jit(solution)/shard_map/psum | solution.py:297
  928.3 7.3 convert_element_type.338
  935.9 6.8 convert_element_type.341
  961.1 77.4 %all-reduce.19 = (f32[768]{0:T(1024)S(1)}, f32[768]{0:T(1024)S(1)}, f32[768]{0:T(1024)S(1)}, f32[768]{0:T(1024)S(1)}, f32[768]{0:T(1024)S(1)}, /*index=5*/f32[30...) all-reduce(bf16[768]{0:T(1024)(128)(2,1)S(1)} %get-tuple-element.11, ...), channel_id=3, replica_groups=mesh['dp'=2,'seq'=16] {'seq'}, use_global_device_ids=true, to_apply=%region_26.27.clone | all-reduce | flops 9408 | bytes 56448
  1051.3 133.0 %reduce-scatter.19.cloned.1.call-done = f32[48,768]{1,0:T(8,128)} async-done(((f32[768,768]{1,0:T(8,128)}), f32[48,768]{1,0:T(8,128)}) %reduce-scatter.19.cloned.1.call-update) | async-done | bytes 147472
  1184.3 132.2 %reduce-scatter.21.cloned.1.call-done = f32[48,768]{1,0:T(8,128)} async-done(((f32[768,768]{1,0:T(8,128)}), f32[48,768]{1,0:T(8,128)}) %reduce-scatter.21.cloned.1.call-update) | async-done | bytes 147472
  1316.5 132.9 %reduce-scatter.13.cloned.1.call-done = f32[48,768]{1,0:T(8,128)} async-done(((f32[768,768]{1,0:T(8,128)}), f32[48,768]{1,0:T(8,128)}) %reduce-scatter.13.cloned.1.call-update) | async-done | bytes 147472 | tf_op jit(solution)/shard_map/reduce_scatter | solution.py:318
  1449.4 176.4 %reduce-scatter.15.cloned.1.call-done = f32[48,3072]{1,0:T(8,128)} async-done(((f32[768,3072]{1,0:T(8,128)}), f32[48,3072]{1,0:T(8,128)}) %reduce-scatter.15.cloned.1.call-update) | async-done | bytes 589840 | tf_op jit(solution)/shard_map/reduce_scatter | solution.py:322
  1625.8 177.2 %reduce-scatter.17.cloned.1.call-done = f32[192,768]{1,0:T(8,128)} async-done(((f32[3072,768]{1,0:T(8,128)}), f32[192,768]{1,0:T(8,128)}) %reduce-scatter.17.cloned.1.call-update) | async-done | bytes 589840 | tf_op jit(solution)/shard_map/reduce_scatter | solution.py:324
  (304 shorter events, 145.0 us)
Async XLA Ops:
  7.2 105.4 %all-gather.7.cloned.1.call-start = ((), (), s32[]{:S(2)}) async-start(), calls=%async_computation.6 | async-start | bytes 1253376 | tf_op jit(solution)/shard_map/all_gather | solution.py:120
  8.8 120.1 %all-gather.9.cloned.1.call-start = ((), (), s32[]{:S(2)}) async-start(), calls=%async_computation.7 | async-start | bytes 1253376 | tf_op jit(solution)/shard_map/all_gather | solution.py:121
  10.4 232.1 %all-gather.11.cloned.1.call-start = ((), (), s32[]{:S(2)}) async-start(), calls=%async_computation.8 | async-start | bytes 1253376 | tf_op jit(solution)/shard_map/all_gather | solution.py:118
  12.1 400.7 %all-gather.13.cloned.1.call-start = ((), (), s32[]{:S(2)}) async-start(), calls=%async_computation.9 | async-start | bytes 1253376 | tf_op jit(solution)/shard_map/all_gather | solution.py:123
  13.7 402.3 %all-gather.15.cloned.1.call-start = ((), (), s32[]{:S(2)}) async-start(), calls=%async_computation.10 | async-start | bytes 5013504 | tf_op jit(solution)/shard_map/all_gather | solution.py:127
  15.6 451.6 %all-gather.17.cloned.1.call-start = ((), (), s32[]{:S(2)}) async-start(), calls=%async_computation.11 | async-start | bytes 5013504 | tf_op jit(solution)/shard_map/all_gather | solution.py:129
  17.5 899.2 %all-reduce.25.cloned.1.call-start = ((), (), s32[]{:S(2)}) async-start(), calls=%async_computation.18 | async-start | bytes 28311552 | tf_op jit(solution)/shard_map/psum | solution.py:297
  132.2 10.0 copy-start.40
  132.2 21.0 %copy-start.39 = (f32[12]{0:T(128)S(1)}, f32[12]{0:T(128)}, u32[]{:S(2)}) copy-start(f32[12]{0:T(128)} %param.37) | copy-start | bytes 148
  134.4 111.4 %collective-permute-start.1 = (bf16[2,1024,768]{2,1,0:T(8,128)(2,1)}, bf16[2,1024,768]{2,1,0:T(8,128)(2,1)}, u32[]{:S(2)}, u32[]{:S(2)}) collective-permute-start(bf16[2,1024,768]{2,1,0:T(8,128)(2,1)} %pad_maximum_fusion.4), channel_id=1, source_target_pairs={{1,0},{2,1},{3,2},{4,3},{5,4},{6,5},{7,6},{8,7},{9,8},{10,9},{11,1... | collective-permute-start | bytes 9437192 | tf_op jit(solution)/shard_map/ppermute | solution.py:20
  135.7 145.9 %collective-permute-start = (bf16[2,1024,768]{2,1,0:T(8,128)(2,1)}, bf16[2,1024,768]{2,1,0:T(8,128)(2,1)}, u32[]{:S(2)}, u32[]{:S(2)}) collective-permute-start(bf16[2,1024,768]{2,1,0:T(8,128)(2,1)} %pad_maximum_fusion.4), channel_id=1, source_target_pairs={{0,1},{1,2},{2,3},{3,4},{4,5},{5,6},{6,7},{7,8},{8,9},{9,10},{10,1... | collective-permute-start | bytes 9437192 | tf_op jit(solution)/shard_map/ppermute | solution.py:17
  153.3 89.3 %copy-start.3 = (f32[512,768]{1,0:T(8,128)S(1)}, f32[512,768]{1,0:T(8,128)}, u32[]{:S(2)}) copy-start(f32[512,768]{1,0:T(8,128)} %reduce_sum.304) | copy-start | bytes 4718596
  298.4 21.7 %slice-start.8 = ((s8[6291456]{0:T(1024)(128)(4,1)}), s8[2097152]{0:T(1024)(128)(4,1)S(1)}, s32[]{:S(2)}) async-start(s8[6291456]{0:T(1024)(128)(4,1)} %bitcast.135), calls=%async_computation.27 | async-start | bytes 4194304
  305.2 15.0 copy-start
  305.2 15.0 slice-start.9
  367.5 22.7 %slice-start.10 = ((s8[4718592]{0:T(1024)(128)(4,1)}), s8[4194304]{0:T(1024)(128)(4,1)S(1)}, s32[]{:S(2)}) async-start(s8[4718592]{0:T(1024)(128)(4,1)} %bitcast.141), calls=%async_computation.29 | async-start | bytes 8388608
  379.2 11.0 slice-start.11
  401.1 11.7 copy-start.4
  401.1 11.7 copy-start.44
  415.5 74.8 %copy-start.9 = (f32[512,768]{1,0:T(8,128)}, f32[512,768]{1,0:T(8,128)S(1)}, u32[]{:S(2)}) copy-start(f32[512,768]{1,0:T(8,128)S(1)} %get-tuple-element.167) | copy-start | bytes 4718596
  415.5 74.8 %copy-start.24 = (f32[512]{0:T(512)}, f32[512]{0:T(512)S(1)}, u32[]{:S(2)}) copy-start(f32[512]{0:T(512)S(1)} %broadcast_multiply_fusion.1) | copy-start | bytes 6148
  415.9 74.5 %copy-start.36 = (f32[512]{0:T(512)}, f32[512]{0:T(512)S(1)}, u32[]{:S(2)}) copy-start(f32[512]{0:T(512)S(1)} %fusion.85) | copy-start | bytes 6148
  415.9 51.2 %copy-start.29 = (f32[3072]{0:T(1024)S(1)}, f32[3072]{0:T(1024)}, u32[]{:S(2)}) copy-start(f32[3072]{0:T(1024)} %convert_element_type.294) | copy-start | bytes 36868
  415.9 51.2 %copy-start.43 = (f32[768]{0:T(1024)S(1)}, f32[768]{0:T(1024)}, u32[]{:S(2)}) copy-start(f32[768]{0:T(1024)} %convert_element_type.298) | copy-start | bytes 9220
  423.2 52.1 %copy-start.2 = (bf16[512,768]{1,0:T(8,128)(2,1)S(1)}, bf16[512,768]{1,0:T(8,128)(2,1)}, u32[]{:S(2)}) copy-start(bf16[512,768]{1,0:T(8,128)(2,1)} %param.20) | copy-start | bytes 2359300
  423.2 52.1 %copy-start.23 = (f32[768]{0:T(1024)S(1)}, f32[768]{0:T(1024)}, u32[]{:S(2)}) copy-start(f32[768]{0:T(1024)} %convert_element_type.300) | copy-start | bytes 9220
  423.2 53.4 %copy-start.26 = (f32[768]{0:T(1024)S(1)}, f32[768]{0:T(1024)}, u32[]{:S(2)}) copy-start(f32[768]{0:T(1024)} %convert_element_type.302) | copy-start | bytes 9220
  608.5 9.1 copy-start.17
  696.5 24.6 %slice-start = ((s8[4718592]{0:T(1024)(128)(4,1)}), s8[524288]{0:T(1024)(128)(4,1)S(1)}, s32[]{:S(2)}) async-start(s8[4718592]{0:T(1024)(128)(4,1)} %bitcast.118), calls=%async_computation.19 | async-start | bytes 1048576
  705.3 15.9 slice-start.1
  716.2 137.6 %collective-permute-start.3 = (bf16[2,1024,768]{1,2,0:T(8,128)(2,1)}, bf16[2,1024,768]{1,2,0:T(8,128)(2,1)S(1)}, u32[]{:S(2)}, u32[]{:S(2)}) collective-permute-start(bf16[2,1024,768]{1,2,0:T(8,128)(2,1)} %get-tuple-element.151), channel_id=1, source_target_pairs={{0,1},{1,2},{2,3},{3,4},{4,5},{5,6},{6,7},{7,8},{8,9},{9,10},{10,1... | collective-permute-start | bytes 9437192 | tf_op jit(solution)/shard_map/ppermute | solution.py:28
  719.7 10.0 copy-start.15
  719.7 10.3 copy-start.18
  719.7 10.3 copy-start.22
  719.7 136.0 %collective-permute-start.2 = (bf16[2,1024,768]{1,2,0:T(8,128)(2,1)}, bf16[2,1024,768]{1,2,0:T(8,128)(2,1)}, u32[]{:S(2)}, u32[]{:S(2)}) collective-permute-start(bf16[2,1024,768]{1,2,0:T(8,128)(2,1)} %get-tuple-element.150), channel_id=1, source_target_pairs={{1,0},{2,1},{3,2},{4,3},{5,4},{6,5},{7,6},{8,7},{9,8},{10,9},{11,1... | collective-permute-start | bytes 9437192 | tf_op jit(solution)/shard_map/ppermute | solution.py:28
  733.7 122.0 %slice-start.2 = ((s8[9437184]{0:T(1024)(128)(4,1)}), s8[4194304]{0:T(1024)(128)(4,1)S(1)}, s32[]{:S(2)}) async-start(s8[9437184]{0:T(1024)(128)(4,1)} %bitcast.122), calls=%async_computation.21 | async-start | bytes 8388608
  733.7 122.0 %slice-start.5 = ((s8[9437184]{0:T(1024)(128)(4,1)}), s8[4194304]{0:T(1024)(128)(4,1)S(1)}, s32[]{:S(2)}) async-start(s8[9437184]{0:T(1024)(128)(4,1)} %bitcast.126), calls=%async_computation.24 | async-start | bytes 8388608
  738.8 116.9 %slice-start.3 = ((s8[9437184]{0:T(1024)(128)(4,1)}), s8[4194304]{0:T(1024)(128)(4,1)S(1)}, s32[]{:S(2)}) async-start(s8[9437184]{0:T(1024)(128)(4,1)} %bitcast.122), calls=%async_computation.22 | async-start | bytes 8388608
  738.8 116.9 %slice-start.4 = ((s8[9437184]{0:T(1024)(128)(4,1)}), s8[1048576]{0:T(1024)(128)(4,1)S(1)}, s32[]{:S(2)}) async-start(s8[9437184]{0:T(1024)(128)(4,1)} %bitcast.122), calls=%async_computation.23 | async-start | bytes 2097152
  738.8 116.9 %slice-start.6 = ((s8[9437184]{0:T(1024)(128)(4,1)}), s8[4194304]{0:T(1024)(128)(4,1)S(1)}, s32[]{:S(2)}) async-start(s8[9437184]{0:T(1024)(128)(4,1)} %bitcast.126), calls=%async_computation.25 | async-start | bytes 8388608
  738.8 116.9 %slice-start.7 = ((s8[9437184]{0:T(1024)(128)(4,1)}), s8[1048576]{0:T(1024)(128)(4,1)S(1)}, s32[]{:S(2)}) async-start(s8[9437184]{0:T(1024)(128)(4,1)} %bitcast.126), calls=%async_computation.26 | async-start | bytes 2097152
  747.6 111.6 %copy-start.13 = (bf16[1024,768]{1,0:T(8,128)(2,1)S(1)}, bf16[1024,768]{1,0:T(8,128)(2,1)}, u32[]{:S(2)}) copy-start(bf16[1024,768]{1,0:T(8,128)(2,1)} %param.19) | copy-start | bytes 4718596
  864.0 187.3 %reduce-scatter.11.cloned.1.call-start = ((), (), s32[]{:S(2)}) async-start(), calls=%async_computation.12 | async-start | bytes 2506752 | tf_op jit(solution)/shard_map/reduce_scatter | solution.py:313
  919.6 264.7 %reduce-scatter.19.cloned.1.call-start = ((), (), s32[]{:S(2)}) async-start(), calls=%async_computation.16 | async-start | bytes 2506752
  922.4 394.1 %reduce-scatter.21.cloned.1.call-start = ((), (), s32[]{:S(2)}) async-start(), calls=%async_computation.17 | async-start | bytes 2506752
  925.3 524.1 %reduce-scatter.13.cloned.1.call-start = ((), (), s32[]{:S(2)}) async-start(), calls=%async_computation.13 | async-start | bytes 2506752 | tf_op jit(solution)/shard_map/reduce_scatter | solution.py:318
  928.2 697.6 %reduce-scatter.15.cloned.1.call-start = ((), (), s32[]{:S(2)}) async-start(), calls=%async_computation.14 | async-start | bytes 10027008 | tf_op jit(solution)/shard_map/reduce_scatter | solution.py:322
  935.6 867.4 %reduce-scatter.17.cloned.1.call-start = ((), (), s32[]{:S(2)}) async-start(), calls=%async_computation.15 | async-start | bytes 10027008 | tf_op jit(solution)/shard_map/reduce_scatter | solution.py:324
  (38 other events, 177.6 us)
Sparse Core Ops, SparseCore 0:
  11.4 59.0 all-gather.6
  73.9 55.0 all-gather.8
  132.3 110.1 all-gather.10
  245.8 56.3 all-gather.12
  305.4 79.3 all-gather.14
  388.0 79.0 all-gather.16
  864.1 52.5 all-reduce.24
  922.2 129.0 reduce-scatter.10
  1057.6 126.6 reduce-scatter.18
  1189.6 126.8 reduce-scatter.20
  1322.7 126.5 reduce-scatter.12
  1455.5 170.2 reduce-scatter.14
  1633.0 169.9 reduce-scatter.16
where the time goes:
time: 1820 us; the launch traced here: 1810 us
  waiting for transfers between devices  1090 us (60%)
  matrix products  282 us (15%)
  other arithmetic  196 us (11%)
  blocking collectives  160 us (9%)
  local copies, waits for them, and re-layouts  51.3 us (3%)
  between operations  18.6 us (1%)
    unnamed x15, waiting for transfers between devices  265 us
    reduce_scatter x1, waiting for transfers between devices, local(): lax.psum_scatter(sum_w2, 'seq', scatter_dimension=0, tiled=True)  177 us
    reduce_scatter x1, waiting for transfers between devices, local(): lax.psum_scatter(sum_w1, 'seq', scatter_dimension=0, tiled=True)  176 us
    unnamed x2, blocking collectives  156 us
    reduce_scatter x1, waiting for transfers between devices, local(): lax.psum_scatter(sum_wo, 'seq', scatter_dimension=0, tiled=True)  133 us
    ppermute x2, waiting for transfers between devices, shifted(): return lax.ppermute(x, axis, pairs)  108 us
    all_gather x1, waiting for transfers between devices, local(): lax.all_gather(low_wq, 'seq', axis=0, tiled=True)  83.7 us
    reduce_sum x1, other arithmetic, local(): jnp.sum(d_scores.astype(fl_type) * distance[None], (1, 2))  63.9 us
  transfers between devices with their start and end apart: 17, of which 13 were waited for; matrix products, arithmetic and copies ran while one was open for 15% of the time, Pallas kernels for 0%

commit v1 on v0

v1 whole, which is shorter than its diff:
```python
import jax
import jax.numpy as jnp
from jax import lax
from jax.experimental import pallas as pl
from jax.experimental.pallas import tpu as pltpu
from jax.sharding import PartitionSpec as P

HD = 64
NB = 16
QB = 128
KC = 256
EPS = 1e-05
FAR = 1e12
BF = jnp.bfloat16
FL = jnp.float32


def rel_a(p):
    return (p & 1) * 8 + ((p >> 1) & 1) * 4 + ((p >> 2) & 1) * 2 + ((p >> 3) & 1)


def rel_b(p):
    return (p & 1) * 8 + ((p >> 1) & 1) * 4 + ((p >> 2) & 1) + ((p >> 3) & 1) * 2


def dot(a, b):
    return jnp.dot(a, b, preferred_element_type=FL)


def dot_t(a, b):
    return lax.dot_general(a, b, (((1,), (1,)), ((), ())), preferred_element_type=FL)


def t_dot(a, b):
    return lax.dot_general(a, b, (((0,), (0,)), ((), ())), preferred_element_type=FL)


def exchange(x, stride_a, stride_b):
    n = lax.axis_size("seq")
    pairs = [(s, s ^ stride_a) for s in range(n)] + [(n + s, n + (s ^ stride_b)) for s in range(n)]
    return lax.ppermute(x, ("dp", "seq"), pairs)


def swap_core(x):
    return lax.ppermute(x, "dp", [(0, 1), (1, 0)])


def gather_set(x):
    x = jnp.concatenate([x, exchange(x, 8, 8)], 0)
    x = jnp.concatenate([x, exchange(x, 4, 4)], 0)
    low = jnp.concatenate([x, exchange(x, 2, 1)], 0)
    high = exchange(low, 1, 2)
    return low, high, swap_core(low), swap_core(high)


def add(*xs):
    total = xs[0].astype(FL)
    for x in xs[1:]:
        total = total + x.astype(FL)
    return total


def reduce_set(keep, send):
    got = swap_core(send)
    up = add(keep[8:], got[8:]).astype(BF)
    got1 = exchange(up, 1, 2)
    up = add(keep[4:8], got[4:8], got1[4:]).astype(BF)
    low = add(keep[:4], got[:4], got1[:4])
    got2 = exchange(up, 2, 1)
    up = (low[2:] + got2[2:].astype(FL)).astype(BF)
    low = low[:2] + got2[:2].astype(FL)
    got3 = exchange(up, 4, 4)
    up = (low[1:] + got3[1:].astype(FL)).astype(BF)
    low = low[:1] + got3[:1].astype(FL)
    got4 = exchange(up, 8, 8)
    mine = (low + got4.astype(FL))[0]
    other = swap_core(mine)
    first = lax.axis_index("dp") == 0
    return jnp.where(first, mine, other), jnp.where(first, other, mine)


def params(**kw):
    return pltpu.CompilerParams(vmem_limit_bytes=58 * 1024 * 1024, **kw)


ANY = pl.BlockSpec(memory_space=pl.ANY)


def load_sets(ids, low, high, olow, ohigh, copies_a, copies_b):
    def start(a_refs, b_refs):
        for p in range(NB):
            copies_a(a_refs[p // 8].at[p % 8], ids[0] ^ rel_a(p), p)
            copies_b(b_refs[p // 8].at[p % 8], ids[0] ^ rel_b(p), p)

    @pl.when(ids[1] == 0)
    def _():
        start((low, high), (olow, ohigh))

    @pl.when(ids[1] != 0)
    def _():
        start((olow, ohigh), (low, high))


def wait_all(ref, sem):
    pltpu.make_async_copy(ref, ref, sem).wait()


def spread_matrix(rows, cols, rb):
    lanes = lax.broadcasted_iota(jnp.int32, (rows, cols), 1)
    return (lax.broadcasted_iota(jnp.int32, (rows, cols), 0) == lanes - rb * div_rb(lanes)).astype(FL).astype(BF)


def div_rb(x):
    return (x * 21846) >> 20


def qkv_kernel(
    ids, tok, low, high, olow, ohigh, q_out, k_out, v_out, pool_out, wq, wk, wv, vec_out, up_out, bias, x32, sems
):
    width = tok.shape[1]
    rb = width // NB

    @pl.when(pl.program_id(0) == 0)
    def _():
        def rows(r, n):
            return pl.ds(pl.multiple_of(r, 16), n)

        def copies_a(block, s, p):
            pltpu.make_async_copy(block.at[pl.ds(0, 48)], wq.at[rows(s * rb, 48)], sems.at[0]).start()
            pltpu.make_async_copy(block.at[pl.ds(48, 32)], wk.at[rows(s * rb, 32)], sems.at[1]).start()

        def copies_b(block, s, p):
            pltpu.make_async_copy(block.at[pl.ds(0, 16)], wk.at[rows(s * rb + 32, 16)], sems.at[1]).start()
            pltpu.make_async_copy(block.at[pl.ds(16, 48)], wv.at[rows(s * rb, 48)], sems.at[2]).start()
            pltpu.make_async_copy(block.at[pl.ds(64, 16)], bias.at[pl.ds(16 * p, 16)], sems.at[3]).start()

        load_sets(ids, low, high, olow, ohigh, copies_a, copies_b)
        wait_all(wq, sems.at[0])
        wait_all(wk, sems.at[1])
        wait_all(wv, sems.at[2])
        wait_all(bias, sems.at[3])
        parts = bias[:, 0:128]
        wide = dot(parts, spread_matrix(128, width, rb))
        block_of = div_rb(lax.broadcasted_iota(jnp.int32, (16, width), 1))
        total = jnp.zeros((16, width), FL)
        for p in range(NB):
            total = total + jnp.where(block_of == (ids[0] ^ rel_b(p)), wide[16 * p : 16 * p + 16], 0.0)
        vec_out[...] = total
        ff = up_out.shape[1]
        wide = dot(parts, spread_matrix(128, ff, rb))
        block_of = div_rb(lax.broadcasted_iota(jnp.int32, (16, ff), 1))
        row = lax.broadcasted_iota(jnp.int32, (16, ff), 0)
        block_of = jnp.where((row >= 8) & (row < 12), block_of - row + 8, -1)
        total = jnp.zeros((16, ff), FL)
        for p in range(NB):
            total = total + jnp.where(block_of == 4 * (ids[0] ^ rel_b(p)), wide[16 * p : 16 * p + 16], 0.0)
        up_out[...] = jnp.broadcast_to(jnp.sum(total, 0, keepdims=True), up_out.shape)

    x = tok[...]
    half = x.shape[0] // 2
    k_out[...] = dot(x, wk[...]).astype(BF)
    v_out[...] = (dot(x, wv[...]) + vec_out[1:2]).astype(BF)
    for j in range(width // 128):
        cols = slice(128 * j, 128 * j + 128)
        x32[j] = x[:, cols].astype(FL)
        pool_out[:, cols] = (x32[j, pl.ds(0, half, stride=2)] + x32[j, pl.ds(1, half, stride=2)]) * 0.5
    q = (dot(pool_out[...].astype(BF), wq[...]) + vec_out[0:1]).astype(BF)
    q_out[...] = (q.astype(FL) * HD**-0.5).astype(BF)


def qkv(ids, tok_ext, sets, ff):
    rows, width = tok_ext.shape
    step = 512
    whole = lambda i, *_: (0, 0)
    return pl.pallas_call(
        qkv_kernel,
        name="qkv",
        grid_spec=pltpu.PrefetchScalarGridSpec(
            num_scalar_prefetch=1,
            grid=(rows // step,),
            in_specs=[pl.BlockSpec((step, width), lambda i, *_: (i, 0)), ANY, ANY, ANY, ANY],
            out_specs=[
                pl.BlockSpec((step // 2, width), lambda i, *_: (i, 0)),
                pl.BlockSpec((step, width), lambda i, *_: (i, 0)),
                pl.BlockSpec((step, width), lambda i, *_: (i, 0)),
                pl.BlockSpec((step // 2, width), lambda i, *_: (i, 0)),
                pl.BlockSpec((width, width), whole),
                pl.BlockSpec((width, width), whole),
                pl.BlockSpec((width, width), whole),
                pl.BlockSpec((16, width), whole),
                pl.BlockSpec((8, ff), whole),
            ],
            scratch_shapes=[
                pltpu.VMEM((16 * NB, width), BF),
                pltpu.VMEM((width // 128, step, 128), FL),
                pltpu.SemaphoreType.DMA((4,)),
            ],
        ),
        out_shape=[
            jax.ShapeDtypeStruct((rows // 2, width), BF),
            jax.ShapeDtypeStruct((rows, width), BF),
            jax.ShapeDtypeStruct((rows, width), BF),
            jax.ShapeDtypeStruct((rows // 2, width), FL),
            jax.ShapeDtypeStruct((width, width), BF),
            jax.ShapeDtypeStruct((width, width), BF),
            jax.ShapeDtypeStruct((width, width), BF),
            jax.ShapeDtypeStruct((16, width), FL),
            jax.ShapeDtypeStruct((8, ff), FL),
        ],
        compiler_params=params(),
    )(ids, tok_ext, *sets)


def two_heads(x):
    lane = lax.broadcasted_iota(jnp.int32, x.shape, 1)
    zero = jnp.zeros_like(x)
    return jnp.concatenate([jnp.where(lane < HD, x, zero), jnp.where(lane < HD, zero, x)], 0)


def one_block(x):
    r = x.shape[0] // 2
    lane = lax.broadcasted_iota(jnp.int32, (r, 128), 1)
    return jnp.where(lane < HD, x[:r], x[r:])


def distances(bounds, row, c):
    low = bounds[pl.ds(row, QB), 0:1]
    high = bounds[pl.ds(row, QB), 1:2]
    query = (2 * (row + lax.broadcasted_iota(jnp.int32, (QB, KC), 0))).astype(FL) + 0.5
    key = (c * KC + lax.broadcasted_iota(jnp.int32, (QB, KC), 1)).astype(FL)
    return jnp.where((key >= low) & (key < high), jnp.abs(query - key), FAR)


def twice(x):
    return jnp.concatenate([x, x], 1)


def forward_kernel(spans, slopes, q, k, v, bounds, o_out, exact_out, lse_out, s_scr, q2, top, total, acc, rest):
    pairs = q.shape[1] // 128
    head0 = pl.program_id(0) * 2 * pairs
    lane = lax.broadcasted_iota(jnp.int32, (QB, 128), 1)
    q_first = q.shape[0] // 4

    def query_block(b, _):
        row = pl.multiple_of(q_first + b * QB, QB)
        out_rows = pl.ds(pl.multiple_of(b * QB, QB), QB)
        block = row // QB
        c0 = spans[block]
        c1 = spans[spans.shape[0] // 2 + block]
        for j in range(pairs):
            q2[j] = two_heads(q[pl.ds(row, QB), 128 * j : 128 * j + 128])
        top[...] = jnp.full(top.shape, -3e38, FL)
        total[...] = jnp.zeros(total.shape, FL)
        acc[...] = jnp.zeros(acc.shape, FL)
        rest[...] = jnp.zeros(rest.shape, FL)

        def score(c, _):
            far = distances(bounds, row, c)
            keys = pl.ds(pl.multiple_of(c * KC, KC), KC)
            for j in range(pairs):
                s = dot_t(q2[j], k[keys, 128 * j : 128 * j + 128])
                s = jnp.concatenate(
                    [s[:QB] - slopes[head0 + 2 * j] * far, s[QB:] - slopes[head0 + 2 * j + 1] * far], 0
                )
                s_scr[c - c0, j] = s
                top[j] = jnp.maximum(top[j], jnp.maximum(s[:, :128], s[:, 128:]))
            return 0

        lax.fori_loop(c0, c1, score, 0)
        for j in range(pairs):
            top[j] = jnp.broadcast_to(jnp.max(top[j], 1, keepdims=True), (2 * QB, 128))

        def exponent(c, _):
            for j in range(pairs):
                e = jnp.exp(s_scr[c - c0, j] - twice(top[j]))
                s_scr[c - c0, j] = e
                total[j] = total[j] + (e[:, :128] + e[:, 128:])
            return 0

        lax.fori_loop(c0, c1, exponent, 0)
        lse = jnp.zeros((QB, 128), FL)
        for j in range(pairs):
            l = jnp.broadcast_to(jnp.sum(total[j], 1, keepdims=True), (2 * QB, 128))
            t = top[j] + jnp.log(l)
            total[j] = 1.0 / l
            lse = jnp.where(lane == 2 * j, t[:QB], jnp.where(lane == 2 * j + 1, t[QB:], lse))
        lse_out[out_rows, :] = lse

        def attend(c, _):
            keys = pl.ds(pl.multiple_of(c * KC, KC), KC)
            for j in range(pairs):
                p = s_scr[c - c0, j] * twice(total[j])
                high = p.astype(BF)
                low = (p - high.astype(FL)).astype(BF)
                values = v[keys, 128 * j : 128 * j + 128]
                acc[j] = acc[j] + dot(high, values)
                rest[j] = rest[j] + dot(low, values)
            return 0

        lax.fori_loop(c0, c1, attend, 0)
        for j in range(pairs):
            cols = slice(128 * j, 128 * j + 128)
            o_out[out_rows, cols] = one_block(acc[j]).astype(BF)
            exact_out[out_rows, cols] = one_block(acc[j] + rest[j])
        return 0

    lax.fori_loop(0, o_out.shape[0] // QB, query_block, 0)


def attend_forward(spans, slopes, q, k, v, bounds, own):
    width = q.shape[1]
    wide = width // 2
    pairs = wide // 128
    chunks = k.shape[0] // KC
    col = lambda i, *_: (0, i)
    return pl.pallas_call(
        forward_kernel,
        name="attend_forward",
        grid_spec=pltpu.PrefetchScalarGridSpec(
            num_scalar_prefetch=2,
            grid=(2,),
            in_specs=[
                pl.BlockSpec((q.shape[0], wide), col),
                pl.BlockSpec((k.shape[0], wide), col),
                pl.BlockSpec((k.shape[0], wide), col),
                pl.BlockSpec(bounds.shape, lambda i, *_: (0, 0)),
            ],
            out_specs=[
                pl.BlockSpec((own, wide), col),
                pl.BlockSpec((own, wide), col),
                pl.BlockSpec((own, 128), col),
            ],
            scratch_shapes=[
                pltpu.VMEM((chunks, pairs, 2 * QB, KC), FL),
                pltpu.VMEM((pairs, 2 * QB, 128), BF),
                pltpu.VMEM((pairs, 2 * QB, 128), FL),
                pltpu.VMEM((pairs, 2 * QB, 128), FL),
                pltpu.VMEM((pairs, 2 * QB, 128), FL),
                pltpu.VMEM((pairs, 2 * QB, 128), FL),
            ],
        ),
        out_shape=[
            jax.ShapeDtypeStruct((own, width), BF),
            jax.ShapeDtypeStruct((own, width), FL),
            jax.ShapeDtypeStruct((own, 256), FL),
        ],
        compiler_params=params(),
    )(spans, slopes, q, k, v, bounds)


def backward_kernel(
    spans, slopes, q, k, v, da, stats, bounds, dq_out, dk_out, dv_out, slope_out, q2, da2, lse2, del2, dq2, dk, dv, sl
):
    pairs = q.shape[1] // 128
    head0 = pl.program_id(0) * 2 * pairs
    blocks = q.shape[0] // QB
    dk[...] = jnp.zeros(dk.shape, FL)
    dv[...] = jnp.zeros(dv.shape, FL)
    sl[...] = jnp.zeros(sl.shape, FL)

    def query_block(b, _):
        row = pl.multiple_of(b * QB, QB)
        c0 = spans[b]
        c1 = spans[blocks + b]
        own = (b >= blocks // 4) & (b < blocks - blocks // 4)
        counted = jnp.where(own, 1.0, 0.0)
        for j in range(pairs):
            cols = slice(128 * j, 128 * j + 128)
            q2[j] = two_heads(q[pl.ds(row, QB), cols])
            da2[j] = two_heads(da[pl.ds(row, QB), cols])
            for i in range(2):
                rows = slice(QB * i, QB * i + QB)
                lse2[j, rows] = jnp.broadcast_to(stats[pl.ds(row, QB), 2 * j + i : 2 * j + i + 1], (QB, 128))
                del2[j, rows] = jnp.broadcast_to(stats[pl.ds(row, QB), 64 + 2 * j + i : 65 + 2 * j + i], (QB, 128))
        dq2[...] = jnp.zeros(dq2.shape, FL)

        def chunk(c, _):
            far = distances(bounds, row, c)
            keys = pl.ds(pl.multiple_of(c * KC, KC), KC)
            for j in range(pairs):
                cols = slice(128 * j, 128 * j + 128)
                kj = k[keys, cols]
                s = dot_t(q2[j], kj)
                s = jnp.concatenate(
                    [s[:QB] - slopes[head0 + 2 * j] * far, s[QB:] - slopes[head0 + 2 * j + 1] * far], 0
                )
                p = jnp.exp(s - twice(lse2[j]))
                dp = dot_t(da2[j], v[keys, cols])
                ds = (p * (dp - twice(del2[j]))).astype(BF)
                dv[keys, cols] = dv[keys, cols] + t_dot(p.astype(BF), da2[j])
                dk[keys, cols] = dk[keys, cols] + t_dot(ds, q2[j])
                dq2[j] = dq2[j] + dot(ds, kj)
                for i in range(2):
                    w = ds[QB * i : QB * i + QB].astype(FL) * far
                    w = jnp.sum(w.reshape(QB // 8, 8, KC), 0)
                    sl[2 * j + i] = sl[2 * j + i] + counted * (w[:, :128] + w[:, 128:])
            return 0

        lax.fori_loop(c0, c1, chunk, 0)

        @pl.when(own)
        def _():
            out_rows = pl.ds(pl.multiple_of(row - q.shape[0] // 4, QB), QB)
            for j in range(pairs):
                dq_out[out_rows, 128 * j : 128 * j + 128] = (one_block(dq2[j]) * HD**-0.5).astype(BF)

        return 0

    lax.fori_loop(0, blocks, query_block, 0)
    quarter = k.shape[0] // 4
    dk_out[...] = dk[quarter : 3 * quarter].astype(BF)
    dv_out[...] = dv[quarter : 3 * quarter].astype(BF)
    slope_out[...] = sl[...].reshape(slope_out.shape)


def attend_backward(spans, slopes, q, k, v, da, stats, bounds):
    width = q.shape[1]
    wide = width // 2
    pairs = wide // 128
    rows = q.shape[0]
    keys = k.shape[0]
    col = lambda i, *_: (0, i)
    return pl.pallas_call(
        backward_kernel,
        name="attend_backward",
        grid_spec=pltpu.PrefetchScalarGridSpec(
            num_scalar_prefetch=2,
            grid=(2,),
            in_specs=[
                pl.BlockSpec((rows, wide), col),
                pl.BlockSpec((keys, wide), col),
                pl.BlockSpec((keys, wide), col),
                pl.BlockSpec((rows, wide), col),
                pl.BlockSpec((rows, 128), col),
                pl.BlockSpec(bounds.shape, lambda i, *_: (0, 0)),
            ],
            out_specs=[
                pl.BlockSpec((rows // 2, wide), col),
                pl.BlockSpec((keys // 2, wide), col),
                pl.BlockSpec((keys // 2, wide), col),
                pl.BlockSpec((16 * pairs, 128), lambda i, *_: (i, 0)),
            ],
            scratch_shapes=[
                pltpu.VMEM((pairs, 2 * QB, 128), BF),
                pltpu.VMEM((pairs, 2 * QB, 128), BF),
                pltpu.VMEM((pairs, 2 * QB, 128), FL),
                pltpu.VMEM((pairs, 2 * QB, 128), FL),
                pltpu.VMEM((pairs, 2 * QB, 128), FL),
                pltpu.VMEM((keys, wide), FL),
                pltpu.VMEM((keys, wide), FL),
                pltpu.VMEM((2 * pairs, 8, 128), FL),
            ],
        ),
        out_shape=[
            jax.ShapeDtypeStruct((rows // 2, width), BF),
            jax.ShapeDtypeStruct((keys // 2, width), BF),
            jax.ShapeDtypeStruct((keys // 2, width), BF),
            jax.ShapeDtypeStruct((32 * pairs, 128), FL),
        ],
        compiler_params=params(),
    )(spans, slopes, q, k, v, da, stats, bounds)


def normalize(z):
    centred = z - jnp.mean(z, -1, keepdims=True)
    scale = lax.rsqrt(jnp.mean(centred * centred, -1, keepdims=True) + EPS)
    return centred * scale, scale


def normalize_back(d, unit, scale):
    return scale * (d - jnp.mean(d, -1, keepdims=True) - unit * jnp.mean(d * unit, -1, keepdims=True))


def rows_sum(x):
    return jnp.sum(x, 0, keepdims=True)


def middle_kernel(
    ids,
    pool,
    att,
    exact,
    lse,
    cot,
    vec,
    upb,
    low,
    high,
    olow,
    ohigh,
    out,
    pay,
    stats,
    mixed,
    gvec,
    gup,
    keep,
    send,
    wo,
    w1,
    w2,
    active,
    slope,
    unit1,
    hid,
    hid_low,
    z,
    d2,
    dw1,
    dw2,
    dwo,
    sems,
):
    n, width = att.shape
    rb = width // NB
    fb = w2.shape[0] // NB
    parts = w1.shape[0]

    def rows(r, size):
        return pl.ds(pl.multiple_of(r, 16), size)

    def copies_a(block, s, p):
        pltpu.make_async_copy(block.at[pl.ds(192, 32)], wo.at[rows(s * rb, 32)], sems.at[0]).start()
        pltpu.make_async_copy(block.at[pl.ds(0, 192)], w2.at[rows(s * fb, 192)], sems.at[2]).start()

    def copies_b(block, s, p):
        pltpu.make_async_copy(block.at[pl.ds(192, 16)], wo.at[rows(s * rb + 32, 16)], sems.at[0]).start()
        for c in range(parts):
            pltpu.make_async_copy(block.at[pl.ds(48 * c, 48)], w1.at[c, rows(s * rb, 48)], sems.at[1]).start()

    load_sets(ids, low, high, olow, ohigh, copies_a, copies_b)
    wait_all(wo, sems.at[0])
    z[...] = dot(att[...], wo[...])
    rc = 128

    def row_loop(f):
        def body(i, _):
            f(pl.ds(pl.multiple_of(i * rc, rc), rc), i)
            return 0

        lax.fori_loop(0, n // rc, body, 0)

    def first_norm(r, i):
        unit, scale = normalize(pool[r, :] + z[r, :] + vec[2:3])
        h = unit * vec[3:4] + vec[4:5]
        unit1[r, :] = unit
        d2[r, 0:128] = jnp.broadcast_to(scale, (rc, 128))
        hid[r, :] = h
        hid_low[r, :] = h.astype(BF)

    row_loop(first_norm)
    wait_all(w1, sems.at[1])
    wait_all(w2, sems.at[2])
    c0 = 0.7978845608028654

    def up(c, _):
        inner = dot(hid_low[...], w1[c]) + upb[pl.ds(0, 1), pl.ds(pl.multiple_of(c * width, 128), width)]
        sq = inner * inner
        t = jnp.tanh(c0 * (inner + 0.044715 * (inner * sq)))
        cdf = 0.5 * (1.0 + t)
        active[c] = (inner * cdf).astype(BF)
        slope[c] = cdf + inner * (0.5 * (1.0 - t * t)) * (c0 + (3 * 0.044715 * c0) * sq)
        return 0

    lax.fori_loop(0, parts, up, 0)
    z[...] = dot(active[0], w2[pl.ds(0, width), :])
    for c in range(1, parts):
        z[...] = z[...] + dot(active[c], w2[pl.ds(c * width, width), :])
    gvec[...] = jnp.zeros(gvec.shape, FL)

    def second_norm(r, i):
        unit, scale = normalize(hid[r, :] + (z[r, :] + vec[5:6]))
        out[r, :] = (unit * vec[6:7] + vec[7:8]).astype(BF)
        dy = cot[r, :].astype(FL)
        gvec[6:7] = gvec[6:7] + rows_sum(dy * unit)
        gvec[7:8] = gvec[7:8] + rows_sum(dy)
        d = normalize_back(dy * vec[6:7], unit, scale)
        hid[r, :] = d
        d_low = d.astype(BF)
        att_like[r, :] = d_low
        gvec[5:6] = gvec[5:6] + rows_sum(d_low.astype(FL))

    att_like = pay.at[:, 0:width]
    scale1 = d2[:, 0:1]
    row_loop(second_norm)
    z[...] = jnp.zeros(z.shape, FL)

    def down(c, _):
        ffn = pay[:, 0:width]
        far = pl.ds(pl.multiple_of(c * width, 128), width)
        d_inner = (dot_t(ffn, w2[far, :]) * slope[c]).astype(BF)
        gup[:, far] = jnp.broadcast_to(rows_sum(d_inner.astype(FL)), (8, width))
        dw2[far, :] = t_dot(active[c], ffn).astype(BF)
        dw1[c] = t_dot(hid_low[...], d_inner).astype(BF)
        z[...] = z[...] + dot_t(d_inner, w1[c])
        return 0

    lax.fori_loop(0, parts, down, 0)

    def store_sets(a_ref, b_ref):
        for p in range(NB):
            s = ids[0] ^ rel_a(p)
            pltpu.make_async_copy(dw2.at[rows(s * fb, 192)], a_ref.at[p, pl.ds(0, 192)], sems.at[3]).start()
            s = ids[0] ^ rel_b(p)
            for c in range(parts):
                pltpu.make_async_copy(
                    dw1.at[c, rows(s * rb, 48)], b_ref.at[p, pl.ds(48 * c, 48)], sems.at[3]
                ).start()

    @pl.when(ids[1] == 0)
    def _():
        store_sets(keep, send)

    @pl.when(ids[1] != 0)
    def _():
        store_sets(send, keep)

    def first_back(r, i):
        unit = unit1[r, :]
        d = hid[r, :] + z[r, :]
        gvec[3:4] = gvec[3:4] + rows_sum(d * unit)
        gvec[4:5] = gvec[4:5] + rows_sum(d)
        d = normalize_back(d * vec[3:4], unit, d2[r, 0:1])
        mixed[r, :] = d
        d_low = d.astype(BF)
        hid_low[r, :] = d_low
        gvec[2:3] = gvec[2:3] + rows_sum(d_low.astype(FL))

    row_loop(first_back)
    dwo[...] = t_dot(att[...], hid_low[...]).astype(BF)

    def store_wo(a_ref, b_ref):
        for p in range(NB):
            s = ids[0] ^ rel_a(p)
            pltpu.make_async_copy(dwo.at[rows(s * rb, 32)], a_ref.at[p, pl.ds(192, 32)], sems.at[3]).start()
            s = ids[0] ^ rel_b(p)
            pltpu.make_async_copy(dwo.at[rows(s * rb + 32, 16)], b_ref.at[p, pl.ds(192, 16)], sems.at[3]).start()
            pltpu.make_async_copy(dwo.at[rows(s * rb + 32, 16)], b_ref.at[p, pl.ds(208, 16)], sems.at[3]).start()

    @pl.when(ids[1] == 0)
    def _():
        store_wo(keep, send)

    @pl.when(ids[1] != 0)
    def _():
        store_wo(send, keep)

    z[...] = dot_t(hid_low[...], wo[...])
    heads = width // HD
    head_of = (lax.broadcasted_iota(jnp.int32, (width, 256), 0)) // HD
    spot = lax.broadcasted_iota(jnp.int32, (width, 256), 1)
    half = heads // 2
    spot_of = jnp.where(head_of < half, head_of + 64, head_of - half + 128 + 64)
    pick = (spot == spot_of).astype(FL).astype(BF)

    def last(r, i):
        d_low = z[r, :].astype(BF)
        prod = d_low.astype(FL) * exact[r, :]
        delta = jnp.zeros((rc, 256), FL)
        for _ in range(3):
            piece = prod.astype(BF)
            delta = delta + dot(piece, pick)
            prod = prod - piece.astype(FL)
        st = jnp.where(lax.broadcasted_iota(jnp.int32, (rc, 256), 1) % 128 < 64, lse[r, :], delta)
        stats[r, :] = st
        pay[r, 0:width] = d_low
        for j in range(3):
            piece = st.astype(BF)
            pay[r, width + 256 * j : width + 256 * j + 256] = piece
            st = st - piece.astype(FL)

    row_loop(last)
    wait_all(keep, sems.at[3])
    wait_all(send, sems.at[3])


def middle(ids, pool, att, exact, lse, cot, vec, upb, sets, set_rows):
    n, width = att.shape
    ff = upb.shape[1]
    parts = ff // width
    whole = lambda i, *_: (0, 0)
    full = lambda x: pl.BlockSpec(x.shape, whole)
    shapes = [
        jax.ShapeDtypeStruct((n, width), BF),
        jax.ShapeDtypeStruct((n, width + 768), BF),
        jax.ShapeDtypeStruct((n, 256), FL),
        jax.ShapeDtypeStruct((n, width), FL),
        jax.ShapeDtypeStruct((8, width), FL),
        jax.ShapeDtypeStruct((8, ff), FL),
    ]
    big = jax.ShapeDtypeStruct((NB, set_rows, width), BF)
    return pl.pallas_call(
        middle_kernel,
        name="middle",
        grid_spec=pltpu.PrefetchScalarGridSpec(
            num_scalar_prefetch=1,
            grid=(1,),
            in_specs=[full(pool)]
            + [full(x) for x in (att, exact, lse, cot, vec, upb)]
            + [ANY] * 4,
            out_specs=[full(x) for x in shapes] + [ANY, ANY],
            scratch_shapes=[
                pltpu.VMEM((width, width), BF),
                pltpu.VMEM((parts, width, width), BF),
                pltpu.VMEM((ff, width), BF),
                pltpu.VMEM((parts, n, width), BF),
                pltpu.VMEM((parts, n, width), FL),
                pltpu.VMEM((n, width), FL),
                pltpu.VMEM((n, width), FL),
                pltpu.VMEM((n, width), BF),
                pltpu.VMEM((n, width), FL),
                pltpu.VMEM((n, 128), FL),
                pltpu.VMEM((parts, width, width), BF),
                pltpu.VMEM((ff, width), BF),
                pltpu.VMEM((width, width), BF),
                pltpu.SemaphoreType.DMA((4,)),
            ],
        ),
        out_shape=shapes + [big, big],
        compiler_params=params(),
    )(ids, pool, att, exact, lse, cot, vec, upb, *sets)


def weights_kernel(ids, pool, tok, dq, dk, dv, gvec, gup, sl, keep, send, dwq, dwk, dwv, bias, sems):
    width = tok.shape[1]
    ff = gup.shape[1]
    rb = width // NB
    dwq[...] = t_dot(pool[...].astype(BF), dq[...]).astype(BF)
    dwk[...] = t_dot(tok[...], dk[...]).astype(BF)
    dwv[...] = t_dot(tok[...], dv[...]).astype(BF)
    row = lax.broadcasted_iota(jnp.int32, (16, width), 0)
    g = jnp.concatenate([gvec[...], jnp.zeros((8, width), FL)], 0)
    g = jnp.where(row == 0, rows_sum(dq[...].astype(FL)), g)
    g = jnp.where(row == 1, rows_sum(dv[...].astype(FL)), g)
    block_of = div_rb(lax.broadcasted_iota(jnp.int32, (16, width), 1))
    parts = []
    for p in range(NB):
        parts.append(jnp.where(block_of == (ids[0] ^ rel_b(p)), g, 0.0).astype(BF))
    total = dot_t(jnp.concatenate(parts, 0), spread_matrix(128, width, rb))
    row = lax.broadcasted_iota(jnp.int32, (16, ff), 0)
    block_of = div_rb(lax.broadcasted_iota(jnp.int32, (16, ff), 1))
    block_of = jnp.where((row >= 8) & (row < 12), block_of - row + 8, -1)
    up = jnp.concatenate([gup[...], gup[...]], 0)
    parts = []
    for p in range(NB):
        parts.append(jnp.where(block_of == 4 * (ids[0] ^ rel_b(p)), up, 0.0).astype(BF))
    total = total + dot_t(jnp.concatenate(parts, 0), spread_matrix(128, ff, rb))
    heads = sl.shape[0] // 8
    per_head = jnp.sum(jnp.sum(sl[...].reshape(heads, 8, 128), 1), 1, keepdims=True)
    at = lax.broadcasted_iota(jnp.int32, (heads, 128), 0) == lax.broadcasted_iota(jnp.int32, (heads, 128), 1)
    line = -jnp.sum(jnp.where(at, per_head, 0.0), 0, keepdims=True)
    row = lax.broadcasted_iota(jnp.int32, (16 * NB, 128), 0)
    total = jnp.where((row & 15) == 12, line, total)
    bias[...] = jnp.zeros(bias.shape, BF)
    bias[:, 0:128] = total.astype(BF)

    def rows(r, size):
        return pl.ds(pl.multiple_of(r, 16), size)

    def store_sets(a_ref, b_ref):
        def go(src, dst):
            pltpu.make_async_copy(src, dst, sems.at[0]).start()

        for p in range(NB):
            s = ids[0] ^ rel_a(p)
            go(dwq.at[rows(s * rb, 48)], a_ref.at[p, pl.ds(0, 48)])
            go(dwk.at[rows(s * rb, 32)], a_ref.at[p, pl.ds(48, 32)])
            s = ids[0] ^ rel_b(p)
            go(dwk.at[rows(s * rb + 32, 16)], b_ref.at[p, pl.ds(0, 16)])
            go(dwv.at[rows(s * rb, 48)], b_ref.at[p, pl.ds(16, 48)])
            go(bias.at[pl.ds(16 * p, 16)], b_ref.at[p, pl.ds(64, 16)])

    @pl.when(ids[1] == 0)
    def _():
        store_sets(keep, send)

    @pl.when(ids[1] != 0)
    def _():
        store_sets(send, keep)

    wait_all(keep, sems.at[0])
    wait_all(send, sems.at[0])


def weight_grads(ids, pool, tok, dq, dk, dv, gvec, gup, sl, set_rows):
    width = tok.shape[1]
    full = lambda x: pl.BlockSpec(x.shape, lambda i, *_: (0, 0))
    big = jax.ShapeDtypeStruct((NB, set_rows, width), BF)
    square = pltpu.VMEM((width, width), BF)
    return pl.pallas_call(
        weights_kernel,
        name="weight_grads",
        grid_spec=pltpu.PrefetchScalarGridSpec(
            num_scalar_prefetch=1,
            grid=(1,),
            in_specs=[full(x) for x in (pool, tok, dq, dk, dv, gvec, gup, sl)],
            out_specs=[ANY, ANY],
            scratch_shapes=[
                square,
                square,
                square,
                pltpu.VMEM((16 * NB, width), BF),
                pltpu.SemaphoreType.DMA((1,)),
            ],
        ),
        out_shape=[big, big],
        compiler_params=params(),
    )(ids, pool, tok, dq, dk, dv, gvec, gup, sl)


def tokens_kernel(mixed, dq, dk, dv, wq, wk, wv, out, acc):
    half = mixed.shape[0]
    up = 0.5 * (mixed[...] + dot_t(dq[...], wq[...]))
    down = dot_t(dk[...], wk[...]) + dot_t(dv[...], wv[...])
    for j in range(mixed.shape[1] // 128):
        cols = slice(128 * j, 128 * j + 128)
        for i in range(2):
            acc[j, pl.ds(i, half, stride=2)] = up[:, cols]
        out[:, cols] = acc[j] + down[:, cols]


def token_grads(mixed, dq, dk, dv, wq, wk, wv):
    rows, width = dk.shape
    step = 512
    half = pl.BlockSpec((step // 2, width), lambda i: (i, 0))
    block = pl.BlockSpec((step, width), lambda i: (i, 0))
    whole = pl.BlockSpec((width, width), lambda i: (0, 0))
    return pl.pallas_call(
        tokens_kernel,
        name="token_grads",
        grid=(rows // step,),
        in_specs=[half, half, block, block, whole, whole, whole],
        out_specs=block,
        out_shape=jax.ShapeDtypeStruct((rows, width), FL),
        scratch_shapes=[pltpu.VMEM((width // 128, step, 128), FL)],
        compiler_params=params(),
    )(mixed, dq, dk, dv, wq, wk, wv)


def blocks_of(x):
    return x.reshape(NB, x.shape[0] // NB, x.shape[1])


def column_parts(x, width):
    return jnp.concatenate([x[..., width * c : width * c + width] for c in range(x.shape[-1] // width)], -2)


def bias_block(small, up, width):
    rb = small[0].shape[-1]
    rows = jnp.stack(list(small) + [up[..., rb * c : rb * c + rb] for c in range(4)], -2)
    pad = [(0, 0)] * (rows.ndim - 2) + [(0, 4), (0, width - rb)]
    return jnp.pad(rows, pad)


def pack(wq, wk, wv, wo, w1, w2, bias, width):
    a1 = jnp.concatenate([wq, wk[..., :32, :]], -2)
    b1 = jnp.concatenate([wk[..., 32:, :], wv, bias], -2)
    a2 = jnp.concatenate([w2, wo[..., :32, :]], -2)
    b2 = jnp.concatenate([column_parts(w1, width), wo[..., 32:, :], wo[..., 32:, :]], -2)
    return a1, b1, a2, b2


def unpack(a1, b1, a2, b2, width):
    wq = a1[..., :48, :]
    wk = jnp.concatenate([a1[..., 48:, :], b1[..., :16, :]], -2)
    wv = b1[..., 16:64, :]
    bias = b1[..., 64:, :]
    wo = jnp.concatenate([a2[..., 192:, :], b2[..., 192:208, :]], -2)
    w2 = a2[..., :192, :]
    parts = 4
    w1 = jnp.concatenate([b2[..., 48 * c : 48 * c + 48, :] for c in range(parts)], -1)
    return wq, wk, wv, wo, w1, w2, bias


def local(
    tokens,
    cotangent,
    lengths,
    w_query,
    b_query,
    w_key,
    w_value,
    b_value,
    w_output,
    b_output,
    gain_attn,
    shift_attn,
    w_up,
    b_up,
    w_down,
    b_down,
    gain_ffn,
    shift_ffn,
    distance_slope,
):
    rows_here, width = tokens.shape
    ff = w_up.shape[1]
    own = rows_here // 2
    halo = rows_here // 2
    seq = lax.axis_size("seq")
    devices = seq * lax.axis_size("dp")
    direct = seq == NB
    order = ("dp", "seq")
    up_pairs = [(i, i + 1) for i in range(devices - 1)]
    down_pairs = [(i + 1, i) for i in range(devices - 1)]

    masters = (w_query, w_key, w_value, w_output, w_up, w_down)
    vectors = (b_query, b_value, b_output, gain_attn, shift_attn, b_down, gain_ffn, shift_ffn)
    if direct:
        core = lax.axis_index("dp")
        ids = jnp.stack([lax.axis_index("seq"), core]).astype(jnp.int32)
        a1, b1, a2, b2 = pack(*masters, bias_block(vectors, b_up, width), width)
        first = jnp.where(core == 0, a1, b1).astype(BF)[None]
        second = jnp.where(core == 0, a2, b2).astype(BF)[None]
        sets1 = gather_set(first)
        sets2 = gather_set(second)
    else:
        ids = jnp.zeros((2,), jnp.int32)
        gather = lambda x: lax.all_gather(x.astype(BF), "seq", axis=0, tiled=True)
        full = [blocks_of(gather(x)) for x in masters]
        small = [gather(x).reshape(NB, -1) for x in vectors]
        bias = bias_block(small, gather(b_up).reshape(NB, -1), width)
        a1, b1, a2, b2 = pack(*full, bias, width)
        at_a = jnp.array([rel_a(p) for p in range(NB)])
        at_b = jnp.array([rel_b(p) for p in range(NB)])
        sets1 = (a1[at_a[:8]], a1[at_a[8:]], b1[at_b[:8]], b1[at_b[8:]])
        sets2 = (a2[at_a[:8]], a2[at_a[8:]], b2[at_b[:8]], b2[at_b[8:]])

    first_row = lax.axis_index(order) * rows_here
    total = devices * rows_here
    starts = 2 * (jnp.cumsum(lengths) - lengths)
    place = first_row - halo + 2 * jnp.arange(2 * own, dtype=jnp.int32)
    before = starts[None, :] <= place[:, None]
    begin = jnp.max(jnp.where(before, starts[None, :], 0), 1)
    end = jnp.min(jnp.where(before, total, starts[None, :]), 1)
    inside = (place >= 0) & (place < total)
    shift = first_row - halo
    begin = jnp.where(inside, begin - shift, 0)
    end = jnp.where(inside, end - shift, 0)
    bounds = jnp.stack([begin, end], 1).astype(FL)
    bounds = jnp.pad(bounds, ((0, 0), (0, 126)))
    blocks = 2 * own // QB
    chunks = (rows_here + 2 * halo) // KC
    low_chunk = jnp.min(jnp.where(inside, begin, 4 * total).reshape(blocks, QB), 1) // KC
    high_chunk = (jnp.max(end.reshape(blocks, QB), 1) + KC - 1) // KC
    index = jnp.arange(blocks)
    away = (index < blocks // 4) | (index >= blocks - blocks // 4)
    low_chunk = jnp.clip(low_chunk, jnp.where(away, chunks // 4, 0), chunks)
    high_chunk = jnp.clip(high_chunk, 0, jnp.where(away, chunks - chunks // 4, chunks))
    spans = jnp.concatenate([low_chunk, high_chunk]).astype(jnp.int32)

    low_tokens = lax.ppermute(tokens[rows_here - halo :], order, up_pairs)
    high_tokens = lax.ppermute(tokens[:halo], order, down_pairs)
    tok_ext = jnp.concatenate([low_tokens, tokens, high_tokens], 0)

    q, k, v, pool, wq, wk, wv, vec, upb = qkv(ids, tok_ext, sets1, ff)
    pool = pool[own // 2 : own // 2 + own]
    att, exact, lse = attend_forward(spans, distance_slope, q, k, v, bounds, own)
    out, pay, stats, mixed, gvec, gup, keep2, send2 = middle(
        ids, pool, att, exact, lse, cotangent, vec, upb, sets2, 224
    )
    low_pay = lax.ppermute(pay[own // 2 :], order, up_pairs)
    high_pay = lax.ppermute(pay[: own // 2], order, down_pairs)

    def stats_of(x):
        return add(*[x[:, width + 256 * j : width + 256 * j + 256] for j in range(3)])

    da = jnp.concatenate([low_pay[:, :width], pay[:, :width], high_pay[:, :width]], 0)
    stats_ext = jnp.concatenate([stats_of(low_pay), stats, stats_of(high_pay)], 0)
    dq, dk, dv, sl = attend_backward(spans, distance_slope, q, k, v, da, stats_ext, bounds)
    keep1, send1 = weight_grads(ids, pool, tokens, dq, dk, dv, gvec, gup, sl, 80)
    grad_tokens = token_grads(mixed, dq, dk, dv, wq, wk, wv)

    if direct:
        a2, b2 = reduce_set(keep2, send2)
        a1, b1 = reduce_set(keep1, send1)
        gq, gk, gv, go, g1, g2, gb = unpack(a1, b1, a2, b2, width)
        rb = width // NB
        small = [gb[i, :rb] for i in range(8)]
        g_up = jnp.concatenate([gb[8 + c, :rb] for c in range(4)], 0)
        g_slope = gb[12, : distance_slope.shape[0]]
    else:
        inv_a = [0] * NB
        inv_b = [0] * NB
        for p in range(NB):
            inv_a[rel_a(p)] = p
            inv_b[rel_b(p)] = p
        inv_a = jnp.array(inv_a)
        inv_b = jnp.array(inv_b)
        gq, gk, gv, go, g1, g2, gb = unpack(keep1[inv_a], send1[inv_b], keep2[inv_a], send2[inv_b], width)
        rb = width // NB

        def share(x):
            x = lax.psum(x.astype(FL), "dp")
            return lax.psum_scatter(x, "seq", scatter_dimension=0, tiled=True)

        gq, gk, gv, go, g1, g2 = [share(x.reshape(-1, x.shape[-1])) for x in (gq, gk, gv, go, g1, g2)]
        small = [share(gb[:, i, :rb].reshape(-1)) for i in range(8)]
        g_up = share(gb[:, 8:12, :rb].reshape(-1))
        g_slope = lax.psum(gb[0, 12, : distance_slope.shape[0]].astype(FL), order)
    return (
        out,
        grad_tokens,
        gq,
        small[0],
        gk,
        gv,
        small[1],
        go,
        small[2],
        small[3],
        small[4],
        g1,
        g_up,
        g2,
        small[5],
        small[6],
        small[7],
        g_slope,
    )


def solution(mesh):
    tall = P(("dp", "seq"), None)
    mat = P("seq", None)
    vec = P("seq")
    return jax.shard_map(
        local,
        mesh=mesh,
        in_specs=(tall, tall, P(), mat, vec, mat, mat, vec, mat, vec, vec, vec, mat, vec, mat, vec, vec, vec, P()),
        out_specs=(tall, tall, mat, vec, mat, mat, vec, mat, vec, vec, vec, mat, vec, mat, vec, vec, vec, P()),
        check_vma=False,
    )
```

time: 1820 us -> 448 us (0.25)
  waiting for transfers between devices: 1090 us -> 198 us
  matrix products: 282 us -> 0 us
  other arithmetic: 196 us -> 22.5 us
  blocking collectives: 160 us -> 0 us
  Pallas kernels: 0 us -> 125 us
  starting transfers between devices: 13.4 us -> 79 us
  local copies, waits for them, and re-layouts: 51.3 us -> 18.3 us
    reduce_scatter x4 -> x0, waiting for transfers between devices: 487 us -> none  [the longest x1 177 us: local(): lax.psum_scatter(sum_w2, 'seq', scatter_dimension=0, tiled=True)]
    dot_general x36 -> x0, matrix products: 282 us -> none  [the longest x3 50.5 us: local(): jnp.einsum('qhd,khd->hqk', att_group, v_group, preferred_element_type=fl_...]
    unnamed x15 -> x0, waiting for transfers between devices: 265 us -> none
    unnamed x2 -> x0, blocking collectives: 156 us -> none
    all_gather x6 -> x0, waiting for transfers between devices: 140 us -> none  [the longest x1 83.7 us: local(): lax.all_gather(low_wq, 'seq', axis=0, tiled=True)]
    pallas_call x0 -> x6, Pallas kernels: none -> 125 us  [the longest x1 36.6 us: middle(): pl.pallas_call(middle_kernel, name='middle', grid_spec=pltpu.PrefetchScal...]
    reduce_sum x16 -> x0, other arithmetic: 114 us -> none  [the longest x1 63.9 us: local(): jnp.sum(d_scores.astype(fl_type) * distance[None], (1, 2))]
    ppermute x4 -> x28, starting transfers between devices: 12.6 us -> 79 us  [the longest x16 48.2 us: exchange(): return lax.ppermute(x, ('dp', 'seq'), pairs)]
  transfers between devices with their start and end apart: 17 -> 28, of which waited for: 13 -> 16; matrix products, arithmetic and copies ran while one was open for 15% -> 6% of each run, Pallas kernels for 0% -> 20%
where the time goes in v1:
time: 448 us; the launch traced here: 444 us
  waiting for transfers between devices  198 us (44%)
  Pallas kernels  125 us (28%)
  starting transfers between devices  79 us (18%)
  other arithmetic  22.5 us (5%)
  local copies, waits for them, and re-layouts  18.3 us (4%)
    ppermute x16, waiting for transfers between devices, exchange(): return lax.ppermute(x, ('dp', 'seq'), pairs)  134 us
    ppermute x16, starting transfers between devices, exchange(): return lax.ppermute(x, ('dp', 'seq'), pairs)  48.2 us
    pallas_call x1, Pallas kernels, middle(): pl.pallas_call(middle_kernel, name='middle', grid_spec=pltpu.PrefetchScal...  36.6 us
    pallas_call x1, Pallas kernels, attend_backward(): pl.pallas_call(backward_kernel, name='attend_backward', grid_spec=pltpu.P...  35.8 us
    ppermute x1, waiting for transfers between devices, local(): low_pay = lax.ppermute(pay[own // 2:], order, up_pairs)  31.1 us
    ppermute x1, waiting for transfers between devices, local(): low_tokens = lax.ppermute(tokens[rows_here - halo:], order, up_pairs)  28.2 us
    pallas_call x1, Pallas kernels, attend_forward(): pl.pallas_call(forward_kernel, name='attend_forward', grid_spec=pltpu.Pre...  22.6 us
    ppermute x8, starting transfers between devices, swap_core(): return lax.ppermute(x, 'dp', [(0, 1), (1, 0)])  18.3 us
  transfers between devices with their start and end apart: 28, of which 16 were waited for; matrix products, arithmetic and copies ran while one was open for 6% of the time, Pallas kernels for 20%

profile of v1, /device:TPU:0, one launch (start us, length us, event | category | flops | bytes accessed | tf_op | source)
XLA Modules:
  0.0 444.3 jit_solution(2697722529638983075)
XLA Ops:
  8.0 4.1 collective-permute-start.8
  12.1 15.4 %collective-permute-done.8 = bf16[1,224,768]{2,1,0:T(8,128)(2,1)S(1)} collective-permute-done((bf16[1,224,768]{2,1,0:T(8,128)(2,1)S(1)}, bf16[1,224,768]{2,1,0:T(8,128)(2,1)S(1)}, u32[]{:S(2)}, u32[]{:S(2)}) %collective-permute-start.8) | collective-permute-done | bytes 344096 | tf_op jit(solution)/shard_map/ppermute | solution.py:41
  28.4 15.9 %collective-permute-done.9 = bf16[2,224,768]{2,1,0:T(8,128)(2,1)S(1)} collective-permute-done((bf16[2,224,768]{2,1,0:T(8,128)(2,1)S(1)}, bf16[2,224,768]{2,1,0:T(8,128)(2,1)S(1)}, u32[]{:S(2)}, u32[]{:S(2)}) %collective-permute-start.9) | collective-permute-done | bytes 688160 | tf_op jit(solution)/shard_map/ppermute | solution.py:41
  44.6 1.3 collective-permute-start.10
  45.9 17.0 %collective-permute-done.10 = bf16[4,224,768]{2,1,0:T(8,128)(2,1)S(1)} collective-permute-done((bf16[4,224,768]{2,1,0:T(8,128)(2,1)S(1)}, bf16[4,224,768]{2,1,0:T(8,128)(2,1)S(1)}, u32[]{:S(2)}, u32[]{:S(2)}) %collective-permute-start.10) | collective-permute-done | bytes 1376288 | tf_op jit(solution)/shard_map/ppermute | solution.py:41
  63.0 1.6 pad_maximum_fusion.1.low
  64.6 1.2 collective-permute-start.11
  66.1 3.4 collective-permute-start.2
  69.5 4.5 %collective-permute-done.2 = bf16[1,80,768]{2,1,0:T(8,128)(2,1)S(1)} collective-permute-done((bf16[1,80,768]{2,1,0:T(8,128)(2,1)S(1)}, bf16[1,80,768]{2,1,0:T(8,128)(2,1)S(1)}, u32[]{:S(2)}, u32[]{:S(2)}) %collective-permute-start.2) | collective-permute-done | bytes 122912 | tf_op jit(solution)/shard_map/ppermute | solution.py:41
  74.8 5.5 %collective-permute-done.3 = bf16[2,80,768]{2,1,0:T(8,128)(2,1)S(1)} collective-permute-done((bf16[2,80,768]{2,1,0:T(8,128)(2,1)S(1)}, bf16[2,80,768]{2,1,0:T(8,128)(2,1)S(1)}, u32[]{:S(2)}, u32[]{:S(2)}) %collective-permute-start.3) | collective-permute-done | bytes 245792 | tf_op jit(solution)/shard_map/ppermute | solution.py:41
  80.4 1.4 collective-permute-start.4
  81.8 21.5 %collective-permute-done.11.high = bf16[8,224,768]{2,1,0:T(8,128)(2,1)} collective-permute-done((bf16[8,224,768]{2,1,0:T(8,128)(2,1)}, bf16[8,224,768]{2,1,0:T(8,128)(2,1)}, u32[]{:S(2)}, u32[]{:S(2)}) %collective-permute-start.11) | collective-permute-done | bytes 2752544 | tf_op jit(solution)/shard_map/ppermute | solution.py:41
  104.5 4.1 collective-permute-start
  108.6 1.3 collective-permute-start.1
  110.5 2.7 collective-permute-start.5
  114.1 28.2 %collective-permute-done = bf16[512,768]{1,0:T(8,128)(2,1)} collective-permute-done((bf16[512,768]{1,0:T(8,128)(2,1)}, bf16[512,768]{1,0:T(8,128)(2,1)}, u32[]{:S(2)}, u32[]{:S(2)}) %collective-permute-start) | collective-permute-done | bytes 786464 | tf_op jit(solution)/shard_map/ppermute | solution.py:952
  142.3 12.5 %collective-permute-done.5.high = bf16[8,80,768]{2,1,0:T(8,128)(2,1)} collective-permute-done((bf16[8,80,768]{2,1,0:T(8,128)(2,1)S(1)}, bf16[8,80,768]{2,1,0:T(8,128)(2,1)}, u32[]{:S(2)}, u32[]{:S(2)}) %collective-permute-start.5) | collective-permute-done | bytes 983072 | tf_op jit(solution)/shard_map/ppermute | solution.py:41
  157.1 3.0 pad_maximum_fusion.tok
  160.1 12.9 %qkv.1 = (bf16[1024,768]{1,0:T(8,128)(2,1)}, bf16[2048,768]{1,0:T(8,128)(2,1)}, bf16[2048,768]{1,0:T(8,128)(2,1)}, f32[1024,768]{1,0:T(8,128)}, bf16[768,768]{1,...) custom-call(s32[2]{0:T(128)} %pad_add_fusion.ids, ...), custom_call_target="tpu_custom_call" | custom-call | tf_op jit(solution)/shard_map/qkv/pallas_call | solution.py:175
  172.9 2.6 slice.276.pool
  175.6 22.6 %attend_forward.1 = (bf16[512,768]{1,0:T(8,128)(2,1)}, f32[512,768]{1,0:T(8,128)}, f32[512,256]{1,0:T(8,128)}) custom-call(s32[16]{0:T(128)} %pad_add_fusion.1.spans, f32[12]{0:T(128)} %slopes.3, bf16[1024,768]{1,0:T(8,128)(2,1)} %get-tuple-element.45.q, bf16[2048,768]{1,0:T(8,128)(2,1)} %get-tuple-element.46.k, bf16[2048,768]{1,0:T(8,128)(2,1)} %get-tuple-element.47.v, ...), custom_call_target="tpu_custom_call" | custom-call | tf_op jit(solution)/shard_map/attend_forward/pallas_call | solution.py:316
  198.1 36.6 %middle.1 = (bf16[512,768]{1,0:T(8,128)(2,1)}, bf16[512,1536]{1,0:T(8,128)(2,1)}, f32[512,256]{1,0:T(8,128)}, f32[512,768]{1,0:T(8,128)}, f32[8,768]{1,0:T(8,128...) custom-call(s32[2]{0:T(128)} %pad_add_fusion.ids, f32[512,768]{1,0:T(8,128)} %slice.276.pool, ...), custom_call_target="tpu_custom_call" | custom-call | tf_op jit(solution)/shard_map/middle/pallas_call | solution.py:692
  234.7 6.6 %collective-permute-start.22 = (bf16[16,224,768]{2,1,0:T(8,128)(2,1)}, bf16[16,224,768]{2,1,0:T(8,128)(2,1)S(1)}, u32[]{:S(2)}, u32[]{:S(2)}) collective-permute-start(bf16[16,224,768]{2,1,0:T(8,128)(2,1)} %get-tuple-element.69), channel_id=1, source_target_pairs={{0,16},{16,0},{1,17},{17,1},{2,18},{18,2},{3,19},{19,3},{4,20},{20... | collective-permute-start | bytes 16515080 | tf_op jit(solution)/shard_map/ppermute | solution.py:45
  241.3 1.6 fusion.18
  243.0 5.7 %collective-permute-start.14 = (bf16[256,1536]{1,0:T(8,128)(2,1)S(1)}, bf16[256,1536]{1,0:T(8,128)(2,1)S(1)}, u32[]{:S(2)}, u32[]{:S(2)}) collective-permute-start(bf16[256,1536]{1,0:T(8,128)(2,1)S(1)} %get-tuple-element.82), channel_id=1, source_target_pairs={{0,1},{1,2},{2,3},{3,4},{4,5},{5,6},{6,7},{7,8},{8,9},{9,10},{10,1... | collective-permute-start | bytes 2359304 | tf_op jit(solution)/shard_map/ppermute | solution.py:962
  248.6 1.5 collective-permute-start.15
  251.3 31.1 %collective-permute-done.14 = bf16[256,1536]{1,0:T(8,128)(2,1)S(1)} collective-permute-done((bf16[256,1536]{1,0:T(8,128)(2,1)S(1)}, bf16[256,1536]{1,0:T(8,128)(2,1)S(1)}, u32[]{:S(2)}, u32[]{:S(2)}) %collective-permute-start.14) | collective-permute-done | bytes 786464 | tf_op jit(solution)/shard_map/ppermute | solution.py:962
  283.3 2.7 add_convert_fusion
  286.5 2.7 collective-permute-start.23
  290.3 1.3 pad_maximum_fusion.2.da
  291.6 35.8 %attend_backward.1 = (bf16[512,768]{1,0:T(8,128)(2,1)}, bf16[1024,768]{1,0:T(8,128)(2,1)}, bf16[1024,768]{1,0:T(8,128)(2,1)}, f32[96,128]{1,0:T(8,128)}) custom-call(s32[16]{0:T(128)} %pad_add_fusion.1.spans, f32[12]{0:T(128)} %slopes.3, bf16[1024,768]{1,0:T(8,128)(2,1)} %get-tuple-element.45.q, bf16[2048,768]{1,0:T(8,128)(2,1)} %get-tuple-element.46.k, ...), custom_call_target="tpu_custom_call" | custom-call | tf_op jit(solution)/shard_map/attend_backward/pallas_call | solution.py:423
  327.4 9.6 %weight_grads.1 = (bf16[16,80,768]{2,1,0:T(8,128)(2,1)}, bf16[16,80,768]{2,1,0:T(8,128)(2,1)}) custom-call(s32[2]{0:T(128)} %pad_add_fusion.ids, f32[512,768]{1,0:T(8,128)} %slice.276.pool, bf16[1024,768]{1,0:T(8,128)(2,1)} %tok.1, bf16[512,768]{1,0:T(8,128)(2,1)} %get-tuple-element.57.dq, bf16[1024,768]{1,0:T(8,128)(2,1)} %get-tuple-element.58.dk, ...), custom_call_target="tpu_custom_call" | custom-call | tf_op jit(solution)/shard_map/weight_grads/pallas_call | solution.py:790
  337.0 11.5 %collective-permute-start.16 = (bf16[16,80,768]{2,1,0:T(8,128)(2,1)}, bf16[16,80,768]{2,1,0:T(8,128)(2,1)S(1)}, u32[]{:S(2)}, u32[]{:S(2)}) collective-permute-start(bf16[16,80,768]{2,1,0:T(8,128)(2,1)} %get-tuple-element.67), channel_id=1, source_target_pairs={{0,16},{16,0},{1,17},{17,1},{2,18},{18,2},{3,19},{19,3},{4,20},{20... | collective-permute-start | bytes 5898248 | tf_op jit(solution)/shard_map/ppermute | solution.py:45
  348.5 3.8 collective-permute-done.16
  352.3 1.4 add_convert_fusion.2
  353.7 7.1 %collective-permute-start.17 = (bf16[8,80,768]{2,1,0:T(8,128)(2,1)S(1)}, bf16[8,80,768]{2,1,0:T(8,128)(2,1)S(1)}, u32[]{:S(2)}, u32[]{:S(2)}) collective-permute-start(bf16[8,80,768]{2,1,0:T(8,128)(2,1)S(1)} %add_convert_fusion.2), channel_id=1, source_target_pairs={{0,1},{1,0},{2,3},{3,2},{4,5},{5,4},{6,7},{7,6},{8,9},{9,8},{10,11... | collective-permute-start | bytes 2949128 | tf_op jit(solution)/shard_map/ppermute | solution.py:41
  360.8 3.5 add_convert_fusion.1
  364.4 1.8 collective-permute-start.24
  366.2 12.4 %collective-permute-done.17 = bf16[8,80,768]{2,1,0:T(8,128)(2,1)S(1)} collective-permute-done((bf16[8,80,768]{2,1,0:T(8,128)(2,1)S(1)}, bf16[8,80,768]{2,1,0:T(8,128)(2,1)S(1)}, u32[]{:S(2)}, u32[]{:S(2)}) %collective-permute-start.17) | collective-permute-done | bytes 983072 | tf_op jit(solution)/shard_map/ppermute | solution.py:41
  378.9 3.1 collective-permute-start.18
  382.1 4.7 %collective-permute-done.24 = bf16[4,224,768]{2,1,0:T(8,128)(2,1)S(1)} collective-permute-done((bf16[4,224,768]{2,1,0:T(8,128)(2,1)S(1)}, bf16[4,224,768]{2,1,0:T(8,128)(2,1)S(1)}, u32[]{:S(2)}, u32[]{:S(2)}) %collective-permute-start.24) | collective-permute-done | bytes 1376288 | tf_op jit(solution)/shard_map/ppermute | solution.py:41
  387.0 5.7 %collective-permute-start.25 = (bf16[2,224,768]{2,1,0:T(8,128)(2,1)S(1)}, bf16[2,224,768]{2,1,0:T(8,128)(2,1)S(1)}, u32[]{:S(2)}, u32[]{:S(2)}) collective-permute-start(bf16[2,224,768]{2,1,0:T(8,128)(2,1)S(1)} %get-tuple-element.80), channel_id=1, source_target_pairs={{0,4},{1,5},{2,6},{3,7},{4,0},{5,1},{6,2},{7,3},{8,12},{9,13},{10,... | collective-permute-start | bytes 2064392 | tf_op jit(solution)/shard_map/ppermute | solution.py:41
  392.8 5.7 %collective-permute-start.19 = (bf16[2,80,768]{2,1,0:T(8,128)(2,1)S(1)}, bf16[2,80,768]{2,1,0:T(8,128)(2,1)S(1)}, u32[]{:S(2)}, u32[]{:S(2)}) collective-permute-start(bf16[2,80,768]{2,1,0:T(8,128)(2,1)S(1)} %get-tuple-element.86), channel_id=1, source_target_pairs={{0,4},{1,5},{2,6},{3,7},{4,0},{5,1},{6,2},{7,3},{8,12},{9,13},{10,... | collective-permute-start | bytes 737288 | tf_op jit(solution)/shard_map/ppermute | solution.py:41
  398.6 11.9 %collective-permute-done.19 = bf16[2,80,768]{2,1,0:T(8,128)(2,1)S(1)} collective-permute-done((bf16[2,80,768]{2,1,0:T(8,128)(2,1)S(1)}, bf16[2,80,768]{2,1,0:T(8,128)(2,1)S(1)}, u32[]{:S(2)}, u32[]{:S(2)}) %collective-permute-start.19) | collective-permute-done | bytes 245792 | tf_op jit(solution)/shard_map/ppermute | solution.py:41
  410.6 6.2 %collective-permute-start.20 = (bf16[1,80,768]{2,1,0:T(8,128)(2,1)S(1)}, bf16[1,80,768]{2,1,0:T(8,128)(2,1)S(1)}, u32[]{:S(2)}, u32[]{:S(2)}) collective-permute-start(bf16[1,80,768]{2,1,0:T(8,128)(2,1)S(1)} %fusion.8), channel_id=1, source_target_pairs={{0,8},{1,9},{2,10},{3,11},{4,12},{5,13},{6,14},{7,15},{8,0},{9,1},... | collective-permute-start | bytes 368648 | tf_op jit(solution)/shard_map/ppermute | solution.py:41
  416.9 7.6 %token_grads.1 = f32[1024,768]{1,0:T(8,128)} custom-call(f32[512,768]{1,0:T(8,128)} %get-tuple-element.54.mixed, bf16[512,768]{1,0:T(8,128)(2,1)} %get-tuple-element.57.dq, bf16[1024,768]{1,0:T(8,128)(2,1)} %get-tuple-element.58.dk, bf16[1024,768]{1,0:T(8,128)(2,1)} %get-tuple-element.59.dv, bf16[768,768]{1,0:T(8,128)(2,1)} %get-tuple-element.60.wq, ...), custom_call_target="tpu_custom_call" | custom-call | tf_op jit(solution)/shard_map/token_grads/pallas_call | solution.py:828
  424.6 6.3 %collective-permute-done.20 = bf16[1,80,768]{2,1,0:T(8,128)(2,1)S(1)} collective-permute-done((bf16[1,80,768]{2,1,0:T(8,128)(2,1)S(1)}, bf16[1,80,768]{2,1,0:T(8,128)(2,1)S(1)}, u32[]{:S(2)}, u32[]{:S(2)}) %collective-permute-start.20) | collective-permute-done | bytes 122912 | tf_op jit(solution)/shard_map/ppermute | solution.py:41
  431.0 6.7 %collective-permute-done.26 = bf16[1,224,768]{2,1,0:T(8,128)(2,1)S(1)} collective-permute-done((bf16[1,224,768]{2,1,0:T(8,128)(2,1)S(1)}, bf16[1,224,768]{2,1,0:T(8,128)(2,1)S(1)}, u32[]{:S(2)}, u32[]{:S(2)}) %collective-permute-start.26) | collective-permute-done | bytes 344096 | tf_op jit(solution)/shard_map/ppermute | solution.py:41
  (128 shorter events, 25.5 us)
Async XLA Ops:
  8.0 19.5 %collective-permute-start.8 = (bf16[1,224,768]{2,1,0:T(8,128)(2,1)S(1)}, bf16[1,224,768]{2,1,0:T(8,128)(2,1)S(1)}, u32[]{:S(2)}, u32[]{:S(2)}) collective-permute-start(bf16[1,224,768]{2,1,0:T(8,128)(2,1)S(1)} %fusion.6), channel_id=1, source_target_pairs={{0,8},{1,9},{2,10},{3,11},{4,12},{5,13},{6,14},{7,15},{8,0},{9,1},... | collective-permute-start | bytes 1032200 | tf_op jit(solution)/shard_map/ppermute | solution.py:41
  27.6 16.7 %collective-permute-start.9 = (bf16[2,224,768]{2,1,0:T(8,128)(2,1)S(1)}, bf16[2,224,768]{2,1,0:T(8,128)(2,1)S(1)}, u32[]{:S(2)}, u32[]{:S(2)}) collective-permute-start(bf16[2,224,768]{2,1,0:T(8,128)(2,1)S(1)} %pad_maximum_fusion.6), channel_id=1, source_target_pairs={{0,4},{1,5},{2,6},{3,7},{4,0},{5,1},{6,2},{7,3},{8,12},{9,13},{10,... | collective-permute-start | bytes 2064392 | tf_op jit(solution)/shard_map/ppermute | solution.py:41
  44.4 21.4 %copy-start.11 = (f32[192]{0:T(256)S(1)}, f32[192]{0:T(256)}, u32[]{:S(2)}) copy-start(f32[192]{0:T(256)} %param.32) | copy-start | bytes 2308
  44.4 21.5 %copy-start.12 = (f32[48]{0:T(128)S(1)}, f32[48]{0:T(128)}, u32[]{:S(2)}) copy-start(f32[48]{0:T(128)} %param.23) | copy-start | bytes 580
  44.5 21.5 %copy-start.13 = (f32[48]{0:T(128)S(1)}, f32[48]{0:T(128)}, u32[]{:S(2)}) copy-start(f32[48]{0:T(128)} %param.26) | copy-start | bytes 580
  44.5 21.5 %copy-start.14 = (f32[48]{0:T(128)S(1)}, f32[48]{0:T(128)}, u32[]{:S(2)}) copy-start(f32[48]{0:T(128)} %param.28) | copy-start | bytes 580
  44.5 21.5 %copy-start.15 = (f32[48]{0:T(128)S(1)}, f32[48]{0:T(128)}, u32[]{:S(2)}) copy-start(f32[48]{0:T(128)} %param.29) | copy-start | bytes 580
  44.5 21.5 %copy-start.16 = (f32[48]{0:T(128)S(1)}, f32[48]{0:T(128)}, u32[]{:S(2)}) copy-start(f32[48]{0:T(128)} %param.30) | copy-start | bytes 580
  44.5 21.5 %copy-start.17 = (f32[48]{0:T(128)S(1)}, f32[48]{0:T(128)}, u32[]{:S(2)}) copy-start(f32[48]{0:T(128)} %param.34) | copy-start | bytes 580
  44.5 21.5 %copy-start.18 = (f32[48]{0:T(128)S(1)}, f32[48]{0:T(128)}, u32[]{:S(2)}) copy-start(f32[48]{0:T(128)} %param.35) | copy-start | bytes 580
  44.5 21.5 %copy-start.19 = (f32[48]{0:T(128)S(1)}, f32[48]{0:T(128)}, u32[]{:S(2)}) copy-start(f32[48]{0:T(128)} %param.36) | copy-start | bytes 580
  44.5 21.5 %copy-start.9 = (f32[48,768]{1,0:T(8,128)S(1)}, f32[48,768]{1,0:T(8,128)}, u32[]{:S(2)}) copy-start(f32[48,768]{1,0:T(8,128)} %param.24) | copy-start | bytes 442372
  44.6 21.5 %copy-start.7 = (f32[48,768]{1,0:T(8,128)S(1)}, f32[48,768]{1,0:T(8,128)}, u32[]{:S(2)}) copy-start(f32[48,768]{1,0:T(8,128)} %param.22) | copy-start | bytes 442372
  44.6 21.5 %copy-start.8 = (f32[48,768]{1,0:T(8,128)S(1)}, f32[48,768]{1,0:T(8,128)}, u32[]{:S(2)}) copy-start(f32[48,768]{1,0:T(8,128)} %param.25) | copy-start | bytes 442372
  44.6 58.7 %copy-start = (bf16[1024,768]{1,0:T(8,128)(2,1)S(1)}, bf16[1024,768]{1,0:T(8,128)(2,1)}, u32[]{:S(2)}) copy-start(bf16[1024,768]{1,0:T(8,128)(2,1)} %tok.1) | copy-start | bytes 4718596
  44.6 18.4 %collective-permute-start.10 = (bf16[4,224,768]{2,1,0:T(8,128)(2,1)S(1)}, bf16[4,224,768]{2,1,0:T(8,128)(2,1)S(1)}, u32[]{:S(2)}, u32[]{:S(2)}) collective-permute-start(bf16[4,224,768]{2,1,0:T(8,128)(2,1)S(1)} %pad_maximum_fusion.3), channel_id=1, source_target_pairs={{0,2},{1,3},{2,0},{3,1},{4,6},{5,7},{6,4},{7,5},{8,10},{9,11},{10,... | collective-permute-start | bytes 4128776 | tf_op jit(solution)/shard_map/ppermute | solution.py:41
  64.6 45.2 %copy-start.10 = (s32[256]{0:T(256)S(1)}, s32[256]{0:T(256)}, u32[]{:S(2)}) copy-start(s32[256]{0:T(256)} %param.21) | copy-start | bytes 3076
  64.6 38.6 %collective-permute-start.11 = (bf16[8,224,768]{2,1,0:T(8,128)(2,1)}, bf16[8,224,768]{2,1,0:T(8,128)(2,1)}, u32[]{:S(2)}, u32[]{:S(2)}) collective-permute-start(bf16[8,224,768]{2,1,0:T(8,128)(2,1)} %pad_maximum_fusion.1.low), channel_id=1, source_target_pairs={{0,1},{1,0},{2,3},{3,2},{4,5},{5,4},{6,7},{7,6},{8,9},{9,8},{10,11... | collective-permute-start | bytes 8257544 | tf_op jit(solution)/shard_map/ppermute | solution.py:41
  66.1 7.9 %collective-permute-start.2 = (bf16[1,80,768]{2,1,0:T(8,128)(2,1)S(1)}, bf16[1,80,768]{2,1,0:T(8,128)(2,1)S(1)}, u32[]{:S(2)}, u32[]{:S(2)}) collective-permute-start(bf16[1,80,768]{2,1,0:T(8,128)(2,1)S(1)} %fusion.11), channel_id=1, source_target_pairs={{0,8},{1,9},{2,10},{3,11},{4,12},{5,13},{6,14},{7,15},{8,0},{9,1},... | collective-permute-start | bytes 368648 | tf_op jit(solution)/shard_map/ppermute | solution.py:41
  74.1 6.3 %collective-permute-start.3 = (bf16[2,80,768]{2,1,0:T(8,128)(2,1)S(1)}, bf16[2,80,768]{2,1,0:T(8,128)(2,1)S(1)}, u32[]{:S(2)}, u32[]{:S(2)}) collective-permute-start(bf16[2,80,768]{2,1,0:T(8,128)(2,1)S(1)} %pad_maximum_fusion.9), channel_id=1, source_target_pairs={{0,4},{1,5},{2,6},{3,7},{4,0},{5,1},{6,2},{7,3},{8,12},{9,13},{10,... | collective-permute-start | bytes 737288 | tf_op jit(solution)/shard_map/ppermute | solution.py:41
  80.4 30.0 %collective-permute-start.4 = (bf16[4,80,768]{2,1,0:T(8,128)(2,1)S(1)}, bf16[4,80,768]{2,1,0:T(8,128)(2,1)S(1)}, u32[]{:S(2)}, u32[]{:S(2)}) collective-permute-start(bf16[4,80,768]{2,1,0:T(8,128)(2,1)S(1)} %pad_maximum_fusion.8), channel_id=1, source_target_pairs={{0,2},{1,3},{2,0},{3,1},{4,6},{5,7},{6,4},{7,5},{8,10},{9,11},{10,... | collective-permute-start | bytes 1474568 | tf_op jit(solution)/shard_map/ppermute | solution.py:41
  81.8 116.4 %collective-permute-start.12 = (bf16[8,224,768]{2,1,0:T(8,128)(2,1)}, bf16[8,224,768]{2,1,0:T(8,128)(2,1)}, u32[]{:S(2)}, u32[]{:S(2)}) collective-permute-start(bf16[8,224,768]{2,1,0:T(8,128)(2,1)} %pad_maximum_fusion.1.low), channel_id=1, source_target_pairs={{0,16},{16,0},{1,17},{17,1},{2,18},{18,2},{3,19},{19,3},{4,20},{20... | collective-permute-start | bytes 8257544 | tf_op jit(solution)/shard_map/ppermute | solution.py:45
  103.2 94.9 %collective-permute-start.13 = (bf16[8,224,768]{2,1,0:T(8,128)(2,1)}, bf16[8,224,768]{2,1,0:T(8,128)(2,1)}, u32[]{:S(2)}, u32[]{:S(2)}) collective-permute-start(bf16[8,224,768]{2,1,0:T(8,128)(2,1)} %collective-permute-done.11.high), channel_id=1, source_target_pairs={{0,16},{16,0},{1,17},{17,1},{2,18},{18,2},{3,19},{19,3},{4,20},{20... | collective-permute-start | bytes 8257544 | tf_op jit(solution)/shard_map/ppermute | solution.py:45
  104.5 37.8 %collective-permute-start = (bf16[512,768]{1,0:T(8,128)(2,1)}, bf16[512,768]{1,0:T(8,128)(2,1)}, u32[]{:S(2)}, u32[]{:S(2)}) collective-permute-start(bf16[512,768]{1,0:T(8,128)(2,1)} %get-tuple-element.84), channel_id=1, source_target_pairs={{0,1},{1,2},{2,3},{3,4},{4,5},{5,6},{6,7},{7,8},{8,9},{9,10},{10,1... | collective-permute-start | bytes 2359304 | tf_op jit(solution)/shard_map/ppermute | solution.py:952
  108.6 48.5 %collective-permute-start.1 = (bf16[512,768]{1,0:T(8,128)(2,1)}, bf16[512,768]{1,0:T(8,128)(2,1)}, u32[]{:S(2)}, u32[]{:S(2)}) collective-permute-start(bf16[512,768]{1,0:T(8,128)(2,1)} %get-tuple-element.85), channel_id=1, source_target_pairs={{1,0},{2,1},{3,2},{4,3},{5,4},{6,5},{7,6},{8,7},{9,8},{10,9},{11,1... | collective-permute-start | bytes 2359304 | tf_op jit(solution)/shard_map/ppermute | solution.py:953
  110.5 49.5 %copy-start.3 = (bf16[8,80,768]{2,1,0:T(8,128)(2,1)}, bf16[8,80,768]{2,1,0:T(8,128)(2,1)S(1)}, u32[]{:S(2)}) copy-start(bf16[8,80,768]{2,1,0:T(8,128)(2,1)S(1)} %pad_maximum_fusion.5.low) | copy-start | bytes 2949124
  110.5 44.3 %collective-permute-start.5 = (bf16[8,80,768]{2,1,0:T(8,128)(2,1)S(1)}, bf16[8,80,768]{2,1,0:T(8,128)(2,1)}, u32[]{:S(2)}, u32[]{:S(2)}) collective-permute-start(bf16[8,80,768]{2,1,0:T(8,128)(2,1)S(1)} %pad_maximum_fusion.5.low), channel_id=1, source_target_pairs={{0,1},{1,0},{2,3},{3,2},{4,5},{5,4},{6,7},{7,6},{8,9},{9,8},{10,11... | collective-permute-start | bytes 2949128 | tf_op jit(solution)/shard_map/ppermute | solution.py:41
  142.3 17.8 %collective-permute-start.6 = (bf16[8,80,768]{2,1,0:T(8,128)(2,1)S(1)}, bf16[8,80,768]{2,1,0:T(8,128)(2,1)}, u32[]{:S(2)}, u32[]{:S(2)}) collective-permute-start(bf16[8,80,768]{2,1,0:T(8,128)(2,1)S(1)} %pad_maximum_fusion.5.low), channel_id=1, source_target_pairs={{0,16},{16,0},{1,17},{17,1},{2,18},{18,2},{3,19},{19,3},{4,20},{20... | collective-permute-start | bytes 2949128 | tf_op jit(solution)/shard_map/ppermute | solution.py:45
  154.8 5.3 %collective-permute-start.7 = (bf16[8,80,768]{2,1,0:T(8,128)(2,1)}, bf16[8,80,768]{2,1,0:T(8,128)(2,1)}, u32[]{:S(2)}, u32[]{:S(2)}) collective-permute-start(bf16[8,80,768]{2,1,0:T(8,128)(2,1)} %collective-permute-done.5.high), channel_id=1, source_target_pairs={{0,16},{16,0},{1,17},{17,1},{2,18},{18,2},{3,19},{19,3},{4,20},{20... | collective-permute-start | bytes 2949128 | tf_op jit(solution)/shard_map/ppermute | solution.py:45
  234.7 48.5 %collective-permute-start.22 = (bf16[16,224,768]{2,1,0:T(8,128)(2,1)}, bf16[16,224,768]{2,1,0:T(8,128)(2,1)S(1)}, u32[]{:S(2)}, u32[]{:S(2)}) collective-permute-start(bf16[16,224,768]{2,1,0:T(8,128)(2,1)} %get-tuple-element.69), channel_id=1, source_target_pairs={{0,16},{16,0},{1,17},{17,1},{2,18},{18,2},{3,19},{19,3},{4,20},{20... | collective-permute-start | bytes 16515080 | tf_op jit(solution)/shard_map/ppermute | solution.py:45
  241.3 41.9 %copy-start.1 = (bf16[16,224,768]{2,1,0:T(8,128)(2,1)S(1)}, bf16[16,224,768]{2,1,0:T(8,128)(2,1)}, u32[]{:S(2)}) copy-start(bf16[16,224,768]{2,1,0:T(8,128)(2,1)} %get-tuple-element.68) | copy-start | bytes 16515076
  243.0 39.4 %collective-permute-start.14 = (bf16[256,1536]{1,0:T(8,128)(2,1)S(1)}, bf16[256,1536]{1,0:T(8,128)(2,1)S(1)}, u32[]{:S(2)}, u32[]{:S(2)}) collective-permute-start(bf16[256,1536]{1,0:T(8,128)(2,1)S(1)} %get-tuple-element.82), channel_id=1, source_target_pairs={{0,1},{1,2},{2,3},{3,4},{4,5},{5,6},{6,7},{7,8},{8,9},{9,10},{10,1... | collective-permute-start | bytes 2359304 | tf_op jit(solution)/shard_map/ppermute | solution.py:962
  248.6 34.5 %collective-permute-start.15 = (bf16[256,1536]{1,0:T(8,128)(2,1)S(1)}, bf16[256,1536]{1,0:T(8,128)(2,1)S(1)}, u32[]{:S(2)}, u32[]{:S(2)}) collective-permute-start(bf16[256,1536]{1,0:T(8,128)(2,1)S(1)} %get-tuple-element.83), channel_id=1, source_target_pairs={{1,0},{2,1},{3,2},{4,3},{5,4},{6,5},{7,6},{8,7},{9,8},{10,9},{11,1... | collective-permute-start | bytes 2359304 | tf_op jit(solution)/shard_map/ppermute | solution.py:963
  282.4 3.6 copy-start.5
  283.3 3.2 copy-start.2
  283.3 5.9 %copy-start.6 = (f32[512,256]{1,0:T(8,128)S(1)}, f32[512,256]{1,0:T(8,128)}, u32[]{:S(2)}) copy-start(f32[512,256]{1,0:T(8,128)} %get-tuple-element.56) | copy-start | bytes 1572868
  286.5 74.3 %collective-permute-start.23 = (bf16[8,224,768]{2,1,0:T(8,128)(2,1)}, bf16[8,224,768]{2,1,0:T(8,128)(2,1)}, u32[]{:S(2)}, u32[]{:S(2)}) collective-permute-start(bf16[8,224,768]{2,1,0:T(8,128)(2,1)} %add_convert_fusion), channel_id=1, source_target_pairs={{0,1},{1,0},{2,3},{3,2},{4,5},{5,4},{6,7},{7,6},{8,9},{9,8},{10,11... | collective-permute-start | bytes 8257544 | tf_op jit(solution)/shard_map/ppermute | solution.py:41
  337.0 15.3 %collective-permute-start.16 = (bf16[16,80,768]{2,1,0:T(8,128)(2,1)}, bf16[16,80,768]{2,1,0:T(8,128)(2,1)S(1)}, u32[]{:S(2)}, u32[]{:S(2)}) collective-permute-start(bf16[16,80,768]{2,1,0:T(8,128)(2,1)} %get-tuple-element.67), channel_id=1, source_target_pairs={{0,16},{16,0},{1,17},{17,1},{2,18},{18,2},{3,19},{19,3},{4,20},{20... | collective-permute-start | bytes 5898248 | tf_op jit(solution)/shard_map/ppermute | solution.py:45
  353.7 24.9 %copy-start.4 = (bf16[16,80,768]{2,1,0:T(8,128)(2,1)S(1)}, bf16[16,80,768]{2,1,0:T(8,128)(2,1)}, u32[]{:S(2)}) copy-start(bf16[16,80,768]{2,1,0:T(8,128)(2,1)} %get-tuple-element.66) | copy-start | bytes 5898244
  353.7 24.9 %collective-permute-start.17 = (bf16[8,80,768]{2,1,0:T(8,128)(2,1)S(1)}, bf16[8,80,768]{2,1,0:T(8,128)(2,1)S(1)}, u32[]{:S(2)}, u32[]{:S(2)}) collective-permute-start(bf16[8,80,768]{2,1,0:T(8,128)(2,1)S(1)} %add_convert_fusion.2), channel_id=1, source_target_pairs={{0,1},{1,0},{2,3},{3,2},{4,5},{5,4},{6,7},{7,6},{8,9},{9,8},{10,11... | collective-permute-start | bytes 2949128 | tf_op jit(solution)/shard_map/ppermute | solution.py:41
  364.4 22.4 %collective-permute-start.24 = (bf16[4,224,768]{2,1,0:T(8,128)(2,1)S(1)}, bf16[4,224,768]{2,1,0:T(8,128)(2,1)S(1)}, u32[]{:S(2)}, u32[]{:S(2)}) collective-permute-start(bf16[4,224,768]{2,1,0:T(8,128)(2,1)S(1)} %get-tuple-element.76), channel_id=1, source_target_pairs={{0,2},{1,3},{2,0},{3,1},{4,6},{5,7},{6,4},{7,5},{8,10},{9,11},{10,... | collective-permute-start | bytes 4128776 | tf_op jit(solution)/shard_map/ppermute | solution.py:41
  378.9 13.8 %collective-permute-start.18 = (bf16[4,80,768]{2,1,0:T(8,128)(2,1)S(1)}, bf16[4,80,768]{2,1,0:T(8,128)(2,1)S(1)}, u32[]{:S(2)}, u32[]{:S(2)}) collective-permute-start(bf16[4,80,768]{2,1,0:T(8,128)(2,1)S(1)} %get-tuple-element.78), channel_id=1, source_target_pairs={{0,2},{1,3},{2,0},{3,1},{4,6},{5,7},{6,4},{7,5},{8,10},{9,11},{10,... | collective-permute-start | bytes 1474568 | tf_op jit(solution)/shard_map/ppermute | solution.py:41
  387.0 29.8 %collective-permute-start.25 = (bf16[2,224,768]{2,1,0:T(8,128)(2,1)S(1)}, bf16[2,224,768]{2,1,0:T(8,128)(2,1)S(1)}, u32[]{:S(2)}, u32[]{:S(2)}) collective-permute-start(bf16[2,224,768]{2,1,0:T(8,128)(2,1)S(1)} %get-tuple-element.80), channel_id=1, source_target_pairs={{0,4},{1,5},{2,6},{3,7},{4,0},{5,1},{6,2},{7,3},{8,12},{9,13},{10,... | collective-permute-start | bytes 2064392 | tf_op jit(solution)/shard_map/ppermute | solution.py:41
  392.8 17.7 %collective-permute-start.19 = (bf16[2,80,768]{2,1,0:T(8,128)(2,1)S(1)}, bf16[2,80,768]{2,1,0:T(8,128)(2,1)S(1)}, u32[]{:S(2)}, u32[]{:S(2)}) collective-permute-start(bf16[2,80,768]{2,1,0:T(8,128)(2,1)S(1)} %get-tuple-element.86), channel_id=1, source_target_pairs={{0,4},{1,5},{2,6},{3,7},{4,0},{5,1},{6,2},{7,3},{8,12},{9,13},{10,... | collective-permute-start | bytes 737288 | tf_op jit(solution)/shard_map/ppermute | solution.py:41
  410.6 20.3 %collective-permute-start.20 = (bf16[1,80,768]{2,1,0:T(8,128)(2,1)S(1)}, bf16[1,80,768]{2,1,0:T(8,128)(2,1)S(1)}, u32[]{:S(2)}, u32[]{:S(2)}) collective-permute-start(bf16[1,80,768]{2,1,0:T(8,128)(2,1)S(1)} %fusion.8), channel_id=1, source_target_pairs={{0,8},{1,9},{2,10},{3,11},{4,12},{5,13},{6,14},{7,15},{8,0},{9,1},... | collective-permute-start | bytes 368648 | tf_op jit(solution)/shard_map/ppermute | solution.py:41
  416.8 20.9 %collective-permute-start.26 = (bf16[1,224,768]{2,1,0:T(8,128)(2,1)S(1)}, bf16[1,224,768]{2,1,0:T(8,128)(2,1)S(1)}, u32[]{:S(2)}, u32[]{:S(2)}) collective-permute-start(bf16[1,224,768]{2,1,0:T(8,128)(2,1)S(1)} %fusion.3), channel_id=1, source_target_pairs={{0,8},{1,9},{2,10},{3,11},{4,12},{5,13},{6,14},{7,15},{8,0},{9,1},... | collective-permute-start | bytes 1032200 | tf_op jit(solution)/shard_map/ppermute | solution.py:41
  430.9 7.0 %collective-permute-start.21 = (f32[80,768]{1,0:T(8,128)S(1)}, f32[80,768]{1,0:T(8,128)S(1)}, u32[]{:S(2)}, u32[]{:S(2)}) collective-permute-start(f32[80,768]{1,0:T(8,128)S(1)} %fusion.10), channel_id=1, source_target_pairs={{0,16},{16,0},{1,17},{17,1},{2,18},{18,2},{3,19},{19,3},{4,20},{20... | collective-permute-start | bytes 737288 | tf_op jit(solution)/shard_map/ppermute | solution.py:45
  437.8 3.9 collective-permute-start.27
  (1 other events, 1.1 us)

commit v2 on v1

--- a/solution.py
+++ b/solution.py
@@ -1,3 +1,5 @@
+import functools
+
 import jax
 import jax.numpy as jnp
 from jax import lax
@@ -45,14 +47,6 @@
     return lax.ppermute(x, "dp", [(0, 1), (1, 0)])
 
 
-def gather_set(x):
-    x = jnp.concatenate([x, exchange(x, 8, 8)], 0)
-    x = jnp.concatenate([x, exchange(x, 4, 4)], 0)
-    low = jnp.concatenate([x, exchange(x, 2, 1)], 0)
-    high = exchange(low, 1, 2)
-    return low, high, swap_core(low), swap_core(high)
-
-
 def add(*xs):
     total = xs[0].astype(FL)
     for x in xs[1:]:
@@ -60,25 +54,6 @@
     return total
 
 
-def reduce_set(keep, send):
-    got = swap_core(send)
-    up = add(keep[8:], got[8:]).astype(BF)
-    got1 = exchange(up, 1, 2)
-    up = add(keep[4:8], got[4:8], got1[4:]).astype(BF)
-    low = add(keep[:4], got[:4], got1[:4])
-    got2 = exchange(up, 2, 1)
-    up = (low[2:] + got2[2:].astype(FL)).astype(BF)
-    low = low[:2] + got2[:2].astype(FL)
-    got3 = exchange(up, 4, 4)
-    up = (low[1:] + got3[1:].astype(FL)).astype(BF)
-    low = low[:1] + got3[:1].astype(FL)
-    got4 = exchange(up, 8, 8)
-    mine = (low + got4.astype(FL))[0]
-    other = swap_core(mine)
-    first = lax.axis_index("dp") == 0
-    return jnp.where(first, mine, other), jnp.where(first, other, mine)
-
-
 def params(**kw):
     return pltpu.CompilerParams(vmem_limit_bytes=58 * 1024 * 1024, **kw)
 
@@ -115,7 +90,7 @@
 
 
 def qkv_kernel(
-    ids, tok, low, high, olow, ohigh, q_out, k_out, v_out, pool_out, wq, wk, wv, vec_out, up_out, bias, x32, sems
+    ids, tok, low, high, olow, ohigh, q_out, k_out, v_out, pool_out, wq, wk, wv, vec_out, up_out, bias, x32, pool, sems
 ):
     width = tok.shape[1]
     rb = width // NB
@@ -163,8 +138,14 @@
     for j in range(width // 128):
         cols = slice(128 * j, 128 * j + 128)
         x32[j] = x[:, cols].astype(FL)
-        pool_out[:, cols] = (x32[j, pl.ds(0, half, stride=2)] + x32[j, pl.ds(1, half, stride=2)]) * 0.5
-    q = (dot(pool_out[...].astype(BF), wq[...]) + vec_out[0:1]).astype(BF)
+        pool[:, cols] = (x32[j, pl.ds(0, half, stride=2)] + x32[j, pl.ds(1, half, stride=2)]) * 0.5
+    step = pl.program_id(0)
+
+    @pl.when((step > 0) & (step < pl.num_programs(0) - 1))
+    def _():
+        pool_out[...] = pool[...]
+
+    q = (dot(pool[...].astype(BF), wq[...]) + vec_out[0:1]).astype(BF)
     q_out[...] = (q.astype(FL) * HD**-0.5).astype(BF)
 
 
@@ -183,7 +164,7 @@
                 pl.BlockSpec((step // 2, width), lambda i, *_: (i, 0)),
                 pl.BlockSpec((step, width), lambda i, *_: (i, 0)),
                 pl.BlockSpec((step, width), lambda i, *_: (i, 0)),
-                pl.BlockSpec((step // 2, width), lambda i, *_: (i, 0)),
+                pl.BlockSpec((step // 2, width), lambda i, *_: (jnp.clip(i - 1, 0, rows // step - 3), 0)),
                 pl.BlockSpec((width, width), whole),
                 pl.BlockSpec((width, width), whole),
                 pl.BlockSpec((width, width), whole),
@@ -193,6 +174,7 @@
             scratch_shapes=[
                 pltpu.VMEM((16 * NB, width), BF),
                 pltpu.VMEM((width // 128, step, 128), FL),
+                pltpu.VMEM((step // 2, width), FL),
                 pltpu.SemaphoreType.DMA((4,)),
             ],
         ),
@@ -200,7 +182,7 @@
             jax.ShapeDtypeStruct((rows // 2, width), BF),
             jax.ShapeDtypeStruct((rows, width), BF),
             jax.ShapeDtypeStruct((rows, width), BF),
-            jax.ShapeDtypeStruct((rows // 2, width), FL),
+            jax.ShapeDtypeStruct((rows // 4, width), FL),
             jax.ShapeDtypeStruct((width, width), BF),
             jax.ShapeDtypeStruct((width, width), BF),
             jax.ShapeDtypeStruct((width, width), BF),
@@ -218,28 +200,41 @@
 
 
 def one_block(x):
-    r = x.shape[0] // 2
-    lane = lax.broadcasted_iota(jnp.int32, (r, 128), 1)
-    return jnp.where(lane < HD, x[:r], x[r:])
+    r = x.shape[1] // 2
+    line = lax.broadcasted_iota(jnp.int32, (128, r), 0)
+    return jnp.where(line < HD, x[:, :r], x[:, r:]).T
 
 
 def distances(bounds, row, c):
-    low = bounds[pl.ds(row, QB), 0:1]
-    high = bounds[pl.ds(row, QB), 1:2]
-    query = (2 * (row + lax.broadcasted_iota(jnp.int32, (QB, KC), 0))).astype(FL) + 0.5
-    key = (c * KC + lax.broadcasted_iota(jnp.int32, (QB, KC), 1)).astype(FL)
-    return jnp.where((key >= low) & (key < high), jnp.abs(query - key), FAR)
-
-
-def twice(x):
-    return jnp.concatenate([x, x], 1)
-
-
-def forward_kernel(spans, slopes, q, k, v, bounds, o_out, exact_out, lse_out, s_scr, q2, top, total, acc, rest):
+    low = bounds[0:1, pl.ds(row, QB)]
+    high = bounds[1:2, pl.ds(row, QB)]
+    query = (2 * (row + lax.broadcasted_iota(jnp.int32, (KC, QB), 1))).astype(FL) + 0.5
+    key = (c * KC + lax.broadcasted_iota(jnp.int32, (KC, QB), 0)).astype(FL)
+    far = jnp.where((key >= low) & (key < high), jnp.abs(query - key), FAR)
+    return jnp.concatenate([far, far], 1)
+
+
+def fold(x, f):
+    n = x.shape[0] // 8
+    parts = [x[8 * i : 8 * i + 8] for i in range(n)]
+    while len(parts) > 1:
+        parts = [f(parts[2 * i], parts[2 * i + 1]) for i in range(len(parts) // 2)]
+    return parts[0]
+
+
+def slope_line(slopes, head):
+    lane = lax.broadcasted_iota(jnp.int32, (1, 2 * QB), 1)
+    return jnp.where(lane < QB, slopes[head], slopes[head + 1])
+
+
+def forward_kernel(half, spans, slopes, q, k, v, bounds, o_out, exact_out, lse_out, s_scr, vt, q2, top, total, acc, rest):
     pairs = q.shape[1] // 128
-    head0 = pl.program_id(0) * 2 * pairs
-    lane = lax.broadcasted_iota(jnp.int32, (QB, 128), 1)
+    head0 = half * 2 * pairs
     q_first = q.shape[0] // 4
+    slope = [slope_line(slopes, head0 + 2 * j) for j in range(pairs)]
+    for c in range(k.shape[0] // KC):
+        for j in range(pairs):
+            vt[c, j] = v[KC * c : KC * c + KC, 128 * j : 128 * j + 128].T
 
     def query_block(b, _):
         row = pl.multiple_of(q_first + b * QB, QB)
@@ -258,43 +253,38 @@
             far = distances(bounds, row, c)
             keys = pl.ds(pl.multiple_of(c * KC, KC), KC)
             for j in range(pairs):
-                s = dot_t(q2[j], k[keys, 128 * j : 128 * j + 128])
-                s = jnp.concatenate(
-                    [s[:QB] - slopes[head0 + 2 * j] * far, s[QB:] - slopes[head0 + 2 * j + 1] * far], 0
-                )
+                s = dot_t(k[keys, 128 * j : 128 * j + 128], q2[j]) - slope[j] * far
                 s_scr[c - c0, j] = s
-                top[j] = jnp.maximum(top[j], jnp.maximum(s[:, :128], s[:, 128:]))
+                top[j] = jnp.maximum(top[j], fold(s, jnp.maximum))
             return 0
 
         lax.fori_loop(c0, c1, score, 0)
-        for j in range(pairs):
-            top[j] = jnp.broadcast_to(jnp.max(top[j], 1, keepdims=True), (2 * QB, 128))
+        peak = [jnp.max(top[j], 0, keepdims=True) for j in range(pairs)]
 
         def exponent(c, _):
             for j in range(pairs):
-                e = jnp.exp(s_scr[c - c0, j] - twice(top[j]))
+                e = jnp.exp(s_scr[c - c0, j] - peak[j])
                 s_scr[c - c0, j] = e
-                total[j] = total[j] + (e[:, :128] + e[:, 128:])
+                total[j] = total[j] + fold(e, jnp.add)
             return 0
 
         lax.fori_loop(c0, c1, exponent, 0)
-        lse = jnp.zeros((QB, 128), FL)
+        inverse = []
         for j in range(pairs):
-            l = jnp.broadcast_to(jnp.sum(total[j], 1, keepdims=True), (2 * QB, 128))
-            t = top[j] + jnp.log(l)
-            total[j] = 1.0 / l
-            lse = jnp.where(lane == 2 * j, t[:QB], jnp.where(lane == 2 * j + 1, t[QB:], lse))
-        lse_out[out_rows, :] = lse
+            l = jnp.sum(total[j], 0, keepdims=True)
+            t = peak[j] + jnp.log(l)
+            inverse.append(1.0 / l)
+            lse_out[2 * j : 2 * j + 1, out_rows] = t[:, :QB]
+            lse_out[2 * j + 1 : 2 * j + 2, out_rows] = t[:, QB:]
 
         def attend(c, _):
-            keys = pl.ds(pl.multiple_of(c * KC, KC), KC)
             for j in range(pairs):
-                p = s_scr[c - c0, j] * twice(total[j])
+                p = s_scr[c - c0, j] * inverse[j]
                 high = p.astype(BF)
                 low = (p - high.astype(FL)).astype(BF)
-                values = v[keys, 128 * j : 128 * j + 128]
-                acc[j] = acc[j] + dot(high, values)
-                rest[j] = rest[j] + dot(low, values)
+                values = vt[c, j]
+                acc[j] = acc[j] + dot(values, high)
+                rest[j] = rest[j] + dot(values, low)
             return 0
 
         lax.fori_loop(c0, c1, attend, 0)
@@ -304,161 +294,246 @@
             exact_out[out_rows, cols] = one_block(acc[j] + rest[j])
         return 0
 
+    lse_out[...] = jnp.zeros(lse_out.shape, FL)
     lax.fori_loop(0, o_out.shape[0] // QB, query_block, 0)
 
 
-def attend_forward(spans, slopes, q, k, v, bounds, own):
-    width = q.shape[1]
-    wide = width // 2
+def attend_forward(half, spans, slopes, q, k, v, bounds, own):
+    wide = q.shape[1] // 2
     pairs = wide // 128
     chunks = k.shape[0] // KC
-    col = lambda i, *_: (0, i)
+    col = lambda i, *_: (0, half)
+    zero = lambda i, *_: (0, 0)
     return pl.pallas_call(
-        forward_kernel,
-        name="attend_forward",
+        functools.partial(forward_kernel, half),
+        name=f"attend_forward_{half}",
         grid_spec=pltpu.PrefetchScalarGridSpec(
             num_scalar_prefetch=2,
-            grid=(2,),
+            grid=(1,),
             in_specs=[
                 pl.BlockSpec((q.shape[0], wide), col),
                 pl.BlockSpec((k.shape[0], wide), col),
                 pl.BlockSpec((k.shape[0], wide), col),
-                pl.BlockSpec(bounds.shape, lambda i, *_: (0, 0)),
+                pl.BlockSpec(bounds.shape, zero),
             ],
             out_specs=[
-                pl.BlockSpec((own, wide), col),
-                pl.BlockSpec((own, wide), col),
-                pl.BlockSpec((own, 128), col),
+                pl.BlockSpec((own, wide), zero),
+                pl.BlockSpec((own, wide), zero),
+                pl.BlockSpec((8, own), zero),
             ],
             scratch_shapes=[
-                pltpu.VMEM((chunks, pairs, 2 * QB, KC), FL),
+                pltpu.VMEM((chunks, pairs, KC, 2 * QB), FL),
+                pltpu.VMEM((chunks, pairs, 128, KC), BF),
                 pltpu.VMEM((pairs, 2 * QB, 128), BF),
-                pltpu.VMEM((pairs, 2 * QB, 128), FL),
-                pltpu.VMEM((pairs, 2 * QB, 128), FL),
-                pltpu.VMEM((pairs, 2 * QB, 128), FL),
-                pltpu.VMEM((pairs, 2 * QB, 128), FL),
+                pltpu.VMEM((pairs, 8, 2 * QB), FL),
+                pltpu.VMEM((pairs, 8, 2 * QB), FL),
+                pltpu.VMEM((pairs, 128, 2 * QB), FL),
+                pltpu.VMEM((pairs, 128, 2 * QB), FL),
             ],
         ),
         out_shape=[
-            jax.ShapeDtypeStruct((own, width), BF),
-            jax.ShapeDtypeStruct((own, width), FL),
-            jax.ShapeDtypeStruct((own, 256), FL),
+            jax.ShapeDtypeStruct((own, wide), BF),
+            jax.ShapeDtypeStruct((own, wide), FL),
+            jax.ShapeDtypeStruct((8, own), FL),
         ],
         compiler_params=params(),
     )(spans, slopes, q, k, v, bounds)
 
 
-def backward_kernel(
-    spans, slopes, q, k, v, da, stats, bounds, dq_out, dk_out, dv_out, slope_out, q2, da2, lse2, del2, dq2, dk, dv, sl
+def chunk_step(q2, da2, far, slope, lse, delta, kj, vj):
+    p = jnp.exp(dot_t(kj, q2) - slope * far - lse)
+    ds = (p * (dot_t(vj, da2) - delta)).astype(BF)
+    return p.astype(BF), ds
+
+
+def own_kernel(
+    half, spans, slopes, q, k, v, da, stats, bounds, dq_out, dk, dv, slope_out, kt, q2, da2, dq2, sl
 ):
     pairs = q.shape[1] // 128
-    head0 = pl.program_id(0) * 2 * pairs
-    blocks = q.shape[0] // QB
+    head0 = half * 2 * pairs
+    total_blocks = bounds.shape[1] // QB
+    quarter = k.shape[0] // KC // 4
+    first = total_blocks // 4
+    slope = [slope_line(slopes, head0 + 2 * j) for j in range(pairs)]
     dk[...] = jnp.zeros(dk.shape, FL)
     dv[...] = jnp.zeros(dv.shape, FL)
     sl[...] = jnp.zeros(sl.shape, FL)
+    for c in range(k.shape[0] // KC):
+        for j in range(pairs):
+            kt[c, j] = k[KC * c : KC * c + KC, 128 * j : 128 * j + 128].T
 
     def query_block(b, _):
-        row = pl.multiple_of(b * QB, QB)
-        c0 = spans[b]
-        c1 = spans[blocks + b]
-        own = (b >= blocks // 4) & (b < blocks - blocks // 4)
-        counted = jnp.where(own, 1.0, 0.0)
+        row = pl.multiple_of((first + b) * QB, QB)
+        rows = pl.ds(pl.multiple_of(b * QB, QB), QB)
+        c0 = spans[first + b]
+        c1 = spans[total_blocks + first + b]
+        lse = []
+        delta = []
         for j in range(pairs):
             cols = slice(128 * j, 128 * j + 128)
             q2[j] = two_heads(q[pl.ds(row, QB), cols])
-            da2[j] = two_heads(da[pl.ds(row, QB), cols])
-            for i in range(2):
-                rows = slice(QB * i, QB * i + QB)
-                lse2[j, rows] = jnp.broadcast_to(stats[pl.ds(row, QB), 2 * j + i : 2 * j + i + 1], (QB, 128))
-                del2[j, rows] = jnp.broadcast_to(stats[pl.ds(row, QB), 64 + 2 * j + i : 65 + 2 * j + i], (QB, 128))
+            da2[j] = two_heads(da[rows, cols])
+            h = head0 + 2 * j
+            lse.append(jnp.concatenate([stats[h : h + 1, rows], stats[h + 1 : h + 2, rows]], 1))
+            delta.append(jnp.concatenate([stats[16 + h : 17 + h, rows], stats[17 + h : 18 + h, rows]], 1))
         dq2[...] = jnp.zeros(dq2.shape, FL)
 
-        def chunk(c, _):
+        def step(c, grads):
             far = distances(bounds, row, c)
             keys = pl.ds(pl.multiple_of(c * KC, KC), KC)
             for j in range(pairs):
                 cols = slice(128 * j, 128 * j + 128)
-                kj = k[keys, cols]
-                s = dot_t(q2[j], kj)
-                s = jnp.concatenate(
-                    [s[:QB] - slopes[head0 + 2 * j] * far, s[QB:] - slopes[head0 + 2 * j + 1] * far], 0
-                )
-                p = jnp.exp(s - twice(lse2[j]))
-                dp = dot_t(da2[j], v[keys, cols])
-                ds = (p * (dp - twice(del2[j]))).astype(BF)
-                dv[keys, cols] = dv[keys, cols] + t_dot(p.astype(BF), da2[j])
-                dk[keys, cols] = dk[keys, cols] + t_dot(ds, q2[j])
-                dq2[j] = dq2[j] + dot(ds, kj)
-                for i in range(2):
-                    w = ds[QB * i : QB * i + QB].astype(FL) * far
-                    w = jnp.sum(w.reshape(QB // 8, 8, KC), 0)
-                    sl[2 * j + i] = sl[2 * j + i] + counted * (w[:, :128] + w[:, 128:])
+                p, ds = chunk_step(q2[j], da2[j], far, slope[j], lse[j], delta[j], k[keys, cols], v[keys, cols])
+                if grads:
+                    mine = pl.ds(pl.multiple_of((c - quarter) * KC, KC), KC)
+                    dv[mine, cols] = dv[mine, cols] + dot(p, da2[j])
+                    dk[mine, cols] = dk[mine, cols] + dot(ds, q2[j])
+                dq2[j] = dq2[j] + dot(kt[c, j], ds)
+                sl[j] = sl[j] + fold(ds.astype(FL) * far, jnp.add)
+
+        def inside(c, _):
+            step(c, True)
             return 0
 
-        lax.fori_loop(c0, c1, chunk, 0)
-
-        @pl.when(own)
-        def _():
-            out_rows = pl.ds(pl.multiple_of(row - q.shape[0] // 4, QB), QB)
-            for j in range(pairs):
-                dq_out[out_rows, 128 * j : 128 * j + 128] = (one_block(dq2[j]) * HD**-0.5).astype(BF)
-
+        left = jnp.maximum(jnp.minimum(c1, quarter) - c0, 0)
+        right0 = jnp.maximum(c0, 3 * quarter)
+
+        def outside(i, _):
+            step(jnp.where(i < left, c0 + i, right0 + i - left), False)
+            return 0
+
+        lax.fori_loop(jnp.maximum(c0, quarter), jnp.minimum(c1, 3 * quarter), inside, 0)
+        lax.fori_loop(0, left + jnp.maximum(c1 - right0, 0), outside, 0)
+        for j in range(pairs):
+            dq_out[rows, 128 * j : 128 * j + 128] = (one_block(dq2[j]) * HD**-0.5).astype(BF)
         return 0
 
-    lax.fori_loop(0, blocks, query_block, 0)
-    quarter = k.shape[0] // 4
-    dk_out[...] = dk[quarter : 3 * quarter].astype(BF)
-    dv_out[...] = dv[quarter : 3 * quarter].astype(BF)
+    lax.fori_loop(0, da.shape[0] // QB, query_block, 0)
     slope_out[...] = sl[...].reshape(slope_out.shape)
 
 
-def attend_backward(spans, slopes, q, k, v, da, stats, bounds):
-    width = q.shape[1]
-    wide = width // 2
+def attend_own(half, spans, slopes, q, k, v, da, stats, bounds):
+    own = stats.shape[1]
+    wide = q.shape[1] // 2
     pairs = wide // 128
-    rows = q.shape[0]
     keys = k.shape[0]
-    col = lambda i, *_: (0, i)
+    chunks = keys // KC
+    col = lambda i, *_: (0, half)
+    zero = lambda i, *_: (0, 0)
     return pl.pallas_call(
-        backward_kernel,
-        name="attend_backward",
+        functools.partial(own_kernel, half),
+        name=f"attend_own_{half}",
         grid_spec=pltpu.PrefetchScalarGridSpec(
             num_scalar_prefetch=2,
-            grid=(2,),
+            grid=(1,),
             in_specs=[
-                pl.BlockSpec((rows, wide), col),
+                pl.BlockSpec((q.shape[0], wide), col),
                 pl.BlockSpec((keys, wide), col),
                 pl.BlockSpec((keys, wide), col),
-                pl.BlockSpec((rows, wide), col),
-                pl.BlockSpec((rows, 128), col),
-                pl.BlockSpec(bounds.shape, lambda i, *_: (0, 0)),
+                pl.BlockSpec((own, wide), col),
+                pl.BlockSpec(stats.shape, zero),
+                pl.BlockSpec(bounds.shape, zero),
             ],
             out_specs=[
-                pl.BlockSpec((rows // 2, wide), col),
-                pl.BlockSpec((keys // 2, wide), col),
-                pl.BlockSpec((keys // 2, wide), col),
-                pl.BlockSpec((16 * pairs, 128), lambda i, *_: (i, 0)),
+                pl.BlockSpec((own, wide), zero),
+                pl.BlockSpec((keys // 2, wide), zero),
+                pl.BlockSpec((keys // 2, wide), zero),
+                pl.BlockSpec((8 * pairs, 2 * QB), zero),
             ],
+            scratch_shapes=[
+                pltpu.VMEM((chunks, pairs, 128, KC), BF),
+                pltpu.VMEM((pairs, 2 * QB, 128), BF),
+                pltpu.VMEM((pairs, 2 * QB, 128), BF),
+                pltpu.VMEM((pairs, 128, 2 * QB), FL),
+                pltpu.VMEM((pairs, 8, 2 * QB), FL),
+            ],
+        ),
+        out_shape=[
+            jax.ShapeDtypeStruct((own, wide), BF),
+            jax.ShapeDtypeStruct((keys // 2, wide), FL),
+            jax.ShapeDtypeStruct((keys // 2, wide), FL),
+            jax.ShapeDtypeStruct((8 * pairs, 2 * QB), FL),
+        ],
+        compiler_params=params(),
+    )(spans, slopes, q, k, v, da, stats, bounds)
+
+
+def halo_kernel(spans, slopes, q, k, v, low_pay, high_pay, bounds, dk0, dv0, dk1, dv1, dk_out, dv_out, q2, da2, st, dk, dv):
+    wide = dk0.shape[1]
+    width = q.shape[1]
+    pairs = width // 128
+    total_blocks = bounds.shape[1] // QB
+    quarter = k.shape[0] // KC // 4
+    count = low_pay.shape[0] // QB
+    dk[:, :wide] = dk0[...]
+    dk[:, wide:] = dk1[...]
+    dv[:, :wide] = dv0[...]
+    dv[:, wide:] = dv1[...]
+    for side, pay in enumerate((low_pay, high_pay)):
+        x = pay[:, width : width + 128].astype(FL)
+        x = x + pltpu.roll(x, 96, 1) + pltpu.roll(x, 64, 1)
+        st[...] = x.T
+        for i in range(count):
+            block = i if side == 0 else total_blocks - count + i
+            row = block * QB
+            rows = slice(i * QB, i * QB + QB)
+            c0 = spans[block]
+            c1 = spans[total_blocks + block]
+
+            @pl.when(c0 < c1)
+            def _():
+                for j in range(pairs):
+                    cols = slice(128 * j, 128 * j + 128)
+                    q2[j] = two_heads(q[row : row + QB, cols])
+                    da2[j] = two_heads(pay[rows, cols])
+
+                def step(c, _):
+                    far = distances(bounds, row, c)
+                    keys = pl.ds(pl.multiple_of(c * KC, KC), KC)
+                    mine = pl.ds(pl.multiple_of((c - quarter) * KC, KC), KC)
+                    for j in range(pairs):
+                        cols = slice(128 * j, 128 * j + 128)
+                        h = 2 * j
+                        lse = jnp.concatenate([st[h : h + 1, rows], st[h + 1 : h + 2, rows]], 1)
+                        delta = jnp.concatenate([st[16 + h : 17 + h, rows], st[17 + h : 18 + h, rows]], 1)
+                        p, ds = chunk_step(
+                            q2[j], da2[j], far, slope_line(slopes, h), lse, delta, k[keys, cols], v[keys, cols]
+                        )
+                        dv[mine, cols] = dv[mine, cols] + dot(p, da2[j])
+                        dk[mine, cols] = dk[mine, cols] + dot(ds, q2[j])
+                    return 0
+
+                lax.fori_loop(c0, c1, step, 0)
+
+    dk_out[...] = dk[...].astype(BF)
+    dv_out[...] = dv[...].astype(BF)
+
+
+def attend_halo(spans, slopes, q, k, v, low_pay, high_pay, bounds, dk0, dv0, dk1, dv1):
+    width = q.shape[1]
+    pairs = width // 128
+    keys = k.shape[0]
+    full = lambda x: pl.BlockSpec(x.shape, lambda i, *_: (0, 0))
+    shape = jax.ShapeDtypeStruct((keys // 2, width), BF)
+    return pl.pallas_call(
+        halo_kernel,
+        name="attend_halo",
+        grid_spec=pltpu.PrefetchScalarGridSpec(
+            num_scalar_prefetch=2,
+            grid=(1,),
+            in_specs=[full(x) for x in (q, k, v, low_pay, high_pay, bounds, dk0, dv0, dk1, dv1)],
+            out_specs=[full(shape), full(shape)],
             scratch_shapes=[
                 pltpu.VMEM((pairs, 2 * QB, 128), BF),
                 pltpu.VMEM((pairs, 2 * QB, 128), BF),
-                pltpu.VMEM((pairs, 2 * QB, 128), FL),
-                pltpu.VMEM((pairs, 2 * QB, 128), FL),
-                pltpu.VMEM((pairs, 2 * QB, 128), FL),
-                pltpu.VMEM((keys, wide), FL),
-                pltpu.VMEM((keys, wide), FL),
-                pltpu.VMEM((2 * pairs, 8, 128), FL),
+                pltpu.VMEM((128, low_pay.shape[0]), FL),
+                pltpu.VMEM((keys // 2, width), FL),
+                pltpu.VMEM((keys // 2, width), FL),
             ],
         ),
-        out_shape=[
-            jax.ShapeDtypeStruct((rows // 2, width), BF),
-            jax.ShapeDtypeStruct((keys // 2, width), BF),
-            jax.ShapeDtypeStruct((keys // 2, width), BF),
-            jax.ShapeDtypeStruct((32 * pairs, 128), FL),
-        ],
+        out_shape=[shape, shape],
         compiler_params=params(),
-    )(spans, slopes, q, k, v, da, stats, bounds)
+    )(spans, slopes, q, k, v, low_pay, high_pay, bounds, dk0, dv0, dk1, dv1)
 
 
 def normalize(z):
@@ -478,9 +553,12 @@
 def middle_kernel(
     ids,
     pool,
-    att,
-    exact,
-    lse,
+    att0,
+    att1,
+    exact0,
+    exact1,
+    lse0,
+    lse1,
     cot,
     vec,
     upb,
@@ -509,9 +587,12 @@
     dw1,
     dw2,
     dwo,
+    att,
     sems,
 ):
     n, width = att.shape
+    att[:, : width // 2] = att0[...]
+    att[:, width // 2 :] = att1[...]
     rb = width // NB
     fb = w2.shape[0] // NB
     parts = w1.shape[0]
@@ -647,43 +728,47 @@
 
     z[...] = dot_t(hid_low[...], wo[...])
     heads = width // HD
-    head_of = (lax.broadcasted_iota(jnp.int32, (width, 256), 0)) // HD
-    spot = lax.broadcasted_iota(jnp.int32, (width, 256), 1)
-    half = heads // 2
-    spot_of = jnp.where(head_of < half, head_of + 64, head_of - half + 128 + 64)
-    pick = (spot == spot_of).astype(FL).astype(BF)
+    head_of = lax.broadcasted_iota(jnp.int32, (16, width), 1) // HD
+    pick = (head_of == lax.broadcasted_iota(jnp.int32, (16, width), 0)).astype(FL).astype(BF)
+    stats[...] = jnp.zeros(stats.shape, FL)
+    stats[0 : heads // 2, :] = lse0[0 : heads // 2, :]
+    stats[heads // 2 : heads, :] = lse1[0 : heads // 2, :]
 
     def last(r, i):
         d_low = z[r, :].astype(BF)
-        prod = d_low.astype(FL) * exact[r, :]
-        delta = jnp.zeros((rc, 256), FL)
+        pay[r, 0:width] = d_low
+        exact = jnp.concatenate([exact0[r, :], exact1[r, :]], 1)
+        prod = d_low.astype(FL) * exact
+        delta = jnp.zeros((16, rc), FL)
         for _ in range(3):
             piece = prod.astype(BF)
-            delta = delta + dot(piece, pick)
+            delta = delta + dot_t(pick, piece)
             prod = prod - piece.astype(FL)
-        st = jnp.where(lax.broadcasted_iota(jnp.int32, (rc, 256), 1) % 128 < 64, lse[r, :], delta)
-        stats[r, :] = st
-        pay[r, 0:width] = d_low
-        for j in range(3):
-            piece = st.astype(BF)
-            pay[r, width + 256 * j : width + 256 * j + 256] = piece
-            st = st - piece.astype(FL)
+        stats[16:32, r] = delta
 
     row_loop(last)
+    st = stats[...].T
+    pieces = []
+    for _ in range(3):
+        piece = st.astype(BF).astype(FL)
+        pieces.append(piece)
+        st = st - piece
+    pieces.append(jnp.zeros_like(st))
+    pay[:, width:] = jnp.concatenate(pieces, 1).astype(BF)
     wait_all(keep, sems.at[3])
     wait_all(send, sems.at[3])
 
 
-def middle(ids, pool, att, exact, lse, cot, vec, upb, sets, set_rows):
-    n, width = att.shape
+def middle(ids, pool, att0, att1, exact0, exact1, lse0, lse1, cot, vec, upb, sets, set_rows):
+    n, width = pool.shape
     ff = upb.shape[1]
     parts = ff // width
     whole = lambda i, *_: (0, 0)
     full = lambda x: pl.BlockSpec(x.shape, whole)
     shapes = [
         jax.ShapeDtypeStruct((n, width), BF),
-        jax.ShapeDtypeStruct((n, width + 768), BF),
-        jax.ShapeDtypeStruct((n, 256), FL),
+        jax.ShapeDtypeStruct((n, width + 128), BF),
+        jax.ShapeDtypeStruct((32, n), FL),
         jax.ShapeDtypeStruct((n, width), FL),
         jax.ShapeDtypeStruct((8, width), FL),
         jax.ShapeDtypeStruct((8, ff), FL),
@@ -696,7 +781,7 @@
             num_scalar_prefetch=1,
             grid=(1,),
             in_specs=[full(pool)]
-            + [full(x) for x in (att, exact, lse, cot, vec, upb)]
+            + [full(x) for x in (att0, att1, exact0, exact1, lse0, lse1, cot, vec, upb)]
             + [ANY] * 4,
             out_specs=[full(x) for x in shapes] + [ANY, ANY],
             scratch_shapes=[
@@ -713,24 +798,26 @@
                 pltpu.VMEM((parts, width, width), BF),
                 pltpu.VMEM((ff, width), BF),
                 pltpu.VMEM((width, width), BF),
+                pltpu.VMEM((n, width), BF),
                 pltpu.SemaphoreType.DMA((4,)),
             ],
         ),
         out_shape=shapes + [big, big],
         compiler_params=params(),
-    )(ids, pool, att, exact, lse, cot, vec, upb, *sets)
-
-
-def weights_kernel(ids, pool, tok, dq, dk, dv, gvec, gup, sl, keep, send, dwq, dwk, dwv, bias, sems):
+    )(ids, pool, att0, att1, exact0, exact1, lse0, lse1, cot, vec, upb, *sets)
+
+
+def weights_kernel(ids, pool, tok, dq0, dq1, dk, dv, gvec, gup, sl0, sl1, keep, send, dwq, dwk, dwv, bias, sems):
     width = tok.shape[1]
     ff = gup.shape[1]
     rb = width // NB
-    dwq[...] = t_dot(pool[...].astype(BF), dq[...]).astype(BF)
+    dq = jnp.concatenate([dq0[...], dq1[...]], 1)
+    dwq[...] = t_dot(pool[...].astype(BF), dq).astype(BF)
     dwk[...] = t_dot(tok[...], dk[...]).astype(BF)
     dwv[...] = t_dot(tok[...], dv[...]).astype(BF)
     row = lax.broadcasted_iota(jnp.int32, (16, width), 0)
     g = jnp.concatenate([gvec[...], jnp.zeros((8, width), FL)], 0)
-    g = jnp.where(row == 0, rows_sum(dq[...].astype(FL)), g)
+    g = jnp.where(row == 0, rows_sum(dq.astype(FL)), g)
     g = jnp.where(row == 1, rows_sum(dv[...].astype(FL)), g)
     block_of = div_rb(lax.broadcasted_iota(jnp.int32, (16, width), 1))
     parts = []
@@ -745,10 +832,15 @@
     for p in range(NB):
         parts.append(jnp.where(block_of == 4 * (ids[0] ^ rel_b(p)), up, 0.0).astype(BF))
     total = total + dot_t(jnp.concatenate(parts, 0), spread_matrix(128, ff, rb))
-    heads = sl.shape[0] // 8
-    per_head = jnp.sum(jnp.sum(sl[...].reshape(heads, 8, 128), 1), 1, keepdims=True)
-    at = lax.broadcasted_iota(jnp.int32, (heads, 128), 0) == lax.broadcasted_iota(jnp.int32, (heads, 128), 1)
-    line = -jnp.sum(jnp.where(at, per_head, 0.0), 0, keepdims=True)
+    line = jnp.zeros((1, 128), FL)
+    lane = lax.broadcasted_iota(jnp.int32, (1, 128), 1)
+    for half, sl in enumerate((sl0, sl1)):
+        pairs = sl.shape[0] // 8
+        for j in range(pairs):
+            x = rows_sum(sl[8 * j : 8 * j + 8, :])
+            for i in range(2):
+                value = jnp.sum(x[:, QB * i : QB * i + QB], 1, keepdims=True)
+                line = jnp.where(lane == 2 * pairs * half + 2 * j + i, -value, line)
     row = lax.broadcasted_iota(jnp.int32, (16 * NB, 128), 0)
     total = jnp.where((row & 15) == 12, line, total)
     bias[...] = jnp.zeros(bias.shape, BF)
@@ -782,7 +874,7 @@
     wait_all(send, sems.at[0])
 
 
-def weight_grads(ids, pool, tok, dq, dk, dv, gvec, gup, sl, set_rows):
+def weight_grads(ids, pool, tok, dq0, dq1, dk, dv, gvec, gup, sl0, sl1, set_rows):
     width = tok.shape[1]
     full = lambda x: pl.BlockSpec(x.shape, lambda i, *_: (0, 0))
     big = jax.ShapeDtypeStruct((NB, set_rows, width), BF)
@@ -793,7 +885,7 @@
         grid_spec=pltpu.PrefetchScalarGridSpec(
             num_scalar_prefetch=1,
             grid=(1,),
-            in_specs=[full(x) for x in (pool, tok, dq, dk, dv, gvec, gup, sl)],
+            in_specs=[full(x) for x in (pool, tok, dq0, dq1, dk, dv, gvec, gup, sl0, sl1)],
             out_specs=[ANY, ANY],
             scratch_shapes=[
                 square,
@@ -805,12 +897,13 @@
         ),
         out_shape=[big, big],
         compiler_params=params(),
-    )(ids, pool, tok, dq, dk, dv, gvec, gup, sl)
-
-
-def tokens_kernel(mixed, dq, dk, dv, wq, wk, wv, out, acc):
+    )(ids, pool, tok, dq0, dq1, dk, dv, gvec, gup, sl0, sl1)
+
+
+def tokens_kernel(mixed, dq0, dq1, dk, dv, wq, wk, wv, out, acc):
     half = mixed.shape[0]
-    up = 0.5 * (mixed[...] + dot_t(dq[...], wq[...]))
+    dq = jnp.concatenate([dq0[...], dq1[...]], 1)
+    up = 0.5 * (mixed[...] + dot_t(dq, wq[...]))
     down = dot_t(dk[...], wk[...]) + dot_t(dv[...], wv[...])
     for j in range(mixed.shape[1] // 128):
         cols = slice(128 * j, 128 * j + 128)
@@ -819,22 +912,23 @@
         out[:, cols] = acc[j] + down[:, cols]
 
 
-def token_grads(mixed, dq, dk, dv, wq, wk, wv):
+def token_grads(mixed, dq0, dq1, dk, dv, wq, wk, wv):
     rows, width = dk.shape
     step = 512
     half = pl.BlockSpec((step // 2, width), lambda i: (i, 0))
     block = pl.BlockSpec((step, width), lambda i: (i, 0))
     whole = pl.BlockSpec((width, width), lambda i: (0, 0))
+    thin = pl.BlockSpec((step // 2, width // 2), lambda i: (i, 0))
     return pl.pallas_call(
         tokens_kernel,
         name="token_grads",
         grid=(rows // step,),
-        in_specs=[half, half, block, block, whole, whole, whole],
+        in_specs=[half, thin, thin, block, block, whole, whole, whole],
         out_specs=block,
         out_shape=jax.ShapeDtypeStruct((rows, width), FL),
         scratch_shapes=[pltpu.VMEM((width // 128, step, 128), FL)],
         compiler_params=params(),
-    )(mixed, dq, dk, dv, wq, wk, wv)
+    )(mixed, dq0, dq1, dk, dv, wq, wk, wv)
 
 
 def blocks_of(x):
@@ -870,6 +964,57 @@
     parts = 4
     w1 = jnp.concatenate([b2[..., 48 * c : 48 * c + 48, :] for c in range(parts)], -1)
     return wq, wk, wv, wo, w1, w2, bias
+
+
+def pack_kernel(ids, wq, wk, wv, wo, w1, w2, b_up, *refs):
+    vectors, (first, second, bias) = refs[:8], refs[8:]
+    rb, width = wq.shape
+
+    @pl.when(ids[1] == 0)
+    def _():
+        first[0, 0:48] = wq[...].astype(BF)
+        first[0, 48:80] = wk[0:32].astype(BF)
+        second[0, 0:192] = w2[...].astype(BF)
+        second[0, 192:224] = wo[0:32].astype(BF)
+
+    @pl.when(ids[1] != 0)
+    def _():
+        bias[...] = jnp.zeros(bias.shape, FL)
+        for i, x in enumerate(vectors):
+            bias[i : i + 1, 0:rb] = x[...]
+        for c in range(4):
+            bias[8 + c : 9 + c, 0:rb] = b_up[:, rb * c : rb * c + rb]
+        first[0, 0:16] = wk[32:48].astype(BF)
+        first[0, 16:64] = wv[...].astype(BF)
+        first[0, 64:80] = bias[...].astype(BF)
+        for c in range(4):
+            second[0, 48 * c : 48 * c + 48] = w1[:, width * c : width * c + width].astype(BF)
+        second[0, 192:208] = wo[32:48].astype(BF)
+        second[0, 208:224] = wo[32:48].astype(BF)
+
+
+def pack_own(ids, masters, b_up, vectors):
+    width = masters[0].shape[1]
+    args = list(masters) + [b_up[None]] + [x[None] for x in vectors]
+    full = lambda x: pl.BlockSpec(x.shape, lambda i, *_: (0,) * len(x.shape))
+    shapes = [jax.ShapeDtypeStruct((1, 80, width), BF), jax.ShapeDtypeStruct((1, 224, width), BF)]
+    return pl.pallas_call(
+        pack_kernel,
+        name="pack",
+        grid_spec=pltpu.PrefetchScalarGridSpec(
+            num_scalar_prefetch=1,
+            grid=(1,),
+            in_specs=[full(x) for x in args],
+            out_specs=[full(x) for x in shapes],
+            scratch_shapes=[pltpu.VMEM((16, width), FL)],
+        ),
+        out_shape=shapes,
+        compiler_params=params(),
+    )(ids, *args)
+
+
+def after(x, *done):
+    return lax.optimization_barrier((x,) + done)[0]
 
 
 def local(
@@ -909,11 +1054,20 @@
     if direct:
         core = lax.axis_index("dp")
         ids = jnp.stack([lax.axis_index("seq"), core]).astype(jnp.int32)
-        a1, b1, a2, b2 = pack(*masters, bias_block(vectors, b_up, width), width)
-        first = jnp.where(core == 0, a1, b1).astype(BF)[None]
-        second = jnp.where(core == 0, a2, b2).astype(BF)[None]
-        sets1 = gather_set(first)
-        sets2 = gather_set(second)
+        first, second = pack_own(ids, masters, b_up, vectors)
+        low_tokens = lax.ppermute(tokens[rows_here - halo :], order, up_pairs)
+        x = jnp.concatenate([first, exchange(first, 8, 8)], 0)
+        x = jnp.concatenate([x, exchange(x, 4, 4)], 0)
+        y0 = after(second, x)
+        x1, y1, low_tokens = lax.optimization_barrier((exchange(x, 2, 1), exchange(y0, 8, 8), low_tokens))
+        low1 = jnp.concatenate([x, x1], 0)
+        y = jnp.concatenate([y0, y1], 0)
+        high_tokens = lax.ppermute(after(tokens[:halo], x1), order, down_pairs)
+        high1, olow1, y1, high_tokens = lax.optimization_barrier(
+            (exchange(low1, 1, 2), swap_core(low1), exchange(y, 4, 4), high_tokens)
+        )
+        sets1 = (low1, high1, olow1, swap_core(high1))
+        y = jnp.concatenate([y, y1], 0)
     else:
         ids = jnp.zeros((2,), jnp.int32)
         gather = lambda x: lax.all_gather(x.astype(BF), "seq", axis=0, tiled=True)
@@ -925,6 +1079,8 @@
         at_b = jnp.array([rel_b(p) for p in range(NB)])
         sets1 = (a1[at_a[:8]], a1[at_a[8:]], b1[at_b[:8]], b1[at_b[8:]])
         sets2 = (a2[at_a[:8]], a2[at_a[8:]], b2[at_b[:8]], b2[at_b[8:]])
+        low_tokens = lax.ppermute(tokens[rows_here - halo :], order, up_pairs)
+        high_tokens = lax.ppermute(tokens[:halo], order, down_pairs)
 
     first_row = lax.axis_index(order) * rows_here
     total = devices * rows_here
@@ -937,8 +1093,7 @@
     shift = first_row - halo
     begin = jnp.where(inside, begin - shift, 0)
     end = jnp.where(inside, end - shift, 0)
-    bounds = jnp.stack([begin, end], 1).astype(FL)
-    bounds = jnp.pad(bounds, ((0, 0), (0, 126)))
+    bounds = jnp.pad(jnp.stack([begin, end], 0).astype(FL), ((0, 6), (0, 0)))
     blocks = 2 * own // QB
     chunks = (rows_here + 2 * halo) // KC
     low_chunk = jnp.min(jnp.where(inside, begin, 4 * total).reshape(blocks, QB), 1) // KC
@@ -949,31 +1104,74 @@
     high_chunk = jnp.clip(high_chunk, 0, jnp.where(away, chunks - chunks // 4, chunks))
     spans = jnp.concatenate([low_chunk, high_chunk]).astype(jnp.int32)
 
-    low_tokens = lax.ppermute(tokens[rows_here - halo :], order, up_pairs)
-    high_tokens = lax.ppermute(tokens[:halo], order, down_pairs)
     tok_ext = jnp.concatenate([low_tokens, tokens, high_tokens], 0)
 
+    slopes = distance_slope
     q, k, v, pool, wq, wk, wv, vec, upb = qkv(ids, tok_ext, sets1, ff)
-    pool = pool[own // 2 : own // 2 + own]
-    att, exact, lse = attend_forward(spans, distance_slope, q, k, v, bounds, own)
+    if direct:
+        y1, k = lax.optimization_barrier((exchange(y, 2, 1), k))
+        low2 = jnp.concatenate([y, y1], 0)
+        bounds = after(bounds, low2)
+    att0, exact0, lse0 = attend_forward(0, spans, slopes, q, k, v, bounds, own)
+    att1, exact1, lse1 = attend_forward(1, spans, slopes, q, k, v, after(bounds, lse0), own)
+    if direct:
+        high2, lse1 = lax.optimization_barrier((exchange(low2, 1, 2), lse1))
+        sets2 = (low2, high2, swap_core(low2), swap_core(high2))
     out, pay, stats, mixed, gvec, gup, keep2, send2 = middle(
-        ids, pool, att, exact, lse, cotangent, vec, upb, sets2, 224
+        ids, pool, att0, att1, exact0, exact1, lse0, lse1, cotangent, vec, upb, sets2, 224
     )
     low_pay = lax.ppermute(pay[own // 2 :], order, up_pairs)
     high_pay = lax.ppermute(pay[: own // 2], order, down_pairs)
-
-    def stats_of(x):
-        return add(*[x[:, width + 256 * j : width + 256 * j + 256] for j in range(3)])
-
-    da = jnp.concatenate([low_pay[:, :width], pay[:, :width], high_pay[:, :width]], 0)
-    stats_ext = jnp.concatenate([stats_of(low_pay), stats, stats_of(high_pay)], 0)
-    dq, dk, dv, sl = attend_backward(spans, distance_slope, q, k, v, da, stats_ext, bounds)
-    keep1, send1 = weight_grads(ids, pool, tokens, dq, dk, dv, gvec, gup, sl, 80)
-    grad_tokens = token_grads(mixed, dq, dk, dv, wq, wk, wv)
-
+    dq0, dk0, dv0, sl0 = attend_own(0, spans, slopes, q, k, v, pay, stats, bounds)
     if direct:
-        a2, b2 = reduce_set(keep2, send2)
-        a1, b1 = reduce_set(keep1, send1)
+        got = swap_core(send2)
+        got, keep2, dq0, low_pay, high_pay = lax.optimization_barrier((got, keep2, dq0, low_pay, high_pay))
+        up = add(keep2[8:], got[8:]).astype(BF)
+        bounds = after(bounds, up)
+    dq1, dk1, dv1, sl1 = attend_own(1, spans, slopes, q, k, v, pay, stats, bounds)
+    if direct:
+        got1 = exchange(up, 1, 2)
+        got1, dq1 = lax.optimization_barrier((got1, dq1))
+        up = add(keep2[4:8], got[4:8], got1[4:]).astype(BF)
+        bounds = after(bounds, up)
+    dk, dv = attend_halo(spans, slopes, q, k, v, low_pay, high_pay, bounds, dk0, dv0, dk1, dv1)
+    if direct:
+        got2 = exchange(up, 2, 1)
+        got2, dk = lax.optimization_barrier((got2, dk))
+        low = add(keep2[:4], got[:4], got1[:4])
+        up = (low[2:] + got2[2:].astype(FL)).astype(BF)
+        sl0 = after(sl0, up)
+    keep1, send1 = weight_grads(ids, pool, tokens, dq0, dq1, dk, dv, gvec, gup, sl0, sl1, 80)
+    if direct:
+        core0 = lax.axis_index("dp") == 0
+        got3 = exchange(up, 4, 4)
+        got3, send1 = lax.optimization_barrier((got3, send1))
+        low = low[:2] + got2[:2].astype(FL)
+        up = (low[1:] + got3[1:].astype(FL)).astype(BF)
+        low = low[:1] + got3[:1].astype(FL)
+        got = swap_core(send1)
+        got4 = exchange(up, 8, 8)
+        part = add(keep1[8:], got[8:]).astype(BF)
+        got1 = exchange(part, 1, 2)
+        mixed = after(mixed, part)
+    grad_tokens = token_grads(mixed, dq0, dq1, dk, dv, wq, wk, wv)
+
+    if direct:
+        got1, grad_tokens = lax.optimization_barrier((got1, grad_tokens))
+        part = add(keep1[4:8], got[4:8], got1[4:]).astype(BF)
+        got2 = exchange(part, 2, 1)
+        mine = (low + got4.astype(FL))[0]
+        other = swap_core(mine)
+        a2, b2 = jnp.where(core0, mine, other), jnp.where(core0, other, mine)
+        low = add(keep1[:4], got[:4], got1[:4])
+        part = (low[2:] + got2[2:].astype(FL)).astype(BF)
+        low = low[:2] + got2[:2].astype(FL)
+        got3 = exchange(part, 4, 4)
+        part = (low[1:] + got3[1:].astype(FL)).astype(BF)
+        low = low[:1] + got3[:1].astype(FL)
+        mine = (low + exchange(part, 8, 8).astype(FL))[0]
+        other = swap_core(mine)
+        a1, b1 = jnp.where(core0, mine, other), jnp.where(core0, other, mine)
         gq, gk, gv, go, g1, g2, gb = unpack(a1, b1, a2, b2, width)
         rb = width // NB
         small = [gb[i, :rb] for i in range(8)]

time: 448 us -> 356 us (0.79)
  waiting for transfers between devices: 198 us -> 106 us
  Pallas kernels: 125 us -> 148 us
  starting transfers between devices: 79 us -> 57.5 us
  local copies, waits for them, and re-layouts: 18.3 us -> 12.7 us
    ppermute x16, waiting for transfers between devices: 134 us -> 97 us  [exchange(): return lax.ppermute(x, ('dp', 'seq'), pairs)]
    ppermute x1, waiting for transfers between devices: 31.1 us -> 0.01 us  [local(): low_pay = lax.ppermute(pay[own // 2:], order, up_pairs)]
    ppermute x1, waiting for transfers between devices: 28.2 us -> 0.01 us  [local(): low_tokens = lax.ppermute(tokens[rows_here - halo:], order, up_pairs)]
    pallas_call x2 -> x6, Pallas kernels: 58.4 us -> 78.4 us  [the longest x2 36.6 us: attend_own(): pl.pallas_call(functools.partial(own_kernel, half), name=f'attend_own_{ha...]
    ppermute x16, starting transfers between devices: 48.2 us -> 37.7 us  [exchange(): return lax.ppermute(x, ('dp', 'seq'), pairs)]
    ppermute x8, starting transfers between devices: 18.3 us -> 8.24 us  [swap_core(): return lax.ppermute(x, 'dp', [(0, 1), (1, 0)])]
    convert_element_type x11 -> x8, other arithmetic: 9.63 us -> 15 us  [the longest x1 4.62 us: local(): up = add(keep2[4:8], got[4:8], got1[4:]).astype(BF)]
    ppermute x8, waiting for transfers between devices: 3.83 us -> 9.19 us  [swap_core(): return lax.ppermute(x, 'dp', [(0, 1), (1, 0)])]
  transfers between devices with their start and end apart: 28 -> 28, of which waited for: 16 -> 16; matrix products, arithmetic and copies ran while one was open for 6% -> 5% of each run, Pallas kernels for 20% -> 31%
where the time goes in v2:
time: 356 us; the launch traced here: 350 us
  Pallas kernels  148 us (42%)
  waiting for transfers between devices  106 us (30%)
  starting transfers between devices  57.5 us (16%)
  other arithmetic  24.7 us (7%)
  local copies, waits for them, and re-layouts  12.7 us (4%)
    ppermute x16, waiting for transfers between devices, exchange(): return lax.ppermute(x, ('dp', 'seq'), pairs)  97 us
    ppermute x16, starting transfers between devices, exchange(): return lax.ppermute(x, ('dp', 'seq'), pairs)  37.7 us
    pallas_call x2, Pallas kernels, attend_own(): pl.pallas_call(functools.partial(own_kernel, half), name=f'attend_own_{ha...  36.6 us
    pallas_call x1, Pallas kernels, middle(): pl.pallas_call(middle_kernel, name='middle', grid_spec=pltpu.PrefetchScal...  36 us
    pallas_call x2, Pallas kernels, attend_forward(): pl.pallas_call(functools.partial(forward_kernel, half), name=f'attend_for...  28.3 us
    pallas_call x1, Pallas kernels, qkv(): pl.pallas_call(qkv_kernel, name='qkv', grid_spec=pltpu.PrefetchScalarGrid...  15.9 us
    pallas_call x1, Pallas kernels, attend_halo(): pl.pallas_call(halo_kernel, name='attend_halo', grid_spec=pltpu.PrefetchS...  10.5 us
    pallas_call x1, Pallas kernels, weight_grads(): pl.pallas_call(weights_kernel, name='weight_grads', grid_spec=pltpu.Prefe...  9.44 us
  transfers between devices with their start and end apart: 28, of which 16 were waited for; matrix products, arithmetic and copies ran while one was open for 5% of the time, Pallas kernels for 31%

profile of v2, /device:TPU:0, one launch (start us, length us, event | category | flops | bytes accessed | tf_op | source)
XLA Modules:
  0.0 350.2 jit_solution(5074978481519267958)
XLA Ops:
  1.3 3.0 pack.1
  4.3 4.1 %collective-permute-start = (bf16[1,80,768]{2,1,0:T(8,128)(2,1)}, bf16[1,80,768]{2,1,0:T(8,128)(2,1)S(1)}, u32[]{:S(2)}, u32[]{:S(2)}) collective-permute-start(bf16[1,80,768]{2,1,0:T(8,128)(2,1)} %get-tuple-element.87), channel_id=1, source_target_pairs={{0,8},{1,9},{2,10},{3,11},{4,12},{5,13},{6,14},{7,15},{8,0},{9,1},... | collective-permute-start | bytes 368648 | tf_op jit(solution)/shard_map/ppermute | solution.py:43
  8.4 6.2 %collective-permute-done = bf16[1,80,768]{2,1,0:T(8,128)(2,1)S(1)} collective-permute-done((bf16[1,80,768]{2,1,0:T(8,128)(2,1)}, bf16[1,80,768]{2,1,0:T(8,128)(2,1)S(1)}, u32[]{:S(2)}, u32[]{:S(2)}) %collective-permute-start) | collective-permute-done | bytes 122912 | tf_op jit(solution)/shard_map/ppermute | solution.py:43
  16.5 3.4 collective-permute-start.4
  20.0 2.7 collective-permute-done.1
  22.8 1.4 collective-permute-start.2
  24.2 3.3 collective-permute-start.3
  27.4 14.8 %collective-permute-done.3 = bf16[1,224,768]{2,1,0:T(8,128)(2,1)S(1)} collective-permute-done((bf16[1,224,768]{2,1,0:T(8,128)(2,1)S(1)}, bf16[1,224,768]{2,1,0:T(8,128)(2,1)S(1)}, u32[]{:S(2)}, u32[]{:S(2)}) %collective-permute-start.3) | collective-permute-done | bytes 344096 | tf_op jit(solution)/shard_map/ppermute | solution.py:43
  44.3 1.3 collective-permute-start.8
  45.6 9.0 %collective-permute-start.7 = (bf16[2,224,768]{2,1,0:T(8,128)(2,1)S(1)}, bf16[2,224,768]{2,1,0:T(8,128)(2,1)S(1)}, u32[]{:S(2)}, u32[]{:S(2)}) collective-permute-start(bf16[2,224,768]{2,1,0:T(8,128)(2,1)S(1)} %pad_maximum_fusion.2), channel_id=1, source_target_pairs={{0,4},{1,5},{2,6},{3,7},{4,0},{5,1},{6,2},{7,3},{8,12},{9,13},{10,... | collective-permute-start | bytes 2064392 | tf_op jit(solution)/shard_map/ppermute | solution.py:43
  54.6 32.5 %collective-permute-done.7 = bf16[2,224,768]{2,1,0:T(8,128)(2,1)S(1)} collective-permute-done((bf16[2,224,768]{2,1,0:T(8,128)(2,1)S(1)}, bf16[2,224,768]{2,1,0:T(8,128)(2,1)S(1)}, u32[]{:S(2)}, u32[]{:S(2)}) %collective-permute-start.7) | collective-permute-done | bytes 688160 | tf_op jit(solution)/shard_map/ppermute | solution.py:43
  90.8 1.8 pad_maximum_fusion.tok
  92.6 15.9 %qkv.1 = (bf16[1024,768]{1,0:T(8,128)(2,1)}, bf16[2048,768]{1,0:T(8,128)(2,1)}, bf16[2048,768]{1,0:T(8,128)(2,1)}, f32[512,768]{1,0:T(8,128)}, bf16[768,768]{1,0...) custom-call(s32[2]{0:T(128)} %pad_add_fusion.ids, ...), custom_call_target="tpu_custom_call" | custom-call | tf_op jit(solution)/shard_map/qkv/pallas_call | solution.py:156
  108.5 1.3 constant_dynamic-update-slice_fusion.7.low
  109.8 1.3 collective-permute-start.11
  114.6 14.2 %attend_forward_0.1 = (bf16[512,384]{1,0:T(8,128)(2,1)}, f32[512,384]{1,0:T(8,128)}, f32[8,512]{1,0:T(8,128)}) custom-call(s32[16]{0:T(128)} %pad_add_fusion.1.spans, f32[12]{0:T(128)} %slopes.9, bf16[1024,768]{1,0:T(8,128)(2,1)} %get-tuple-element.98.q, bf16[2048,768]{1,0:T(8,128)(2,1)} %get-tuple-element.101.k, bf16[2048,768]{1,0:T(8,128)(2,1)} %get-tuple-element.102.v, ...), custom_call_target="tpu_custom_call" | custom-call | tf_op jit(solution)/shard_map/attend_forward_0/pallas_call | solution.py:307
  128.7 14.2 %attend_forward_1.1 = (bf16[512,384]{1,0:T(8,128)(2,1)}, f32[512,384]{1,0:T(8,128)}, f32[8,512]{1,0:T(8,128)}) custom-call(s32[16]{0:T(128)} %pad_add_fusion.1.spans, f32[12]{0:T(128)} %slopes.9, bf16[1024,768]{1,0:T(8,128)(2,1)} %get-tuple-element.98.q, bf16[2048,768]{1,0:T(8,128)(2,1)} %get-tuple-element.101.k, bf16[2048,768]{1,0:T(8,128)(2,1)} %get-tuple-element.102.v, ...), custom_call_target="tpu_custom_call" | custom-call | tf_op jit(solution)/shard_map/attend_forward_1/pallas_call | solution.py:307
  143.1 2.5 collective-permute-start.13
  145.6 4.7 %collective-permute-done.13.ohigh = bf16[8,224,768]{2,1,0:T(8,128)(2,1)S(1)} collective-permute-done((bf16[8,224,768]{2,1,0:T(8,128)(2,1)S(1)}, bf16[8,224,768]{2,1,0:T(8,128)(2,1)S(1)}, u32[]{:S(2)}, u32[]{:S(2)}) %collective-permute-start.13) | collective-permute-done | bytes 2752544 | tf_op jit(solution)/shard_map/ppermute | solution.py:47
  150.3 1.5 copy-done.3
  151.8 36.0 %middle.1 = (bf16[512,768]{1,0:T(8,128)(2,1)}, bf16[512,896]{1,0:T(8,128)(2,1)}, f32[32,512]{1,0:T(8,128)}, f32[512,768]{1,0:T(8,128)}, f32[8,768]{1,0:T(8,128)}...) custom-call(s32[2]{0:T(128)} %pad_add_fusion.ids, ...), custom_call_target="tpu_custom_call" | custom-call | tf_op jit(solution)/shard_map/middle/pallas_call | solution.py:777
  188.3 2.1 fusion.17
  190.4 1.3 collective-permute-start.16
  191.7 5.6 %collective-permute-start.15 = (bf16[256,896]{1,0:T(8,128)(2,1)S(1)}, bf16[256,896]{1,0:T(8,128)(2,1)}, u32[]{:S(2)}, u32[]{:S(2)}) collective-permute-start(bf16[256,896]{1,0:T(8,128)(2,1)S(1)} %get-tuple-element.175), channel_id=1, source_target_pairs={{0,1},{1,2},{2,3},{3,4},{4,5},{5,6},{6,7},{7,8},{8,9},{9,10},{10,1... | collective-permute-start | bytes 1376264 | tf_op jit(solution)/shard_map/ppermute | solution.py:1123
  197.3 18.4 %attend_own_0.1 = (bf16[512,384]{1,0:T(8,128)(2,1)}, f32[1024,384]{1,0:T(8,128)}, f32[1024,384]{1,0:T(8,128)}, f32[24,256]{1,0:T(8,128)}) custom-call(s32[16]{0:T(128)} %pad_add_fusion.1.spans, f32[12]{0:T(128)} %slopes.9, bf16[1024,768]{1,0:T(8,128)(2,1)} %get-tuple-element.98.q, bf16[2048,768]{1,0:T(8,128)(2,1)} %get-tuple-element.101.k, ...), custom_call_target="tpu_custom_call" | custom-call | tf_op jit(solution)/shard_map/attend_own_0/pallas_call | solution.py:423
  215.7 4.0 %add_convert_fusion = bf16[8,224,768]{2,1,0:T(8,128)(2,1)} fusion(bf16[16,224,768]{2,1,0:T(8,128)(2,1)} %collective-permute-done.14, bf16[16,224,768]{2,1,0:T(8,128)(2,1)S(1)} %bitcast.55), kind=kLoop, calls=%fused_computation | loop fusion | flops 5505024 | bytes 8257536 | tf_op jit(solution)/shard_map/convert_element_type | solution.py:1129
  219.7 1.9 collective-permute-start.17
  221.6 18.2 %attend_own_1.1 = (bf16[512,384]{1,0:T(8,128)(2,1)}, f32[1024,384]{1,0:T(8,128)}, f32[1024,384]{1,0:T(8,128)}, f32[24,256]{1,0:T(8,128)}) custom-call(s32[16]{0:T(128)} %pad_add_fusion.1.spans, f32[12]{0:T(128)} %slopes.9, bf16[1024,768]{1,0:T(8,128)(2,1)} %get-tuple-element.98.q, bf16[2048,768]{1,0:T(8,128)(2,1)} %get-tuple-element.101.k, ...), custom_call_target="tpu_custom_call" | custom-call | tf_op jit(solution)/shard_map/attend_own_1/pallas_call | solution.py:423
  239.8 13.2 %collective-permute-done.17 = bf16[8,224,768]{2,1,0:T(8,128)(2,1)S(1)} collective-permute-done((bf16[8,224,768]{2,1,0:T(8,128)(2,1)}, bf16[8,224,768]{2,1,0:T(8,128)(2,1)S(1)}, u32[]{:S(2)}, u32[]{:S(2)}) %collective-permute-start.17) | collective-permute-done | bytes 2752544 | tf_op jit(solution)/shard_map/ppermute | solution.py:43
  252.9 4.6 %add_convert_fusion.1 = (bf16[4,224,768]{2,1,0:T(8,128)(2,1)}, f32[4,224,768]{2,1,0:T(8,128)S(1)}) fusion(bf16[8,224,768]{2,1,0:T(8,128)(2,1)S(1)} %collective-permute-done.17, bf16[16,224,768]{2,1,0:T(8,128)(2,1)} %collective-permute-done.14, bf16[16,224,768]{2,1,0:T(8,128)(2,1)} %get-tuple-element.123), kind=kLoop, calls=%fused_computation.3 | loop fusion | flops 7569408 | bytes 12386304 | tf_op jit(solution)/shard_map/convert_element_type | solution.py:1135
  258.7 10.5 %attend_halo.1 = (bf16[1024,768]{1,0:T(8,128)(2,1)}, bf16[1024,768]{1,0:T(8,128)(2,1)}) custom-call(s32[16]{0:T(128)} %pad_add_fusion.1.spans, f32[12]{0:T(128)} %slopes.9, bf16[1024,768]{1,0:T(8,128)(2,1)} %get-tuple-element.98.q, bf16[2048,768]{1,0:T(8,128)(2,1)} %get-tuple-element.101.k, bf16[2048,768]{1,0:T(8,128)(2,1)} %get-tuple-element.102.v, ...), custom_call_target="tpu_custom_call" | custom-call | tf_op jit(solution)/shard_map/attend_halo/pallas_call | solution.py:518
  269.2 6.9 %collective-permute-done.18 = bf16[4,224,768]{2,1,0:T(8,128)(2,1)S(1)} collective-permute-done((bf16[4,224,768]{2,1,0:T(8,128)(2,1)}, bf16[4,224,768]{2,1,0:T(8,128)(2,1)S(1)}, u32[]{:S(2)}, u32[]{:S(2)}) %collective-permute-start.18) | collective-permute-done | bytes 1376288 | tf_op jit(solution)/shard_map/ppermute | solution.py:43
  276.4 9.4 %weight_grads.1 = (bf16[16,80,768]{2,1,0:T(8,128)(2,1)}, bf16[16,80,768]{2,1,0:T(8,128)(2,1)}) custom-call(s32[2]{0:T(128)} %pad_add_fusion.ids, f32[512,768]{1,0:T(8,128)} %get-tuple-element.97.pool, bf16[1024,768]{1,0:T(8,128)(2,1)} %tok.1, bf16[512,384]{1,0:T(8,128)(2,1)} %get-tuple-element.122.dq0, bf16[512,384]{1,0:T(8,128)(2,1)} %get-tuple-element.127.dq1, ...), custom_call_target="tpu_custom_call" | custom-call | tf_op jit(solution)/shard_map/weight_grads/pallas_call | solution.py:882
  285.9 5.5 %collective-permute-done.19 = bf16[2,224,768]{2,1,0:T(8,128)(2,1)S(1)} collective-permute-done((bf16[2,224,768]{2,1,0:T(8,128)(2,1)S(1)}, bf16[2,224,768]{2,1,0:T(8,128)(2,1)S(1)}, u32[]{:S(2)}, u32[]{:S(2)}) %collective-permute-start.19) | collective-permute-done | bytes 688160 | tf_op jit(solution)/shard_map/ppermute | solution.py:43
  291.3 3.2 collective-permute-start.20
  294.6 3.8 %collective-permute-done.20 = bf16[16,80,768]{2,1,0:T(8,128)(2,1)S(1)} collective-permute-done((bf16[16,80,768]{2,1,0:T(8,128)(2,1)}, bf16[16,80,768]{2,1,0:T(8,128)(2,1)S(1)}, u32[]{:S(2)}, u32[]{:S(2)}) %collective-permute-start.20) | collective-permute-done | bytes 1966112 | tf_op jit(solution)/shard_map/ppermute | solution.py:47
  298.4 2.2 add_convert_fusion.2
  300.5 1.9 collective-permute-start.21
  303.3 4.8 %collective-permute-start.26 = (bf16[1,224,768]{2,1,0:T(8,128)(2,1)}, bf16[1,224,768]{2,1,0:T(8,128)(2,1)}, u32[]{:S(2)}, u32[]{:S(2)}) collective-permute-start(bf16[1,224,768]{2,1,0:T(8,128)(2,1)} %fusion.3), channel_id=1, source_target_pairs={{0,8},{1,9},{2,10},{3,11},{4,12},{5,13},{6,14},{7,15},{8,0},{9,1},... | collective-permute-start | bytes 1032200 | tf_op jit(solution)/shard_map/ppermute | solution.py:43
  308.1 8.0 %token_grads.1 = f32[1024,768]{1,0:T(8,128)} custom-call(f32[512,768]{1,0:T(8,128)} %get-tuple-element.149.mixed, bf16[512,384]{1,0:T(8,128)(2,1)} %get-tuple-element.122.dq0, bf16[512,384]{1,0:T(8,128)(2,1)} %get-tuple-element.127.dq1, bf16[1024,768]{1,0:T(8,128)(2,1)} %get-tuple-element.137.dk, bf16[1024,768]{1,0:T(8,128)(2,1)} %get-tuple-element.138.dv, ...), custom_call_target="tpu_custom_call" | custom-call | tf_op jit(solution)/shard_map/token_grads/pallas_call | solution.py:922
  316.1 2.3 add_convert_fusion.3
  319.4 4.7 %collective-permute-done.26 = bf16[1,224,768]{2,1,0:T(8,128)(2,1)} collective-permute-done((bf16[1,224,768]{2,1,0:T(8,128)(2,1)}, bf16[1,224,768]{2,1,0:T(8,128)(2,1)}, u32[]{:S(2)}, u32[]{:S(2)}) %collective-permute-start.26) | collective-permute-done | bytes 344096 | tf_op jit(solution)/shard_map/ppermute | solution.py:43
  325.3 2.2 collective-permute-done.22
  327.5 1.1 fusion.6
  328.6 1.8 collective-permute-start.23
  330.5 5.0 %collective-permute-done.23 = bf16[2,80,768]{2,1,0:T(8,128)(2,1)S(1)} collective-permute-done((bf16[2,80,768]{2,1,0:T(8,128)(2,1)S(1)}, bf16[2,80,768]{2,1,0:T(8,128)(2,1)S(1)}, u32[]{:S(2)}, u32[]{:S(2)}) %collective-permute-start.23) | collective-permute-done | bytes 245792 | tf_op jit(solution)/shard_map/ppermute | solution.py:43
  335.6 4.6 %collective-permute-start.24 = (bf16[1,80,768]{2,1,0:T(8,128)(2,1)S(1)}, bf16[1,80,768]{2,1,0:T(8,128)(2,1)S(1)}, u32[]{:S(2)}, u32[]{:S(2)}) collective-permute-start(bf16[1,80,768]{2,1,0:T(8,128)(2,1)S(1)} %fusion.7), channel_id=1, source_target_pairs={{0,8},{1,9},{2,10},{3,11},{4,12},{5,13},{6,14},{7,15},{8,0},{9,1},... | collective-permute-start | bytes 368648 | tf_op jit(solution)/shard_map/ppermute | solution.py:43
  341.8 2.6 collective-permute-done.24
  (101 shorter events, 24.0 us)
Async XLA Ops:
  0.7 15.8 %copy-start = (bf16[1024,768]{1,0:T(8,128)(2,1)S(1)}, bf16[1024,768]{1,0:T(8,128)(2,1)}, u32[]{:S(2)}) copy-start(bf16[1024,768]{1,0:T(8,128)(2,1)} %tok.1) | copy-start | bytes 4718596
  4.3 15.7 %copy-start.9 = (bf16[1,80,768]{2,1,0:T(8,128)(2,1)S(1)}, bf16[1,80,768]{2,1,0:T(8,128)(2,1)}, u32[]{:S(2)}) copy-start(bf16[1,80,768]{2,1,0:T(8,128)(2,1)} %get-tuple-element.87) | copy-start | bytes 368644
  4.3 19.9 %copy-start.1 = (bf16[1,224,768]{2,1,0:T(8,128)(2,1)S(1)}, bf16[1,224,768]{2,1,0:T(8,128)(2,1)}, u32[]{:S(2)}) copy-start(bf16[1,224,768]{2,1,0:T(8,128)(2,1)} %get-tuple-element.89) | copy-start | bytes 1032196
  4.3 10.3 %collective-permute-start = (bf16[1,80,768]{2,1,0:T(8,128)(2,1)}, bf16[1,80,768]{2,1,0:T(8,128)(2,1)S(1)}, u32[]{:S(2)}, u32[]{:S(2)}) collective-permute-start(bf16[1,80,768]{2,1,0:T(8,128)(2,1)} %get-tuple-element.87), channel_id=1, source_target_pairs={{0,8},{1,9},{2,10},{3,11},{4,12},{5,13},{6,14},{7,15},{8,0},{9,1},... | collective-permute-start | bytes 368648 | tf_op jit(solution)/shard_map/ppermute | solution.py:43
  15.5 7.2 %collective-permute-start.1 = (bf16[2,80,768]{2,1,0:T(8,128)(2,1)S(1)}, bf16[2,80,768]{2,1,0:T(8,128)(2,1)S(1)}, u32[]{:S(2)}, u32[]{:S(2)}) collective-permute-start(bf16[2,80,768]{2,1,0:T(8,128)(2,1)S(1)} %pad_maximum_fusion.4), channel_id=1, source_target_pairs={{0,4},{1,5},{2,6},{3,7},{4,0},{5,1},{6,2},{7,3},{8,12},{9,13},{10,... | collective-permute-start | bytes 737288 | tf_op jit(solution)/shard_map/ppermute | solution.py:43
  16.5 25.7 %collective-permute-start.4 = (bf16[512,768]{1,0:T(8,128)(2,1)S(1)}, bf16[512,768]{1,0:T(8,128)(2,1)S(1)}, u32[]{:S(2)}, u32[]{:S(2)}) collective-permute-start(bf16[512,768]{1,0:T(8,128)(2,1)S(1)} %get-tuple-element.169), channel_id=1, source_target_pairs={{0,1},{1,2},{2,3},{3,4},{4,5},{5,6},{6,7},{7,8},{8,9},{9,10},{10,1... | collective-permute-start | bytes 2359304 | tf_op jit(solution)/shard_map/ppermute | solution.py:1058
  22.8 20.0 %collective-permute-start.2 = (bf16[4,80,768]{2,1,0:T(8,128)(2,1)S(1)}, bf16[4,80,768]{2,1,0:T(8,128)(2,1)S(1)}, u32[]{:S(2)}, u32[]{:S(2)}) collective-permute-start(bf16[4,80,768]{2,1,0:T(8,128)(2,1)S(1)} %get-tuple-element.194), channel_id=1, source_target_pairs={{0,2},{1,3},{2,0},{3,1},{4,6},{5,7},{6,4},{7,5},{8,10},{9,11},{10,... | collective-permute-start | bytes 1474568 | tf_op jit(solution)/shard_map/ppermute | solution.py:43
  24.2 18.1 %collective-permute-start.3 = (bf16[1,224,768]{2,1,0:T(8,128)(2,1)S(1)}, bf16[1,224,768]{2,1,0:T(8,128)(2,1)S(1)}, u32[]{:S(2)}, u32[]{:S(2)}) collective-permute-start(bf16[1,224,768]{2,1,0:T(8,128)(2,1)S(1)} %copy-done.1), channel_id=1, source_target_pairs={{0,8},{1,9},{2,10},{3,11},{4,12},{5,13},{6,14},{7,15},{8,0},{9,1},... | collective-permute-start | bytes 1032200 | tf_op jit(solution)/shard_map/ppermute | solution.py:43
  42.8 47.1 %copy-start.6 = (bf16[8,80,768]{2,1,0:T(8,128)(2,1)}, bf16[8,80,768]{2,1,0:T(8,128)(2,1)S(1)}, u32[]{:S(2)}) copy-start(bf16[8,80,768]{2,1,0:T(8,128)(2,1)S(1)} %constant_dynamic-update-slice_fusion.3.low) | copy-start | bytes 2949124
  42.8 44.2 %collective-permute-start.6 = (bf16[8,80,768]{2,1,0:T(8,128)(2,1)S(1)}, bf16[8,80,768]{2,1,0:T(8,128)(2,1)S(1)}, u32[]{:S(2)}, u32[]{:S(2)}) collective-permute-start(bf16[8,80,768]{2,1,0:T(8,128)(2,1)S(1)} %constant_dynamic-update-slice_fusion.3.low), channel_id=1, source_target_pairs={{0,16},{16,0},{1,17},{17,1},{2,18},{18,2},{3,19},{19,3},{4,20},{20... | collective-permute-start | bytes 2949128 | tf_op jit(solution)/shard_map/ppermute | solution.py:47
  43.8 44.3 %collective-permute-start.5 = (bf16[8,80,768]{2,1,0:T(8,128)(2,1)S(1)}, bf16[8,80,768]{2,1,0:T(8,128)(2,1)S(1)}, u32[]{:S(2)}, u32[]{:S(2)}) collective-permute-start(bf16[8,80,768]{2,1,0:T(8,128)(2,1)S(1)} %constant_dynamic-update-slice_fusion.3.low), channel_id=1, source_target_pairs={{0,1},{1,0},{2,3},{3,2},{4,5},{5,4},{6,7},{7,6},{8,9},{9,8},{10,11... | collective-permute-start | bytes 2949128 | tf_op jit(solution)/shard_map/ppermute | solution.py:43
  44.3 42.8 %collective-permute-start.8 = (bf16[512,768]{1,0:T(8,128)(2,1)S(1)}, bf16[512,768]{1,0:T(8,128)(2,1)S(1)}, u32[]{:S(2)}, u32[]{:S(2)}) collective-permute-start(bf16[512,768]{1,0:T(8,128)(2,1)S(1)} %get-tuple-element.93), channel_id=1, source_target_pairs={{1,0},{2,1},{3,2},{4,3},{5,4},{6,5},{7,6},{8,7},{9,8},{10,9},{11,1... | collective-permute-start | bytes 2359304 | tf_op jit(solution)/shard_map/ppermute | solution.py:1065
  45.6 41.4 %collective-permute-start.7 = (bf16[2,224,768]{2,1,0:T(8,128)(2,1)S(1)}, bf16[2,224,768]{2,1,0:T(8,128)(2,1)S(1)}, u32[]{:S(2)}, u32[]{:S(2)}) collective-permute-start(bf16[2,224,768]{2,1,0:T(8,128)(2,1)S(1)} %pad_maximum_fusion.2), channel_id=1, source_target_pairs={{0,4},{1,5},{2,6},{3,7},{4,0},{5,1},{6,2},{7,3},{8,12},{9,13},{10,... | collective-permute-start | bytes 2064392 | tf_op jit(solution)/shard_map/ppermute | solution.py:43
  87.1 0.9 copy-start.7
  88.0 2.8 copy-start.8
  88.2 20.3 %collective-permute-start.10 = (bf16[4,224,768]{2,1,0:T(8,128)(2,1)S(1)}, bf16[4,224,768]{2,1,0:T(8,128)(2,1)S(1)}, u32[]{:S(2)}, u32[]{:S(2)}) collective-permute-start(bf16[4,224,768]{2,1,0:T(8,128)(2,1)S(1)} %pad_maximum_fusion.1), channel_id=1, source_target_pairs={{0,2},{1,3},{2,0},{3,1},{4,6},{5,7},{6,4},{7,5},{8,10},{9,11},{10,... | collective-permute-start | bytes 4128776 | tf_op jit(solution)/shard_map/ppermute | solution.py:43
  88.3 4.4 %collective-permute-start.9 = (bf16[8,80,768]{2,1,0:T(8,128)(2,1)S(1)}, bf16[8,80,768]{2,1,0:T(8,128)(2,1)}, u32[]{:S(2)}, u32[]{:S(2)}) collective-permute-start(bf16[8,80,768]{2,1,0:T(8,128)(2,1)S(1)} %collective-permute-done.5.high), channel_id=1, source_target_pairs={{0,16},{16,0},{1,17},{17,1},{2,18},{18,2},{3,19},{19,3},{4,20},{20... | collective-permute-start | bytes 2949128 | tf_op jit(solution)/shard_map/ppermute | solution.py:47
  108.5 2.6 copy-start.10
  109.8 33.3 %collective-permute-start.11 = (bf16[8,224,768]{2,1,0:T(8,128)(2,1)}, bf16[8,224,768]{2,1,0:T(8,128)(2,1)S(1)}, u32[]{:S(2)}, u32[]{:S(2)}) collective-permute-start(bf16[8,224,768]{2,1,0:T(8,128)(2,1)} %constant_dynamic-update-slice_fusion.7.low), channel_id=1, source_target_pairs={{0,1},{1,0},{2,3},{3,2},{4,5},{5,4},{6,7},{7,6},{8,9},{9,8},{10,11... | collective-permute-start | bytes 8257544 | tf_op jit(solution)/shard_map/ppermute | solution.py:43
  113.7 31.9 %collective-permute-start.12 = (bf16[8,224,768]{2,1,0:T(8,128)(2,1)}, bf16[8,224,768]{2,1,0:T(8,128)(2,1)}, u32[]{:S(2)}, u32[]{:S(2)}) collective-permute-start(bf16[8,224,768]{2,1,0:T(8,128)(2,1)} %constant_dynamic-update-slice_fusion.7.low), channel_id=1, source_target_pairs={{0,16},{16,0},{1,17},{17,1},{2,18},{18,2},{3,19},{19,3},{4,20},{20... | collective-permute-start | bytes 8257544 | tf_op jit(solution)/shard_map/ppermute | solution.py:47
  143.0 8.8 %copy-start.2 = (bf16[8,224,768]{2,1,0:T(8,128)(2,1)}, bf16[8,224,768]{2,1,0:T(8,128)(2,1)S(1)}, u32[]{:S(2)}) copy-start(bf16[8,224,768]{2,1,0:T(8,128)(2,1)S(1)} %collective-permute-done.11.high) | copy-start | bytes 8257540
  143.1 7.3 %collective-permute-start.13 = (bf16[8,224,768]{2,1,0:T(8,128)(2,1)S(1)}, bf16[8,224,768]{2,1,0:T(8,128)(2,1)S(1)}, u32[]{:S(2)}, u32[]{:S(2)}) collective-permute-start(bf16[8,224,768]{2,1,0:T(8,128)(2,1)S(1)} %collective-permute-done.11.high), channel_id=1, source_target_pairs={{0,16},{16,0},{1,17},{17,1},{2,18},{18,2},{3,19},{19,3},{4,20},{20... | collective-permute-start | bytes 8257544 | tf_op jit(solution)/shard_map/ppermute | solution.py:47
  150.3 1.5 copy-start.3
  187.8 27.9 %collective-permute-start.14 = (bf16[16,224,768]{2,1,0:T(8,128)(2,1)}, bf16[16,224,768]{2,1,0:T(8,128)(2,1)}, u32[]{:S(2)}, u32[]{:S(2)}) collective-permute-start(bf16[16,224,768]{2,1,0:T(8,128)(2,1)} %get-tuple-element.117), channel_id=1, source_target_pairs={{0,16},{16,0},{1,17},{17,1},{2,18},{18,2},{3,19},{19,3},{4,20},{20... | collective-permute-start | bytes 16515080 | tf_op jit(solution)/shard_map/ppermute | solution.py:47
  188.3 27.4 %slice-start = ((s8[5505024]{0:T(1024)(128)(4,1)}), s8[4194304]{0:T(1024)(128)(4,1)S(1)}, s32[]{:S(2)}) async-start(s8[5505024]{0:T(1024)(128)(4,1)} %bitcast.54), calls=%async_computation | async-start | bytes 8388608
  190.4 25.3 %collective-permute-start.16 = (bf16[256,896]{1,0:T(8,128)(2,1)}, bf16[256,896]{1,0:T(8,128)(2,1)}, u32[]{:S(2)}, u32[]{:S(2)}) collective-permute-start(bf16[256,896]{1,0:T(8,128)(2,1)} %get-tuple-element.174), channel_id=1, source_target_pairs={{1,0},{2,1},{3,2},{4,3},{5,4},{6,5},{7,6},{8,7},{9,8},{10,9},{11,1... | collective-permute-start | bytes 1376264 | tf_op jit(solution)/shard_map/ppermute | solution.py:1124
  191.7 24.0 %collective-permute-start.15 = (bf16[256,896]{1,0:T(8,128)(2,1)S(1)}, bf16[256,896]{1,0:T(8,128)(2,1)}, u32[]{:S(2)}, u32[]{:S(2)}) collective-permute-start(bf16[256,896]{1,0:T(8,128)(2,1)S(1)} %get-tuple-element.175), channel_id=1, source_target_pairs={{0,1},{1,2},{2,3},{3,4},{4,5},{5,6},{6,7},{7,8},{8,9},{9,10},{10,1... | collective-permute-start | bytes 1376264 | tf_op jit(solution)/shard_map/ppermute | solution.py:1123
  197.3 18.4 %slice-start.1 = ((s8[5505024]{0:T(1024)(128)(4,1)}), s8[1310720]{0:T(1024)(128)(4,1)S(1)}, s32[]{:S(2)}) async-start(s8[5505024]{0:T(1024)(128)(4,1)} %bitcast.54), calls=%async_computation.1 | async-start | bytes 2621440
  219.7 33.3 %collective-permute-start.17 = (bf16[8,224,768]{2,1,0:T(8,128)(2,1)}, bf16[8,224,768]{2,1,0:T(8,128)(2,1)S(1)}, u32[]{:S(2)}, u32[]{:S(2)}) collective-permute-start(bf16[8,224,768]{2,1,0:T(8,128)(2,1)} %add_convert_fusion), channel_id=1, source_target_pairs={{0,1},{1,0},{2,3},{3,2},{4,5},{5,4},{6,7},{7,6},{8,9},{9,8},{10,11... | collective-permute-start | bytes 8257544 | tf_op jit(solution)/shard_map/ppermute | solution.py:43
  257.6 18.5 %collective-permute-start.18 = (bf16[4,224,768]{2,1,0:T(8,128)(2,1)}, bf16[4,224,768]{2,1,0:T(8,128)(2,1)S(1)}, u32[]{:S(2)}, u32[]{:S(2)}) collective-permute-start(bf16[4,224,768]{2,1,0:T(8,128)(2,1)} %get-tuple-element.162), channel_id=1, source_target_pairs={{0,2},{1,3},{2,0},{3,1},{4,6},{5,7},{6,4},{7,5},{8,10},{9,11},{10,... | collective-permute-start | bytes 4128776 | tf_op jit(solution)/shard_map/ppermute | solution.py:43
  276.4 15.0 %collective-permute-start.19 = (bf16[2,224,768]{2,1,0:T(8,128)(2,1)S(1)}, bf16[2,224,768]{2,1,0:T(8,128)(2,1)S(1)}, u32[]{:S(2)}, u32[]{:S(2)}) collective-permute-start(bf16[2,224,768]{2,1,0:T(8,128)(2,1)S(1)} %get-tuple-element.167), channel_id=1, source_target_pairs={{0,4},{1,5},{2,6},{3,7},{4,0},{5,1},{6,2},{7,3},{8,12},{9,13},{10,... | collective-permute-start | bytes 2064392 | tf_op jit(solution)/shard_map/ppermute | solution.py:43
  291.3 7.0 %collective-permute-start.20 = (bf16[16,80,768]{2,1,0:T(8,128)(2,1)}, bf16[16,80,768]{2,1,0:T(8,128)(2,1)S(1)}, u32[]{:S(2)}, u32[]{:S(2)}) collective-permute-start(bf16[16,80,768]{2,1,0:T(8,128)(2,1)} %get-tuple-element.147), channel_id=1, source_target_pairs={{0,16},{16,0},{1,17},{17,1},{2,18},{18,2},{3,19},{19,3},{4,20},{20... | collective-permute-start | bytes 5898248 | tf_op jit(solution)/shard_map/ppermute | solution.py:47
  298.4 9.7 %copy-start.5 = (bf16[16,80,768]{2,1,0:T(8,128)(2,1)}, bf16[16,80,768]{2,1,0:T(8,128)(2,1)S(1)}, u32[]{:S(2)}) copy-start(bf16[16,80,768]{2,1,0:T(8,128)(2,1)S(1)} %collective-permute-done.20) | copy-start | bytes 5898244
  300.5 15.5 %collective-permute-start.21 = (bf16[8,80,768]{2,1,0:T(8,128)(2,1)S(1)}, bf16[8,80,768]{2,1,0:T(8,128)(2,1)S(1)}, u32[]{:S(2)}, u32[]{:S(2)}) collective-permute-start(bf16[8,80,768]{2,1,0:T(8,128)(2,1)S(1)} %add_convert_fusion.2), channel_id=1, source_target_pairs={{0,1},{1,0},{2,3},{3,2},{4,5},{5,4},{6,7},{7,6},{8,9},{9,8},{10,11... | collective-permute-start | bytes 2949128 | tf_op jit(solution)/shard_map/ppermute | solution.py:43
  303.3 20.9 %collective-permute-start.26 = (bf16[1,224,768]{2,1,0:T(8,128)(2,1)}, bf16[1,224,768]{2,1,0:T(8,128)(2,1)}, u32[]{:S(2)}, u32[]{:S(2)}) collective-permute-start(bf16[1,224,768]{2,1,0:T(8,128)(2,1)} %fusion.3), channel_id=1, source_target_pairs={{0,8},{1,9},{2,10},{3,11},{4,12},{5,13},{6,14},{7,15},{8,0},{9,1},... | collective-permute-start | bytes 1032200 | tf_op jit(solution)/shard_map/ppermute | solution.py:43
  308.1 8.0 %copy-start.4 = (bf16[16,80,768]{2,1,0:T(8,128)(2,1)S(1)}, bf16[16,80,768]{2,1,0:T(8,128)(2,1)}, u32[]{:S(2)}) copy-start(bf16[16,80,768]{2,1,0:T(8,128)(2,1)} %get-tuple-element.145) | copy-start | bytes 5898244
  318.3 9.1 %collective-permute-start.22 = (bf16[4,80,768]{2,1,0:T(8,128)(2,1)}, bf16[4,80,768]{2,1,0:T(8,128)(2,1)}, u32[]{:S(2)}, u32[]{:S(2)}) collective-permute-start(bf16[4,80,768]{2,1,0:T(8,128)(2,1)} %get-tuple-element.164), channel_id=1, source_target_pairs={{0,2},{1,3},{2,0},{3,1},{4,6},{5,7},{6,4},{7,5},{8,10},{9,11},{10,... | collective-permute-start | bytes 1474568 | tf_op jit(solution)/shard_map/ppermute | solution.py:43
  325.2 5.2 %collective-permute-start.27 = (f32[224,768]{1,0:T(8,128)S(1)}, f32[224,768]{1,0:T(8,128)S(1)}, u32[]{:S(2)}, u32[]{:S(2)}) collective-permute-start(f32[224,768]{1,0:T(8,128)S(1)} %fusion.5), channel_id=1, source_target_pairs={{0,16},{16,0},{1,17},{17,1},{2,18},{18,2},{3,19},{19,3},{4,20},{20... | collective-permute-start | bytes 2064392 | tf_op jit(solution)/shard_map/ppermute | solution.py:47
  328.6 6.9 %collective-permute-start.23 = (bf16[2,80,768]{2,1,0:T(8,128)(2,1)S(1)}, bf16[2,80,768]{2,1,0:T(8,128)(2,1)S(1)}, u32[]{:S(2)}, u32[]{:S(2)}) collective-permute-start(bf16[2,80,768]{2,1,0:T(8,128)(2,1)S(1)} %get-tuple-element.170), channel_id=1, source_target_pairs={{0,4},{1,5},{2,6},{3,7},{4,0},{5,1},{6,2},{7,3},{8,12},{9,13},{10,... | collective-permute-start | bytes 737288 | tf_op jit(solution)/shard_map/ppermute | solution.py:43
  335.6 8.8 %collective-permute-start.24 = (bf16[1,80,768]{2,1,0:T(8,128)(2,1)S(1)}, bf16[1,80,768]{2,1,0:T(8,128)(2,1)S(1)}, u32[]{:S(2)}, u32[]{:S(2)}) collective-permute-start(bf16[1,80,768]{2,1,0:T(8,128)(2,1)S(1)} %fusion.7), channel_id=1, source_target_pairs={{0,8},{1,9},{2,10},{3,11},{4,12},{5,13},{6,14},{7,15},{8,0},{9,1},... | collective-permute-start | bytes 368648 | tf_op jit(solution)/shard_map/ppermute | solution.py:43
  344.4 1.6 collective-permute-start.25
